TPU v7x, 512 devices: a whole 4x4x16 slice. The times are simulated.
512 devices in a mesh: grp: 8 (over x, core), wide: 64 (over z, y).
Axes of the slice: x: 4, y: 4, z: 16, core: 2. Of those that a mesh axis runs over, the one named last changes fastest.
Arguments:
- anchor_states: bfloat16 [65536, 1024], P(('wide', 'grp')), may hold values from -6 to 6
- key_weight: bfloat16 [1024, 1024], P(None, 'grp'), may hold values from -0.1875 to 0.1875
- value_weight: bfloat16 [1024, 1024], P(None, 'grp'), may hold values from -0.1875 to 0.1875
- panel_query: bfloat16 [131072, 1024], P(('wide', 'grp')), may hold values from -160 to 160
- cell_list: int32 [1024, 4], P('wide'), may hold values from 0 to 7, as said below
- cell_count: int32 [1024], P('wide'), may hold values from 1 to 4, as said below
- norm_gain: float32 [1024], replicated, may hold values from 0.1 to 1.9
- up_weight: bfloat16 [1024, 512], replicated, may hold values from -0.1875 to 0.1875
- flux_weight: bfloat16 [4, 512], replicated, may hold values from -0.25 to 0.25
Outputs:
- flux: float32 [4, 131072], P(None, ('wide', 'grp'))
Inputs may be any that keep to these rules, and one draw needn't show every extreme that they name: `cell_list`: the entries of a row are distinct cell blocks of that panel block's region; entries past cell_count are not used. `cell_count`: every region has a panel block whose list uses all 4 slots.
All inputs are finite; a program needn't handle non-finite values.
Results may differ from a plain program's by a relative error of at most 0.007.
Values may be sent and summed in bfloat16 or wider, within the bound.
No kernel may reach another device: no remote copies, remote signals or barrier semaphores. Data moves between devices by JAX's collectives and lax.ppermute only.
A program may use at most 64 MiB of HBM per device.

v0:
```python
import math

import jax
import jax.numpy as jnp
from jax import lax
from jax.sharding import PartitionSpec as P

BLK = 128
LMAX = 4
HD = 64


def softmax_rows(scores, mask):
    scores = jnp.where(mask[:, None, None, :], scores, -jnp.inf)
    top = jnp.max(scores, axis=-1, keepdims=True)
    expo = jnp.exp(scores - top)
    return (expo / jnp.sum(expo, axis=-1, keepdims=True)).astype(jnp.bfloat16)


def wall_flux(query_rows, attended_rows, norm_gain, up_weight, flux_weight):
    stream = query_rows.astype(jnp.float32) + attended_rows.astype(jnp.float32)
    scale = lax.rsqrt(jnp.mean(stream * stream, axis=-1, keepdims=True) + 1e-06)
    normed = (stream * scale * norm_gain[None, :]).astype(jnp.bfloat16)
    hidden = jax.nn.gelu(jnp.dot(normed, up_weight, preferred_element_type=jnp.float32)).astype(
        jnp.bfloat16
    )
    return lax.dot_general(
        flux_weight, hidden, (((1,), (1,)), ((), ())), preferred_element_type=jnp.float32
    )


def body(
    anchor_states,
    key_weight,
    value_weight,
    panel_query,
    cell_list,
    cell_count,
    norm_gain,
    up_weight,
    flux_weight,
):
    full_keys_w, full_values_w = (
        lax.all_gather(key_weight, "grp", axis=1, tiled=True),
        lax.all_gather(value_weight, "grp", axis=1, tiled=True),
    )
    local_keys = jnp.dot(anchor_states, full_keys_w, preferred_element_type=jnp.float32).astype(
        jnp.bfloat16
    )
    local_values = jnp.dot(anchor_states, full_values_w, preferred_element_type=jnp.float32).astype(
        jnp.bfloat16
    )
    region_keys, region_values = (
        lax.all_to_all(local_keys, "grp", split_axis=1, concat_axis=0, tiled=True),
        lax.all_to_all(local_values, "grp", split_axis=1, concat_axis=0, tiled=True),
    )
    region_query = lax.all_to_all(
        lax.all_to_all(panel_query, "grp", split_axis=1, concat_axis=0, tiled=True),
        "wide",
        split_axis=0,
        concat_axis=0,
        tiled=True,
    )
    local_heads = region_keys.shape[1] // HD
    cell_blocks = region_keys.shape[0] // BLK
    block_count = region_query.shape[0] // BLK
    per_step = math.gcd(block_count, 4)
    steps = block_count // per_step
    key_blocks = region_keys.reshape(cell_blocks, BLK, local_heads, HD)
    value_blocks = region_values.reshape(cell_blocks, BLK, local_heads, HD)
    query_groups = region_query.reshape(steps, per_step, BLK, local_heads, HD)
    list_groups = cell_list.reshape(steps, per_step, LMAX)
    count_groups = cell_count.reshape(steps, per_step)
    slot_index = jnp.arange(LMAX, dtype=jnp.int32)

    def attend(item):
        query_group, listed, counts = item
        live = slot_index[None, :] < counts[:, None]
        picked_keys = key_blocks[listed].reshape(per_step, LMAX * BLK, local_heads, HD)
        picked_values = value_blocks[listed].reshape(per_step, LMAX * BLK, local_heads, HD)
        mask = jnp.repeat(live, BLK, axis=1)
        scores = jnp.einsum(
            "bihd,bjhd->bhij", query_group, picked_keys, preferred_element_type=jnp.float32
        ) / math.sqrt(HD)
        weights = softmax_rows(scores, mask)
        output = jnp.einsum(
            "bhij,bjhd->bihd", weights, picked_values, preferred_element_type=jnp.float32
        )
        return output.astype(jnp.bfloat16)

    attended = lax.map(attend, (query_groups, list_groups, count_groups))
    attended = attended.reshape(block_count * BLK, local_heads * HD)
    panel_rows = lax.all_to_all(
        lax.all_to_all(attended, "wide", split_axis=0, concat_axis=0, tiled=True),
        "grp",
        split_axis=0,
        concat_axis=1,
        tiled=True,
    )
    return wall_flux(panel_query, panel_rows, norm_gain, up_weight, flux_weight)


def solution(mesh):
    in_specs = (
        P(("wide", "grp"), None),
        P(None, "grp"),
        P(None, "grp"),
        P(("wide", "grp"), None),
        P("wide", None),
        P("wide"),
        P(),
        P(),
        P(),
    )
    out_specs = P(None, ("wide", "grp"))
    return jax.shard_map(body, mesh=mesh, in_specs=in_specs, out_specs=out_specs, check_vma=False)
```

profile of v0, /device:TPU:1, one launch (start us, length us, event | category | flops | bytes accessed | tf_op | source)
XLA Modules:
  0.0 225.5 jit_solution(5993352546024872910)
XLA Ops:
  9.3 18.6 %all_to_all.79 = bf16[256,8,128]{0,2,1:T(8,128)(2,1)S(1)} all-to-all(bf16[256,8,128]{0,2,1:T(8,128)(2,1)S(1)} %bitcast.78), channel_id=1, replica_groups=mesh['grp'=8,'wide'=64] {'grp'}, dimensions={1} | all-to-all | bytes 1048576 | tf_op jit(solution)/shard_map/all_to_all | solution.py:58
  29.0 14.8 %all-to-all-start.2 = ((bf16[64,32,128]{2,1,0:T(8,128)(2,1)}), bf16[64,32,128]{2,1,0:T(8,128)(2,1)S(1)}, u32[]{:S(2)}, u32[]{:S(2)}) async-start(bf16[64,32,128]{2,1,0:T(8,128)(2,1)} %bitcast.6), calls=%async_computation.2 | async-start | bytes 1048576 | tf_op jit(solution)/shard_map/all_to_all | solution.py:57
  43.7 6.4 %all-gather.3.cloned.1.call-done = bf16[1024,1024]{1,0:T(8,128)(2,1)} async-done(((bf16[1024,128]{1,0:T(8,128)(2,1)}), bf16[1024,1024]{1,0:T(8,128)(2,1)}) %all-gather.3.cloned.1.call-update) | async-done | bytes 2097168 | tf_op jit(solution)/shard_map/all_gather | solution.py:45
  53.0 19.9 %all-to-all-done.2 = bf16[64,32,128]{2,1,0:T(8,128)(2,1)S(1)} async-done(((bf16[64,32,128]{2,1,0:T(8,128)(2,1)}), bf16[64,32,128]{2,1,0:T(8,128)(2,1)S(1)}, u32[]{:S(2)}, u32[]{:S(2)}) %all-to-all-start.2) | async-done | bytes 524320 | tf_op jit(solution)/shard_map/all_to_all | solution.py:57
  72.9 8.1 %all-to-all-start = ((bf16[128,8,128]{0,2,1:T(8,128)(2,1)}), bf16[128,8,128]{0,2,1:T(8,128)(2,1)S(1)}, u32[]{:S(2)}, u32[]{:S(2)}) async-start(bf16[128,8,128]{0,2,1:T(8,128)(2,1)} %bitcast.1), calls=%async_computation | async-start | bytes 524288 | tf_op jit(solution)/shard_map/all_to_all | solution.py:55
  81.0 10.1 %all-gather.5.cloned.1.call-done = bf16[1024,1024]{1,0:T(8,128)(2,1)} async-done(((bf16[1024,128]{1,0:T(8,128)(2,1)}), bf16[1024,1024]{1,0:T(8,128)(2,1)}) %all-gather.5.cloned.1.call-update) | async-done | bytes 2097168 | tf_op jit(solution)/shard_map/all_gather | solution.py:44
  93.9 4.2 %all-to-all-start.3 = ((bf16[128,8,128]{0,2,1:T(8,128)(2,1)}), bf16[128,8,128]{0,2,1:T(8,128)(2,1)S(1)}, u32[]{:S(2)}, u32[]{:S(2)}) async-start(bf16[128,8,128]{0,2,1:T(8,128)(2,1)} %bitcast.7), calls=%async_computation.3 | async-start | bytes 524288 | tf_op jit(solution)/shard_map/all_to_all | solution.py:54
  100.9 3.8 %all-to-all-done.3 = bf16[128,8,128]{0,2,1:T(8,128)(2,1)S(1)} async-done(((bf16[128,8,128]{0,2,1:T(8,128)(2,1)}), bf16[128,8,128]{0,2,1:T(8,128)(2,1)S(1)}, u32[]{:S(2)}, u32[]{:S(2)}) %all-to-all-start.3) | async-done | bytes 262176 | tf_op jit(solution)/shard_map/all_to_all | solution.py:54
  105.1 46.4 %while.11 = (s32[]{:T(128)}, bf16[4,4,128,2,64]{2,4,3,1,0:T(8,128)(2,1)}, s32[4,4,4]{2,1,0:T(4,128)S(1)}, bf16[8,128,2,64]{3,2,1,0:T(2,128)(2,1)S(1)}, s32[4,4]{...) while((s32[]{:T(128)}, ...), condition=%wide.region_3.4_spmd.clone, body=%wide.region_0.3_spmd.clone.sunk | while | flops 137430592 | bytes 7624301 | solution.py:91
  105.2 2.7 %gather_fusion.1 = bf16[16,128,2,64]{3,2,1,0:T(2,128)(2,1)S(1)} fusion(bf16[8,128,2,64]{3,2,1,0:T(2,128)(2,1)S(1)} %get-tuple-element.170, s32[1024]{0:T(1024)S(1)} %pad_clamp_fusion.2), kind=kCustom, calls=%fused_computation.1.clone.clone.1 | custom fusion | bytes 1048640 | tf_op jit(solution)/shard_map/while/body/eval_jaxpr/gather | solution.py:79
  108.1 3.1 %fusion.69 = (f32[4,2,128]{2,1,0:T(2,128)S(1)}, f32[4,2,128,512]{3,2,1,0:T(8,128)}) fusion(pred[4,512]{1,0:T(4,128)(4,1)S(1)} %bitcast.83, bf16[4,512,2,64]{3,2,1,0:T(2,128)(2,1)S(1)} %bitcast.76, bf16[4,4,128,2,64]{2,4,3,1,0:T(8,128)(2,1)} %get-tuple-element.169, s32[]{:T(128)} %get-tuple-element.156), kind=kOutput, calls=%fused_computation.51.clone.1 | convolution fusion | flops 69206528 | bytes 2759168 | tf_op jit(solution)/shard_map/while/body/eval_jaxpr/sub | solution.py:16
  111.1 2.7 %gather_fusion = bf16[16,128,2,64]{3,2,1,0:T(2,128)(2,1)S(1)} fusion(bf16[8,128,2,64]{3,2,1,0:T(2,128)(2,1)S(1)} %get-tuple-element.167, s32[1024]{0:T(1024)S(1)} %pad_clamp_fusion.2), kind=kCustom, calls=%fused_computation.clone.clone.1 | custom fusion | bytes 1048640 | tf_op jit(solution)/shard_map/while/body/eval_jaxpr/gather | solution.py:80
  113.8 2.9 %fusion.70 = bf16[4,4,128,2,64]{2,4,3,1,0:T(8,128)(2,1)} fusion(bf16[4,4,128,2,64]{2,4,3,1,0:T(8,128)(2,1)} %get-tuple-element.157, s32[]{:T(128)} %get-tuple-element.156, bf16[4,512,2,64]{3,2,1,0:T(2,128)(2,1)S(1)} %bitcast.77, f32[4,2,128,512]{3,2,1,0:T(8,128)} %get-tuple-element.146, f32[4,2,128]{2,1,0:T(2,128)S(1)} %get-tuple-element.147), kind=kOutput, calls=%fused_computation.10.clone.1 | convolution fusion | flops 68222976 | bytes 2757120 | tf_op jit(solution)/shard_map/while/body/eval_jaxpr/bhij,bjhd->bihd/dot_general | solution.py:86
  116.8 2.7 %gather_fusion.1 = bf16[16,128,2,64]{3,2,1,0:T(2,128)(2,1)S(1)} fusion(bf16[8,128,2,64]{3,2,1,0:T(2,128)(2,1)S(1)} %get-tuple-element.170, s32[1024]{0:T(1024)S(1)} %pad_clamp_fusion.2), kind=kCustom, calls=%fused_computation.1.clone.clone.1 | custom fusion | bytes 1048640 | tf_op jit(solution)/shard_map/while/body/eval_jaxpr/gather | solution.py:79
  119.6 3.1 %fusion.69 = (f32[4,2,128]{2,1,0:T(2,128)S(1)}, f32[4,2,128,512]{3,2,1,0:T(8,128)}) fusion(pred[4,512]{1,0:T(4,128)(4,1)S(1)} %bitcast.83, bf16[4,512,2,64]{3,2,1,0:T(2,128)(2,1)S(1)} %bitcast.76, bf16[4,4,128,2,64]{2,4,3,1,0:T(8,128)(2,1)} %get-tuple-element.169, s32[]{:T(128)} %get-tuple-element.156), kind=kOutput, calls=%fused_computation.51.clone.1 | convolution fusion | flops 69206528 | bytes 2759168 | tf_op jit(solution)/shard_map/while/body/eval_jaxpr/sub | solution.py:16
  125.4 2.9 %fusion.70 = bf16[4,4,128,2,64]{2,4,3,1,0:T(8,128)(2,1)} fusion(bf16[4,4,128,2,64]{2,4,3,1,0:T(8,128)(2,1)} %get-tuple-element.157, s32[]{:T(128)} %get-tuple-element.156, bf16[4,512,2,64]{3,2,1,0:T(2,128)(2,1)S(1)} %bitcast.77, f32[4,2,128,512]{3,2,1,0:T(8,128)} %get-tuple-element.146, f32[4,2,128]{2,1,0:T(2,128)S(1)} %get-tuple-element.147), kind=kOutput, calls=%fused_computation.10.clone.1 | convolution fusion | flops 68222976 | bytes 2757120 | tf_op jit(solution)/shard_map/while/body/eval_jaxpr/bhij,bjhd->bihd/dot_general | solution.py:86
  128.4 2.7 %gather_fusion.1 = bf16[16,128,2,64]{3,2,1,0:T(2,128)(2,1)S(1)} fusion(bf16[8,128,2,64]{3,2,1,0:T(2,128)(2,1)S(1)} %get-tuple-element.170, s32[1024]{0:T(1024)S(1)} %pad_clamp_fusion.2), kind=kCustom, calls=%fused_computation.1.clone.clone.1 | custom fusion | bytes 1048640 | tf_op jit(solution)/shard_map/while/body/eval_jaxpr/gather | solution.py:79
  131.2 3.1 %fusion.69 = (f32[4,2,128]{2,1,0:T(2,128)S(1)}, f32[4,2,128,512]{3,2,1,0:T(8,128)}) fusion(pred[4,512]{1,0:T(4,128)(4,1)S(1)} %bitcast.83, bf16[4,512,2,64]{3,2,1,0:T(2,128)(2,1)S(1)} %bitcast.76, bf16[4,4,128,2,64]{2,4,3,1,0:T(8,128)(2,1)} %get-tuple-element.169, s32[]{:T(128)} %get-tuple-element.156), kind=kOutput, calls=%fused_computation.51.clone.1 | convolution fusion | flops 69206528 | bytes 2759168 | tf_op jit(solution)/shard_map/while/body/eval_jaxpr/sub | solution.py:16
  137.0 2.9 %fusion.70 = bf16[4,4,128,2,64]{2,4,3,1,0:T(8,128)(2,1)} fusion(bf16[4,4,128,2,64]{2,4,3,1,0:T(8,128)(2,1)} %get-tuple-element.157, s32[]{:T(128)} %get-tuple-element.156, bf16[4,512,2,64]{3,2,1,0:T(2,128)(2,1)S(1)} %bitcast.77, f32[4,2,128,512]{3,2,1,0:T(8,128)} %get-tuple-element.146, f32[4,2,128]{2,1,0:T(2,128)S(1)} %get-tuple-element.147), kind=kOutput, calls=%fused_computation.10.clone.1 | convolution fusion | flops 68222976 | bytes 2757120 | tf_op jit(solution)/shard_map/while/body/eval_jaxpr/bhij,bjhd->bihd/dot_general | solution.py:86
  140.0 2.7 %gather_fusion.1 = bf16[16,128,2,64]{3,2,1,0:T(2,128)(2,1)S(1)} fusion(bf16[8,128,2,64]{3,2,1,0:T(2,128)(2,1)S(1)} %get-tuple-element.170, s32[1024]{0:T(1024)S(1)} %pad_clamp_fusion.2), kind=kCustom, calls=%fused_computation.1.clone.clone.1 | custom fusion | bytes 1048640 | tf_op jit(solution)/shard_map/while/body/eval_jaxpr/gather | solution.py:79
  142.8 3.1 %fusion.69 = (f32[4,2,128]{2,1,0:T(2,128)S(1)}, f32[4,2,128,512]{3,2,1,0:T(8,128)}) fusion(pred[4,512]{1,0:T(4,128)(4,1)S(1)} %bitcast.83, bf16[4,512,2,64]{3,2,1,0:T(2,128)(2,1)S(1)} %bitcast.76, bf16[4,4,128,2,64]{2,4,3,1,0:T(8,128)(2,1)} %get-tuple-element.169, s32[]{:T(128)} %get-tuple-element.156), kind=kOutput, calls=%fused_computation.51.clone.1 | convolution fusion | flops 69206528 | bytes 2759168 | tf_op jit(solution)/shard_map/while/body/eval_jaxpr/sub | solution.py:16
  148.6 2.9 %fusion.70 = bf16[4,4,128,2,64]{2,4,3,1,0:T(8,128)(2,1)} fusion(bf16[4,4,128,2,64]{2,4,3,1,0:T(8,128)(2,1)} %get-tuple-element.157, s32[]{:T(128)} %get-tuple-element.156, bf16[4,512,2,64]{3,2,1,0:T(2,128)(2,1)S(1)} %bitcast.77, f32[4,2,128,512]{3,2,1,0:T(8,128)} %get-tuple-element.146, f32[4,2,128]{2,1,0:T(2,128)S(1)} %get-tuple-element.147), kind=kOutput, calls=%fused_computation.10.clone.1 | convolution fusion | flops 68222976 | bytes 2757120 | tf_op jit(solution)/shard_map/while/body/eval_jaxpr/bhij,bjhd->bihd/dot_general | solution.py:86
  154.3 43.2 %all_to_all.80 = bf16[64,32,128]{2,1,0:T(8,128)(2,1)S(1)} all-to-all(bf16[64,32,128]{2,1,0:T(8,128)(2,1)S(1)} %all_to_all.69), channel_id=1, replica_groups=mesh['grp'=8,'wide'=64] {'wide'}, dimensions={0} | all-to-all | bytes 1048576 | tf_op jit(solution)/shard_map/all_to_all | solution.py:94
  197.6 16.5 %all_to_all.81 = bf16[8,256,128]{2,1,0:T(8,128)(2,1)S(1)} all-to-all(bf16[8,256,128]{2,1,0:T(8,128)(2,1)S(1)} %bitcast.79), channel_id=1, replica_groups=mesh['grp'=8,'wide'=64] {'grp'}, dimensions={0} | all-to-all | bytes 1048576 | tf_op jit(solution)/shard_map/all_to_all | solution.py:93
  (73 shorter events, 29.0 us)
Async XLA Ops:
  6.5 210.6 %copy-start = (bf16[1024,512]{1,0:T(8,128)(2,1)S(1)}, bf16[1024,512]{1,0:T(8,128)(2,1)}, u32[]{:S(2)}) copy-start(bf16[1024,512]{1,0:T(8,128)(2,1)} %param.18) | copy-start | bytes 3145732
  6.5 43.6 %all-gather.3.cloned.1.call-start = ((), (), s32[]{:S(2)}) async-start(), calls=%async_computation.6 | async-start | bytes 2359296 | tf_op jit(solution)/shard_map/all_gather | solution.py:45
  7.3 83.8 %all-gather.5.cloned.1.call-start = ((), (), s32[]{:S(2)}) async-start(), calls=%async_computation.7 | async-start | bytes 2359296 | tf_op jit(solution)/shard_map/all_gather | solution.py:44
  8.0 42.1 %copy-start.3 = (bf16[128,1024]{1,0:T(8,128)(2,1)S(1)}, bf16[128,1024]{1,0:T(8,128)(2,1)}, u32[]{:S(2)}) copy-start(bf16[128,1024]{1,0:T(8,128)(2,1)} %param.11) | copy-start | bytes 786436
  9.3 42.9 %copy-start.1 = (bf16[256,1024]{0,1:T(8,128)(2,1)}, bf16[256,1024]{0,1:T(8,128)(2,1)S(1)}, u32[]{:S(2)}) copy-start(bf16[256,1024]{0,1:T(8,128)(2,1)S(1)} %copy.26) | copy-start | bytes 1572868
  29.0 43.9 %all-to-all-start.2 = ((bf16[64,32,128]{2,1,0:T(8,128)(2,1)}), bf16[64,32,128]{2,1,0:T(8,128)(2,1)S(1)}, u32[]{:S(2)}, u32[]{:S(2)}) async-start(bf16[64,32,128]{2,1,0:T(8,128)(2,1)} %bitcast.6), calls=%async_computation.2 | async-start | bytes 1048576 | tf_op jit(solution)/shard_map/all_to_all | solution.py:57
  72.9 25.3 %copy-start.5 = (s32[16,4]{0,1:T(4,128)S(1)}, s32[16,4]{0,1:T(4,128)}, u32[]{:S(2)}) copy-start(s32[16,4]{0,1:T(4,128)} %param.15) | copy-start | bytes 772
  72.9 25.4 %copy-start.6 = (s32[16]{0:T(128)S(1)}, s32[16]{0:T(128)}, u32[]{:S(2)}) copy-start(s32[16]{0:T(128)} %param.16) | copy-start | bytes 196
  72.9 21.0 %all-to-all-start = ((bf16[128,8,128]{0,2,1:T(8,128)(2,1)}), bf16[128,8,128]{0,2,1:T(8,128)(2,1)S(1)}, u32[]{:S(2)}, u32[]{:S(2)}) async-start(bf16[128,8,128]{0,2,1:T(8,128)(2,1)} %bitcast.1), calls=%async_computation | async-start | bytes 524288 | tf_op jit(solution)/shard_map/all_to_all | solution.py:55
  93.9 10.7 %all-to-all-start.3 = ((bf16[128,8,128]{0,2,1:T(8,128)(2,1)}), bf16[128,8,128]{0,2,1:T(8,128)(2,1)S(1)}, u32[]{:S(2)}, u32[]{:S(2)}) async-start(bf16[128,8,128]{0,2,1:T(8,128)(2,1)} %bitcast.7), calls=%async_computation.3 | async-start | bytes 524288 | tf_op jit(solution)/shard_map/all_to_all | solution.py:54
  197.6 19.1 %copy-start.2 = (bf16[256,1024]{0,1:T(8,128)(2,1)S(1)}, bf16[256,1024]{0,1:T(8,128)(2,1)}, u32[]{:S(2)}) copy-start(bf16[256,1024]{0,1:T(8,128)(2,1)} %copy-done.1) | copy-start | bytes 1572868
  215.1 1.8 copy-start.4
  216.7 0.7 copy-start.7
Sparse Core Ops, SparseCore 0:
  9.5 40.6 all-gather.2
  52.2 38.7 all-gather.4
where the time goes:
time: 226 us; the launch traced here: 225 us
  blocking collectives  78.4 us (35%)
  waiting for transfers between devices  41.5 us (18%)
  local copies, waits for them, and re-layouts  33.7 us (15%)
  matrix products  29.3 us (13%)
  starting transfers between devices  27.1 us (12%)
  between operations  13.5 us (6%)
    all_to_all x1, blocking collectives, body(): lax.all_to_all(attended, 'wide', split_axis=0, concat_axis=0, tiled=True)  43.2 us
    all_to_all x1, waiting for transfers between devices, body(): lax.all_to_all(lax.all_to_all(panel_query, 'grp', split_axis=1, concat_ax...  19.9 us
    all_to_all x1, blocking collectives, body(): lax.all_to_all(panel_query, 'grp', split_axis=1, concat_axis=0, tiled=True)  18.6 us
    all_to_all x1, blocking collectives, body(): lax.all_to_all(lax.all_to_all(attended, 'wide', split_axis=0, concat_axis...  16.5 us
    all_to_all x1, starting transfers between devices, body(): lax.all_to_all(lax.all_to_all(panel_query, 'grp', split_axis=1, concat_ax...  14.8 us
    sub x4, matrix products, softmax_rows(): expo = jnp.exp(scores - top)  12.3 us
    dot_general x4, matrix products, attend(): jnp.einsum('bhij,bjhd->bihd', weights, picked_values, preferred_element_t...  11.7 us
    gather x4, local copies, waits for them, and re-layouts, attend(): key_blocks[listed].reshape(per_step, LMAX * BLK, local_heads, HD)  10.6 us
  transfers between devices with their start and end apart: 5, of which 4 were waited for; matrix products, arithmetic and copies ran while one was open for 5% of the time, Pallas kernels for 0%

commit v1 on v0

v1 whole, which is shorter than its diff:
```python
import functools
import math

import jax
import jax.numpy as jnp
from jax import lax
from jax.experimental import pallas as pl
from jax.experimental.pallas import tpu as pltpu
from jax.sharding import Mesh
from jax.sharding import PartitionSpec as P

BLK = 128
LMAX = 4
HD = 64
SLAB = 32
GRP = ("x", "core")
PLANE = ("x", "core", "y")


def exchange(array, axes):
    return lax.all_to_all(array, axes, split_axis=0, concat_axis=0, tiled=True)


def attend_kernel(cells_ref, counts_ref, query_ref, keys_ref, values_ref, out_ref):
    block = pl.program_id(0)
    parts, _, part_rows, width = out_ref.shape
    slab_part = SLAB // parts
    to_row = lax.broadcasted_iota(jnp.int32, (BLK, BLK), 0)
    from_row = lax.broadcasted_iota(jnp.int32, (BLK, BLK), 1)
    part, rest = to_row // part_rows, to_row % part_rows
    wanted = rest // slab_part * SLAB + part * slab_part + rest % slab_part
    select = (from_row == wanted).astype(jnp.bfloat16)
    query = jnp.dot(select, query_ref[0], preferred_element_type=jnp.float32)
    scaled = query * (1.0 / math.sqrt(HD))
    first = lax.broadcasted_iota(jnp.int32, (BLK, width), 1) < HD
    both = jnp.concatenate(
        [jnp.where(first, scaled, 0.0), jnp.where(first, 0.0, scaled)], axis=0
    ).astype(jnp.bfloat16)
    picked = [
        pl.multiple_of(jnp.clip(cells_ref[block, slot], 0, keys_ref.shape[0] // BLK - 1) * BLK, BLK)
        for slot in range(LMAX)
    ]
    keys = jnp.concatenate([keys_ref[pl.ds(row, BLK), :] for row in picked], axis=0)
    values = jnp.concatenate([values_ref[pl.ds(row, BLK), :] for row in picked], axis=0)
    scores = lax.dot_general(
        both, keys, (((1,), (1,)), ((), ())), preferred_element_type=jnp.float32
    )
    slot_of = lax.broadcasted_iota(jnp.int32, (1, LMAX * BLK), 1) // BLK
    scores = jnp.where(slot_of < counts_ref[block], scores, -jnp.inf)
    top = jnp.max(scores, axis=-1, keepdims=True)
    expo = jnp.exp(scores - top)
    total = jnp.sum(expo, axis=-1, keepdims=True)
    summed = jnp.dot(expo.astype(jnp.bfloat16), values, preferred_element_type=jnp.float32) / total
    attended = jnp.where(first, summed[:BLK], summed[BLK:]).astype(jnp.bfloat16)
    stream = query + attended.astype(jnp.float32)
    out_ref[:, 0] = stream.astype(jnp.bfloat16).reshape(parts, part_rows, width)


def attend(query, keys, values, cells, counts, parts):
    blocks, _, width = query.shape
    part_rows = BLK // parts
    return pl.pallas_call(
        attend_kernel,
        out_shape=jax.ShapeDtypeStruct((parts, blocks, part_rows, width), jnp.bfloat16),
        grid_spec=pltpu.PrefetchScalarGridSpec(
            num_scalar_prefetch=2,
            grid=(blocks,),
            in_specs=[
                pl.BlockSpec((1, BLK, width), lambda i, *_: (i, 0, 0)),
                pl.BlockSpec(keys.shape, lambda i, *_: (0, 0)),
                pl.BlockSpec(values.shape, lambda i, *_: (0, 0)),
            ],
            out_specs=pl.BlockSpec((parts, 1, part_rows, width), lambda i, *_: (0, i, 0, 0)),
        ),
        name="attend",
    )(cells, counts, query, keys, values)


def flux_kernel(stream_ref, gain_ref, up_ref, flux_ref, out_ref):
    groups = stream_ref.shape[0]
    stream = jnp.concatenate(
        [stream_ref[h].astype(jnp.float32) for h in range(groups)], axis=1
    )
    scale = lax.rsqrt(jnp.mean(stream * stream, axis=-1, keepdims=True) + 1e-06)
    normed = (stream * scale * gain_ref[...]).astype(jnp.bfloat16)
    hidden = jax.nn.gelu(
        jnp.dot(normed, up_ref[...], preferred_element_type=jnp.float32)
    ).astype(jnp.bfloat16)
    out_ref[...] = lax.dot_general(
        flux_ref[...], hidden, (((1,), (1,)), ((), ())), preferred_element_type=jnp.float32
    )


def wall_flux(stream, norm_gain, up_weight, flux_weight):
    rows = stream.shape[1]
    return pl.pallas_call(
        flux_kernel,
        out_shape=jax.ShapeDtypeStruct((flux_weight.shape[0], rows), jnp.float32),
        name="wall_flux",
    )(stream, norm_gain[None, :], up_weight, flux_weight)


def body(
    sizes,
    anchor_states,
    key_weight,
    value_weight,
    panel_query,
    cell_list,
    cell_count,
    norm_gain,
    up_weight,
    flux_weight,
):
    grp, n_z, n_y = sizes
    region_anchors = lax.all_gather(anchor_states, GRP, axis=0, tiled=True)
    width = key_weight.shape[1]
    hi = n_z // grp
    query = panel_query.reshape(hi, n_y, SLAB, grp, width).transpose(3, 1, 0, 2, 4)
    query = exchange(query.reshape(grp * n_y, hi * SLAB, width), PLANE)
    query = query.reshape(grp, n_y, hi, SLAB, width).transpose(0, 2, 1, 3, 4)
    query = exchange(query.reshape(n_z, n_y * SLAB, width), "z")
    keys = jnp.dot(region_anchors, key_weight, preferred_element_type=jnp.float32)
    values = jnp.dot(region_anchors, value_weight, preferred_element_type=jnp.float32)
    stream = attend(
        query, keys.astype(jnp.bfloat16), values.astype(jnp.bfloat16), cell_list, cell_count, grp
    )
    stream = exchange(stream, GRP)
    flux = wall_flux(stream.reshape(grp, -1, width), norm_gain, up_weight, flux_weight)
    parts = flux.shape[0]
    few = SLAB // grp
    flux = exchange(flux.reshape(parts, n_z, n_y * few).transpose(1, 0, 2), "z")
    flux = flux.reshape(grp, hi, parts, n_y, few).transpose(0, 3, 1, 2, 4)
    flux = exchange(flux.reshape(grp * n_y, hi * parts, few), PLANE)
    flux = flux.reshape(grp, n_y, hi, parts, few).transpose(3, 2, 1, 0, 4)
    return flux.reshape(parts, -1)


def solution(mesh):
    grp, wide = mesh.devices.shape
    sizes = (grp, 16, wide // 16)
    fine = Mesh(mesh.devices.reshape(grp // 2, 2, 16, wide // 16), ("x", "core", "z", "y"))
    rows = ("z", "y", "x", "core")
    in_specs = (
        P(rows, None),
        P(None, GRP),
        P(None, GRP),
        P(rows, None),
        P(("z", "y"), None),
        P(("z", "y")),
        P(),
        P(),
        P(),
    )
    return jax.shard_map(
        functools.partial(body, sizes),
        mesh=fine,
        in_specs=in_specs,
        out_specs=P(None, rows),
        check_vma=False,
    )
```

time: 226 us -> 146 us (0.65)
  local copies, waits for them, and re-layouts: 33.7 us -> 6.54 us
  matrix products: 29.3 us -> 4.57 us
  waiting for transfers between devices: 41.5 us -> 18.3 us
  Pallas kernels: 0 us -> 15.9 us
  starting transfers between devices: 27.1 us -> 13.8 us
  blocking collectives: 78.4 us -> 71.7 us
    gather x8 -> x0, local copies, waits for them, and re-layouts: 21.2 us -> none  [the longest x4 10.6 us: attend(): key_blocks[listed].reshape(per_step, LMAX * BLK, local_heads, HD)]
    pallas_call x0 -> x2, Pallas kernels: none -> 15.9 us  [the longest x1 13.1 us: attend(): pl.pallas_call(attend_kernel, out_shape=jax.ShapeDtypeStruct((parts, bloc...]
    all_to_all x3 -> x1, starting transfers between devices: 27.1 us -> 13.8 us  [exchange(): return lax.all_to_all(array, axes, split_axis=0, concat_axis=0, tiled=True)]
    all_gather x2 -> x1, waiting for transfers between devices: 16.5 us -> 3.51 us  [body(): region_anchors = lax.all_gather(anchor_states, GRP, axis=0, tiled=True)]
    dot_general x7 -> x2, matrix products: 17 us -> 4.57 us  [the longest x1 3.15 us: body(): jnp.dot(region_anchors, value_weight, preferred_element_type=jnp.float32)]
    sub x4 -> x0, matrix products: 12.3 us -> none  [softmax_rows(): expo = jnp.exp(scores - top)]
    all_to_all x3 -> x1, waiting for transfers between devices: 23.6 us -> 14 us  [exchange(): return lax.all_to_all(array, axes, split_axis=0, concat_axis=0, tiled=True)]
    all_to_all x3 -> x4, blocking collectives: 78.4 us -> 71.7 us  [exchange(): return lax.all_to_all(array, axes, split_axis=0, concat_axis=0, tiled=True)]
  transfers between devices with their start and end apart: 5 -> 2, of which waited for: 4 -> 2; matrix products, arithmetic and copies ran while one was open for 5% -> 5% of each run, Pallas kernels for 0% -> 0%
where the time goes in v1:
time: 146 us; the launch traced here: 144 us
  blocking collectives  71.7 us (49%)
  waiting for transfers between devices  18.3 us (13%)
  Pallas kernels  15.9 us (11%)
  starting transfers between devices  13.8 us (9%)
  between operations  13.5 us (9%)
  local copies, waits for them, and re-layouts  6.54 us (4%)
  matrix products  4.57 us (3%)
    all_to_all x4, blocking collectives, exchange(): return lax.all_to_all(array, axes, split_axis=0, concat_axis=0, tiled=True)  71.7 us
    all_to_all x1, waiting for transfers between devices, exchange(): return lax.all_to_all(array, axes, split_axis=0, concat_axis=0, tiled=True)  14 us
    all_to_all x1, starting transfers between devices, exchange(): return lax.all_to_all(array, axes, split_axis=0, concat_axis=0, tiled=True)  13.8 us
    pallas_call x1, Pallas kernels, attend(): pl.pallas_call(attend_kernel, out_shape=jax.ShapeDtypeStruct((parts, bloc...  13.1 us
    all_gather x1, waiting for transfers between devices, body(): region_anchors = lax.all_gather(anchor_states, GRP, axis=0, tiled=True)  3.51 us
    dot_general x1, matrix products, body(): jnp.dot(region_anchors, value_weight, preferred_element_type=jnp.float32)  3.15 us
  transfers between devices with their start and end apart: 2, of which 2 were waited for; matrix products, arithmetic and copies ran while one was open for 5% of the time, Pallas kernels for 0%

profile of v1, /device:TPU:1, one launch (start us, length us, event | category | flops | bytes accessed | tf_op | source)
XLA Modules:
  0.0 144.2 jit_solution(18084411920067963854)
XLA Ops:
  6.5 0.7 all-gather.2.cloned.1.call-update
  7.3 1.1 copy.31
  8.4 0.1 copy.20
  8.5 20.7 %all_to_all.25 = bf16[32,64,128]{2,1,0:T(8,128)(2,1)S(1)} all-to-all(bf16[32,64,128]{2,1,0:T(8,128)(2,1)S(1)} %bitcast.30), channel_id=1, replica_groups=mesh['x'=4,'core'=2,'z'=16,'y'=4] {'x','core','y'}, dimensions={0} | all-to-all | bytes 1048576 | tf_op jit(solution)/shard_map/all_to_all | solution.py:21
  29.2 0.9 copy.21
  30.1 13.8 %all-to-all-start.1 = ((bf16[16,128,128]{2,1,0:T(8,128)(2,1)}), bf16[16,128,128]{2,1,0:T(8,128)(2,1)S(1)}, u32[]{:S(2)}, u32[]{:S(2)}) async-start(bf16[16,128,128]{2,1,0:T(8,128)(2,1)} %bitcast.4), calls=%async_computation.1 | async-start | bytes 1048576 | tf_op jit(solution)/shard_map/all_to_all | solution.py:21
  43.9 0.7 copy.22.cells_ref
  44.6 3.5 %all-gather.2.cloned.1.call-done = bf16[1024,1024]{1,0:T(8,128)(2,1)} async-done(((bf16[128,1024]{1,0:T(8,128)(2,1)}), bf16[1024,1024]{1,0:T(8,128)(2,1)}) %all-gather.2.cloned.1.call-update) | async-done | bytes 2097168 | tf_op jit(solution)/shard_map/all_gather | solution.py:116
  48.1 3.1 %convolution_convert_fusion.values_ref = bf16[1024,128]{1,0:T(8,128)(2,1)} fusion(bf16[1024,1024]{1,0:T(8,128)(2,1)} %all-gather.2.cloned.1.call-done, bf16[1024,128]{1,0:T(8,128)(2,1)S(1)} %copy-done), kind=kOutput, calls=%fused_computation | convolution fusion | flops 268566528 | bytes 2621440 | tf_op jit(solution)/shard_map/dot_general | solution.py:124
  51.2 1.4 convolution_convert_fusion.1.keys_ref
  52.7 14.0 %all-to-all-done.1.query_ref = bf16[16,128,128]{2,1,0:T(8,128)(2,1)S(1)} async-done(((bf16[16,128,128]{2,1,0:T(8,128)(2,1)}), bf16[16,128,128]{2,1,0:T(8,128)(2,1)S(1)}, u32[]{:S(2)}, u32[]{:S(2)}) %all-to-all-start.1) | async-done | bytes 524320 | tf_op jit(solution)/shard_map/all_to_all | solution.py:21
  66.7 0.8 copy-done.2
  67.5 13.1 %attend.1 = bf16[8,16,16,128]{3,2,1,0:T(8,128)(2,1)} custom-call(s32[16,4]{1,0:T(8,128)} %copy.22.cells_ref, s32[16]{0:T(128)} %counts_ref.1, bf16[16,128,128]{2,1,0:T(8,128)(2,1)} %copy-done.2, bf16[1024,128]{1,0:T(8,128)(2,1)} %convolution_convert_fusion.1.keys_ref, bf16[1024,128]{1,0:T(8,128)(2,1)} %convolution_convert_fusion.values_ref), custom_call_target="tpu_custom_call" | custom-call | tf_op jit(solution)/shard_map/attend/pallas_call | solution.py:62
  80.6 20.5 %all_to_all.26 = bf16[8,16,16,128]{3,2,1,0:T(8,128)(2,1)} all-to-all(bf16[8,16,16,128]{3,2,1,0:T(8,128)(2,1)} %attend.1), channel_id=1, replica_groups=mesh['x'=4,'core'=2,'z'=16,'y'=4] {'x','core'}, dimensions={0} | all-to-all | bytes 1048576 | tf_op jit(solution)/shard_map/all_to_all | solution.py:21
  101.1 2.8 %wall_flux.1 = f32[4,256]{1,0:T(4,128)} custom-call(bf16[8,256,128]{2,1,0:T(8,128)(2,1)} %bitcast.29, f32[1,1024]{1,0:T(1,128)} %bitcast.37, bf16[1024,512]{1,0:T(8,128)(2,1)} %up_ref.1, bf16[4,512]{1,0:T(4,128)(2,1)} %flux_ref.1), custom_call_target="tpu_custom_call" | custom-call | tf_op jit(solution)/shard_map/wall_flux/pallas_call | solution.py:96
  103.9 0.8 reshape.35
  104.7 17.5 %all_to_all.27 = f32[16,4,16]{2,1,0:T(4,128)S(1)} all-to-all(f32[16,4,16]{2,1,0:T(4,128)S(1)} %bitcast.36), channel_id=1, replica_groups=mesh['x'=4,'core'=2,'z'=16,'y'=4] {'z'}, dimensions={0} | all-to-all | bytes 8192 | tf_op jit(solution)/shard_map/all_to_all | solution.py:21
  122.2 0.1 reshape.36
  122.3 0.5 copy.29
  122.8 0.1 reshape.40
  123.0 12.9 %all_to_all.28 = f32[32,8,4]{1,2,0:T(4,128)S(1)} all-to-all(f32[32,8,4]{1,2,0:T(4,128)S(1)} %reshape.40), channel_id=1, replica_groups=mesh['x'=4,'core'=2,'z'=16,'y'=4] {'x','core','y'}, dimensions={0} | all-to-all | bytes 8192 | tf_op jit(solution)/shard_map/all_to_all | solution.py:21
  136.0 0.1 reshape.38
  136.1 0.5 copy.28
  136.6 0.7 reshape.39
  (13 shorter events, 0.1 us)
Async XLA Ops:
  6.5 41.5 %copy-start = (bf16[1024,128]{1,0:T(8,128)(2,1)S(1)}, bf16[1024,128]{1,0:T(8,128)(2,1)}, u32[]{:S(2)}) copy-start(bf16[1024,128]{1,0:T(8,128)(2,1)} %param.11) | copy-start | bytes 786436
  6.5 41.5 %all-gather.2.cloned.1.call-start = ((), (), s32[]{:S(2)}) async-start(), calls=%async_computation.5 | async-start | bytes 2359296 | tf_op jit(solution)/shard_map/all_gather | solution.py:116
  8.4 35.5 %copy-start.4 = (s32[16,4]{0,1:T(4,128)S(1)}, s32[16,4]{0,1:T(4,128)}, u32[]{:S(2)}) copy-start(s32[16,4]{0,1:T(4,128)} %param.13) | copy-start | bytes 772
  30.1 21.2 %copy-start.3 = (bf16[1024,128]{1,0:T(8,128)(2,1)S(1)}, bf16[1024,128]{1,0:T(8,128)(2,1)}, u32[]{:S(2)}) copy-start(bf16[1024,128]{1,0:T(8,128)(2,1)} %param.10) | copy-start | bytes 786436
  30.1 36.6 %all-to-all-start.1 = ((bf16[16,128,128]{2,1,0:T(8,128)(2,1)}), bf16[16,128,128]{2,1,0:T(8,128)(2,1)S(1)}, u32[]{:S(2)}, u32[]{:S(2)}) async-start(bf16[16,128,128]{2,1,0:T(8,128)(2,1)} %bitcast.4), calls=%async_computation.1 | async-start | bytes 1048576 | tf_op jit(solution)/shard_map/all_to_all | solution.py:21
  48.1 3.2 %copy-start.1 = (bf16[1024,1024]{1,0:T(8,128)(2,1)S(1)}, bf16[1024,1024]{1,0:T(8,128)(2,1)}, u32[]{:S(2)}) copy-start(bf16[1024,1024]{1,0:T(8,128)(2,1)} %all-gather.2.cloned.1.call-done) | copy-start | bytes 6291460
  66.7 0.8 copy-start.2
Sparse Core Ops, SparseCore 0:
  9.5 38.5 all-gather.1

commit v2 on v1

v2 whole, which is shorter than its diff:
```python
import functools
import math

import jax
import jax.numpy as jnp
from jax import lax
from jax.experimental import pallas as pl
from jax.experimental.pallas import tpu as pltpu
from jax.sharding import Mesh
from jax.sharding import PartitionSpec as P

BLK = 128
LMAX = 4
HD = 64
SLAB = 32
GRP = ("x", "core")
PLANE = ("x", "core", "y")


def exchange(array, axes):
    return lax.all_to_all(array, axes, split_axis=0, concat_axis=0, tiled=True)


def attend_step(step, per, place_ref, cells_ref, counts_ref, query_ref, kv_ref, out_ref):
    parts, _, part_rows, width = out_ref.shape
    cells = kv_ref.shape[0] // BLK
    first = lax.broadcasted_iota(jnp.int32, (BLK, width), 1) < HD
    for item in range(per):
        block = step * per + item
        query = query_ref[block].astype(jnp.float32)
        scaled = query * (1.0 / math.sqrt(HD))
        both = jnp.concatenate(
            [jnp.where(first, scaled, 0.0), jnp.where(first, 0.0, scaled)], axis=0
        ).astype(jnp.bfloat16)
        picked = []
        for slot in range(LMAX):
            cell = jnp.clip(cells_ref[block * LMAX + slot], 0, cells - 1)
            far = (cell // 2 - place_ref[0] + cells) % (cells // 2)
            row = far + (cells // 2) * ((cell + place_ref[1]) % 2)
            picked.append(pl.multiple_of(row * BLK, BLK))
        keys = jnp.concatenate([kv_ref[pl.ds(row, BLK), :width] for row in picked], axis=0)
        values = jnp.concatenate([kv_ref[pl.ds(row, BLK), width:] for row in picked], axis=0)
        scores = lax.dot_general(
            both, keys, (((1,), (1,)), ((), ())), preferred_element_type=jnp.float32
        )
        slot_of = lax.broadcasted_iota(jnp.int32, (1, LMAX * BLK), 1) // BLK
        scores = scores + jnp.where(slot_of < counts_ref[block], 0.0, -jnp.inf)
        top = jnp.max(scores, axis=-1, keepdims=True)
        expo = jnp.exp(scores - top)
        total = jnp.sum(expo, axis=-1, keepdims=True)
        summed = jnp.dot(expo.astype(jnp.bfloat16), values, preferred_element_type=jnp.float32)
        summed = summed / total
        attended = jnp.where(first, summed[:BLK], summed[BLK:]).astype(jnp.bfloat16)
        stream = query + attended.astype(jnp.float32)
        out_ref[:, block] = stream.astype(jnp.bfloat16).reshape(parts, part_rows, width)


def attend_kernel(per, *refs):
    steps = refs[3].shape[0] // per
    lax.fori_loop(0, steps, lambda step, _: attend_step(step, per, *refs), None)


def attend(query, kv, place, cells, counts, parts, per):
    blocks, _, width = query.shape
    return pl.pallas_call(
        functools.partial(attend_kernel, per),
        out_shape=jax.ShapeDtypeStruct((parts, blocks, BLK // parts, width), jnp.bfloat16),
        in_specs=[pl.BlockSpec(memory_space=pltpu.SMEM)] * 3
        + [pl.BlockSpec(memory_space=pltpu.VMEM)] * 2,
        out_specs=pl.BlockSpec(memory_space=pltpu.VMEM),
        name="attend",
    )(place, cells, counts, query, kv)


def flux_kernel(stream_ref, gain_ref, up_ref, flux_ref, out_ref):
    groups = stream_ref.shape[0]
    stream = jnp.concatenate(
        [stream_ref[h].astype(jnp.float32) for h in range(groups)], axis=1
    )
    scale = lax.rsqrt(jnp.mean(stream * stream, axis=-1, keepdims=True) + 1e-06)
    normed = (stream * scale * gain_ref[...]).astype(jnp.bfloat16)
    hidden = jax.nn.gelu(
        jnp.dot(normed, up_ref[...], preferred_element_type=jnp.float32)
    ).astype(jnp.bfloat16)
    flux = lax.dot_general(
        flux_ref[...], hidden, (((1,), (1,)), ((), ())), preferred_element_type=jnp.float32
    )
    for block in range(out_ref.shape[0]):
        few = out_ref.shape[2]
        out_ref[block] = flux[:, block * few : (block + 1) * few]


def wall_flux(stream, norm_gain, up_weight, flux_weight, blocks):
    few = stream.shape[1] // blocks
    return pl.pallas_call(
        flux_kernel,
        out_shape=jax.ShapeDtypeStruct((blocks, flux_weight.shape[0], few), jnp.float32),
        name="wall_flux",
    )(stream, norm_gain[None, :], up_weight, flux_weight)


def place_kernel(y_ref, flux_ref, out_ref):
    _, halves, n_y, both, few = flux_ref.shape
    comps = out_ref.shape[0]
    mine = flux_ref[y_ref[0]]
    pieces = [
        mine[half, low, top * comps : (top + 1) * comps]
        for top in range(both // comps)
        for low in range(n_y)
        for half in range(halves)
    ]
    out_ref[...] = jnp.concatenate(pieces, axis=1)


def place_flux(flux, comps, y):
    return pl.pallas_call(
        place_kernel,
        out_shape=jax.ShapeDtypeStruct((comps, flux[0].size // comps), jnp.float32),
        in_specs=[
            pl.BlockSpec(memory_space=pltpu.SMEM),
            pl.BlockSpec(memory_space=pltpu.VMEM),
        ],
        name="place_flux",
    )(y, flux)


def body(
    sizes,
    anchor_states,
    key_weight,
    value_weight,
    panel_query,
    cell_list,
    cell_count,
    norm_gain,
    up_weight,
    flux_weight,
):
    n_x, n_z, n_y = sizes
    grp = 2 * n_x
    width = key_weight.shape[1]
    hi = n_z // grp
    query = panel_query.reshape(hi, n_y, SLAB, grp, width).transpose(3, 1, 0, 2, 4)
    query = exchange(query.reshape(grp * n_y, hi * SLAB, width), PLANE)
    query = query.reshape(grp, n_y, hi, SLAB, width).transpose(0, 2, 1, 3, 4)
    query = query.reshape(n_z, n_y * SLAB, width)
    query, anchors = lax.optimization_barrier((query, anchor_states))
    query = exchange(query, "z")
    along = [anchors] + [
        lax.ppermute(anchors, "x", [((i + far) % n_x, i) for i in range(n_x)])
        for far in range(1, n_x)
    ]
    along = jnp.concatenate(along, axis=0)
    across = lax.ppermute(along, "core", [(0, 1), (1, 0)])
    weights = jnp.concatenate([key_weight, value_weight], axis=1)
    kv = jnp.concatenate(
        [
            jnp.dot(part, weights, preferred_element_type=jnp.float32).astype(jnp.bfloat16)
            for part in (along, across)
        ],
        axis=0,
    )
    place = jnp.stack([lax.axis_index("x"), lax.axis_index("core")]).astype(jnp.int32)
    stream = attend(query, kv, place, cell_list.reshape(-1), cell_count, grp, 4)
    stream = exchange(stream, GRP)
    flux = wall_flux(
        stream.reshape(grp, -1, width), norm_gain, up_weight, flux_weight, n_z
    )
    comps = flux_weight.shape[0]
    few = flux.shape[2]
    flux = exchange(flux, "z").reshape(grp, 1, hi * comps, few)
    flux = jnp.broadcast_to(flux, (grp, n_y, hi * comps, few))
    flux = exchange(flux.reshape(grp * n_y, hi * comps, few), PLANE)
    return place_flux(
        flux.reshape(n_x, 2, n_y, hi * comps, few), comps, lax.axis_index("y").reshape(1)
    )


def solution(mesh):
    grp, wide = mesh.devices.shape
    sizes = (grp // 2, 16, wide // 16)
    fine = Mesh(mesh.devices.reshape(grp // 2, 2, 16, wide // 16), ("x", "core", "z", "y"))
    rows = ("z", "y", "x", "core")
    in_specs = (
        P(rows, None),
        P(None, GRP),
        P(None, GRP),
        P(rows, None),
        P(("z", "y"), None),
        P(("z", "y")),
        P(),
        P(),
        P(),
    )
    return jax.shard_map(
        functools.partial(body, sizes),
        mesh=fine,
        in_specs=in_specs,
        out_specs=P(None, rows),
        check_vma=False,
    )
```

time: 146 us -> 130 us (0.89)
  starting transfers between devices: 13.8 us -> 30.3 us
  blocking collectives: 71.7 us -> 57.4 us
  between operations: 13.5 us -> 0.17 us
  Pallas kernels: 15.9 us -> 12.1 us
  matrix products: 4.57 us -> 0.88 us
  other arithmetic: 0 us -> 2.05 us
    all_to_all x4 -> x3, blocking collectives: 71.7 us -> 57.4 us  [exchange(): return lax.all_to_all(array, axes, split_axis=0, concat_axis=0, tiled=True)]
    ppermute x0 -> x4, waiting for transfers between devices: none -> 12 us  [the longest x3 12 us: body(): lax.ppermute(anchors, 'x', [((i + far) % n_x, i) for i in range(n_x)])]
    ppermute x0 -> x4, starting transfers between devices: none -> 10.7 us  [the longest x3 8.15 us: body(): lax.ppermute(anchors, 'x', [((i + far) % n_x, i) for i in range(n_x)])]
    all_to_all x1 -> x2, waiting for transfers between devices: 14 us -> 7.01 us  [exchange(): return lax.all_to_all(array, axes, split_axis=0, concat_axis=0, tiled=True)]
    all_to_all x1 -> x2, starting transfers between devices: 13.8 us -> 19.6 us  [exchange(): return lax.all_to_all(array, axes, split_axis=0, concat_axis=0, tiled=True)]
    pallas_call x2 -> x3, Pallas kernels: 15.9 us -> 12.1 us  [the longest x1 7.68 us: attend(): pl.pallas_call(functools.partial(attend_kernel, per), out_shape=jax.Shape...]
    dot_general x2, matrix products: 4.57 us -> 0.88 us  [body(): jnp.dot(part, weights, preferred_element_type=jnp.float32)]
    all_gather x1 -> x0, waiting for transfers between devices: 3.51 us -> none  [body(): region_anchors = lax.all_gather(anchor_states, GRP, axis=0, tiled=True)]
  transfers between devices with their start and end apart: 2 -> 6, of which waited for: 2 -> 3; matrix products, arithmetic and copies ran while one was open for 5% -> 2% of each run, Pallas kernels for 0% -> 0%
where the time goes in v2:
time: 130 us; the launch traced here: 129 us
  blocking collectives  57.4 us (44%)
  starting transfers between devices  30.3 us (23%)
  waiting for transfers between devices  19 us (15%)
  Pallas kernels  12.1 us (9%)
  local copies, waits for them, and re-layouts  7.49 us (6%)
  other arithmetic  2.05 us (2%)
    all_to_all x3, blocking collectives, exchange(): return lax.all_to_all(array, axes, split_axis=0, concat_axis=0, tiled=True)  57.4 us
    all_to_all x2, starting transfers between devices, exchange(): return lax.all_to_all(array, axes, split_axis=0, concat_axis=0, tiled=True)  19.6 us
    ppermute x3, waiting for transfers between devices, body(): lax.ppermute(anchors, 'x', [((i + far) % n_x, i) for i in range(n_x)])  12 us
    ppermute x3, starting transfers between devices, body(): lax.ppermute(anchors, 'x', [((i + far) % n_x, i) for i in range(n_x)])  8.15 us
    pallas_call x1, Pallas kernels, attend(): pl.pallas_call(functools.partial(attend_kernel, per), out_shape=jax.Shape...  7.68 us
    all_to_all x2, waiting for transfers between devices, exchange(): return lax.all_to_all(array, axes, split_axis=0, concat_axis=0, tiled=True)  7.01 us
    unnamed x18, local copies, waits for them, and re-layouts  5.3 us
    pallas_call x1, Pallas kernels, wall_flux(): pl.pallas_call(flux_kernel, out_shape=jax.ShapeDtypeStruct((blocks, flux_...  2.86 us
  transfers between devices with their start and end apart: 6, of which 3 were waited for; matrix products, arithmetic and copies ran while one was open for 2% of the time, Pallas kernels for 0%

profile of v2, /device:TPU:1, one launch (start us, length us, event | category | flops | bytes accessed | tf_op | source)
XLA Modules:
  0.0 129.3 jit_solution(2346117747498351630)
XLA Ops:
  0.0 1.1 copy.16
  1.3 20.7 %all_to_all.25 = bf16[32,64,128]{2,1,0:T(8,128)(2,1)S(1)} all-to-all(bf16[32,64,128]{2,1,0:T(8,128)(2,1)S(1)} %bitcast.23), channel_id=1, replica_groups=mesh['x'=4,'core'=2,'z'=16,'y'=4] {'x','core','y'}, dimensions={0} | all-to-all | bytes 1048576 | tf_op jit(solution)/shard_map/all_to_all | solution.py:21
  21.9 0.8 copy.15
  22.9 3.1 %collective-permute-start = (bf16[128,1024]{1,0:T(8,128)(2,1)S(1)}, bf16[128,1024]{1,0:T(8,128)(2,1)S(1)}, u32[]{:S(2)}, u32[]{:S(2)}) collective-permute-start(bf16[128,1024]{1,0:T(8,128)(2,1)S(1)} %copy-done.1), channel_id=1, source_target_pairs={{128,0},{256,128},{384,256},{0,384},{129,1},{257,129},{385,257},{1... | collective-permute-start | bytes 786440 | tf_op jit(solution)/shard_map/ppermute | solution.py:150
  26.0 13.7 %all-to-all-start.1 = ((bf16[16,128,128]{2,1,0:T(8,128)(2,1)}), bf16[16,128,128]{2,1,0:T(8,128)(2,1)S(1)}, u32[]{:S(2)}, u32[]{:S(2)}) async-start(bf16[16,128,128]{2,1,0:T(8,128)(2,1)} %bitcast.7), calls=%async_computation.1 | async-start | bytes 1048576 | tf_op jit(solution)/shard_map/all_to_all | solution.py:21
  39.7 3.1 %collective-permute-start.1 = (bf16[128,1024]{1,0:T(8,128)(2,1)S(1)}, bf16[128,1024]{1,0:T(8,128)(2,1)S(1)}, u32[]{:S(2)}, u32[]{:S(2)}) collective-permute-start(bf16[128,1024]{1,0:T(8,128)(2,1)S(1)} %copy-done.1), channel_id=1, source_target_pairs={{256,0},{384,128},{0,256},{128,384},{257,1},{385,129},{1,257},{129... | collective-permute-start | bytes 786440 | tf_op jit(solution)/shard_map/ppermute | solution.py:150
  42.9 1.9 %collective-permute-start.2 = (bf16[128,1024]{1,0:T(8,128)(2,1)S(1)}, bf16[128,1024]{1,0:T(8,128)(2,1)S(1)}, u32[]{:S(2)}, u32[]{:S(2)}) collective-permute-start(bf16[128,1024]{1,0:T(8,128)(2,1)S(1)} %copy-done.1), channel_id=1, source_target_pairs={{384,0},{0,128},{128,256},{256,384},{385,1},{1,129},{129,257},{257... | collective-permute-start | bytes 786440 | tf_op jit(solution)/shard_map/ppermute | solution.py:150
  44.9 5.1 %collective-permute-done.1 = bf16[128,1024]{1,0:T(8,128)(2,1)S(1)} collective-permute-done((bf16[128,1024]{1,0:T(8,128)(2,1)S(1)}, bf16[128,1024]{1,0:T(8,128)(2,1)S(1)}, u32[]{:S(2)}, u32[]{:S(2)}) %collective-permute-start.1) | collective-permute-done | bytes 262176 | tf_op jit(solution)/shard_map/ppermute | solution.py:150
  50.0 6.9 %collective-permute-done.2 = bf16[128,1024]{1,0:T(8,128)(2,1)S(1)} collective-permute-done((bf16[128,1024]{1,0:T(8,128)(2,1)S(1)}, bf16[128,1024]{1,0:T(8,128)(2,1)S(1)}, u32[]{:S(2)}, u32[]{:S(2)}) %collective-permute-start.2) | collective-permute-done | bytes 262176 | tf_op jit(solution)/shard_map/ppermute | solution.py:150
  56.9 2.5 %collective-permute-start.3 = (bf16[512,1024]{1,0:T(8,128)(2,1)S(1)}, bf16[512,1024]{1,0:T(8,128)(2,1)S(1)}, u32[]{:S(2)}, u32[]{:S(2)}) collective-permute-start(bf16[512,1024]{1,0:T(8,128)(2,1)S(1)} %constant_dynamic-update-slice_fusion), channel_id=1, source_target_pairs={{0,64},{64,0},{1,65},{65,1},{2,66},{66,2},{3,67},{67,3},{4,68},{68... | collective-permute-start | bytes 3145736 | tf_op jit(solution)/shard_map/ppermute | solution.py:154
  59.4 0.7 copy-done.4
  61.4 0.9 copy-done.3
  63.3 0.8 pad_maximum_fusion.refs_4_
  64.1 0.8 copy-done
  64.9 7.7 %attend.1 = bf16[8,16,16,128]{3,2,1,0:T(8,128)(2,1)} custom-call(s32[2]{0:T(128)} %pad_add_fusion.refs_0_, s32[64]{0:T(128)} %reshape.30.refs_1_, s32[16]{0:T(128)} %refs_2_.1, bf16[16,128,128]{2,1,0:T(8,128)(2,1)} %copy-done, bf16[1024,256]{1,0:T(8,128)(2,1)} %pad_maximum_fusion.refs_4_), custom_call_target="tpu_custom_call" | custom-call | tf_op jit(solution)/shard_map/attend/pallas_call | solution.py:65
  72.6 19.2 %all_to_all.26 = bf16[8,16,16,128]{3,2,1,0:T(8,128)(2,1)} all-to-all(bf16[8,16,16,128]{3,2,1,0:T(8,128)(2,1)} %attend.1), channel_id=1, replica_groups=mesh['x'=4,'core'=2,'z'=16,'y'=4] {'x','core'}, dimensions={0} | all-to-all | bytes 1048576 | tf_op jit(solution)/shard_map/all_to_all | solution.py:21
  91.8 2.9 %wall_flux.1 = f32[16,4,16]{2,1,0:T(4,128)} custom-call(bf16[8,256,128]{2,1,0:T(8,128)(2,1)} %bitcast.22, f32[1,1024]{1,0:T(1,128)} %bitcast.30, bf16[1024,512]{1,0:T(8,128)(2,1)} %up_ref.1, bf16[4,512]{1,0:T(4,128)(2,1)} %flux_ref.1), custom_call_target="tpu_custom_call" | custom-call | tf_op jit(solution)/shard_map/wall_flux/pallas_call | solution.py:95
  94.6 17.5 %all_to_all.27 = f32[16,4,16]{2,1,0:T(4,128)S(1)} all-to-all(f32[16,4,16]{2,1,0:T(4,128)} %wall_flux.1), channel_id=1, replica_groups=mesh['x'=4,'core'=2,'z'=16,'y'=4] {'z'}, dimensions={0} | all-to-all | bytes 8192 | tf_op jit(solution)/shard_map/all_to_all | solution.py:21
  112.2 0.7 reshape.38
  112.9 5.9 %all-to-all-start.4 = ((f32[32,1,128]{2,1,0:T(1,128)}), f32[32,1,128]{2,1,0:T(1,128)S(1)}, u32[]{:S(2)}, u32[]{:S(2)}) async-start(f32[32,1,128]{2,1,0:T(1,128)} %reshape.38), calls=%async_computation.4 | async-start | bytes 32768 | tf_op jit(solution)/shard_map/all_to_all | solution.py:21
  118.8 7.0 %all-to-all-done.4 = f32[32,1,128]{2,1,0:T(1,128)S(1)} async-done(((f32[32,1,128]{2,1,0:T(1,128)}), f32[32,1,128]{2,1,0:T(1,128)S(1)}, u32[]{:S(2)}, u32[]{:S(2)}) %all-to-all-start.4) | async-done | bytes 16416 | tf_op jit(solution)/shard_map/all_to_all | solution.py:21
  126.3 0.7 reduce
  127.0 0.7 reshape.39
  127.7 1.6 %place_flux.1 = f32[4,256]{1,0:T(4,128)} custom-call(s32[1]{0:T(128)} %bitcast.y_ref, f32[4,2,4,8,16]{4,3,2,1,0:T(8,128)} %bitcast.28), custom_call_target="tpu_custom_call" | custom-call | tf_op jit(solution)/shard_map/place_flux/pallas_call | solution.py:116
  (24 shorter events, 3.1 us)
Async XLA Ops:
  21.9 1.0 copy-start.1
  22.9 21.9 %collective-permute-start = (bf16[128,1024]{1,0:T(8,128)(2,1)S(1)}, bf16[128,1024]{1,0:T(8,128)(2,1)S(1)}, u32[]{:S(2)}, u32[]{:S(2)}) collective-permute-start(bf16[128,1024]{1,0:T(8,128)(2,1)S(1)} %copy-done.1), channel_id=1, source_target_pairs={{128,0},{256,128},{384,256},{0,384},{129,1},{257,129},{385,257},{1... | collective-permute-start | bytes 786440 | tf_op jit(solution)/shard_map/ppermute | solution.py:150
  26.0 38.1 %all-to-all-start.1 = ((bf16[16,128,128]{2,1,0:T(8,128)(2,1)}), bf16[16,128,128]{2,1,0:T(8,128)(2,1)S(1)}, u32[]{:S(2)}, u32[]{:S(2)}) async-start(bf16[16,128,128]{2,1,0:T(8,128)(2,1)} %bitcast.7), calls=%async_computation.1 | async-start | bytes 1048576 | tf_op jit(solution)/shard_map/all_to_all | solution.py:21
  39.7 10.2 %collective-permute-start.1 = (bf16[128,1024]{1,0:T(8,128)(2,1)S(1)}, bf16[128,1024]{1,0:T(8,128)(2,1)S(1)}, u32[]{:S(2)}, u32[]{:S(2)}) collective-permute-start(bf16[128,1024]{1,0:T(8,128)(2,1)S(1)} %copy-done.1), channel_id=1, source_target_pairs={{256,0},{384,128},{0,256},{128,384},{257,1},{385,129},{1,257},{129... | collective-permute-start | bytes 786440 | tf_op jit(solution)/shard_map/ppermute | solution.py:150
  42.9 14.0 %collective-permute-start.2 = (bf16[128,1024]{1,0:T(8,128)(2,1)S(1)}, bf16[128,1024]{1,0:T(8,128)(2,1)S(1)}, u32[]{:S(2)}, u32[]{:S(2)}) collective-permute-start(bf16[128,1024]{1,0:T(8,128)(2,1)S(1)} %copy-done.1), channel_id=1, source_target_pairs={{384,0},{0,128},{128,256},{256,384},{385,1},{1,129},{129,257},{257... | collective-permute-start | bytes 786440 | tf_op jit(solution)/shard_map/ppermute | solution.py:150
  50.0 11.4 %copy-start.2 = (bf16[1024,128]{1,0:T(8,128)(2,1)S(1)}, bf16[1024,128]{1,0:T(8,128)(2,1)}, u32[]{:S(2)}) copy-start(bf16[1024,128]{1,0:T(8,128)(2,1)} %param.10) | copy-start | bytes 786436
  56.9 5.9 %collective-permute-start.3 = (bf16[512,1024]{1,0:T(8,128)(2,1)S(1)}, bf16[512,1024]{1,0:T(8,128)(2,1)S(1)}, u32[]{:S(2)}, u32[]{:S(2)}) collective-permute-start(bf16[512,1024]{1,0:T(8,128)(2,1)S(1)} %constant_dynamic-update-slice_fusion), channel_id=1, source_target_pairs={{0,64},{64,0},{1,65},{65,1},{2,66},{66,2},{3,67},{67,3},{4,68},{68... | collective-permute-start | bytes 3145736 | tf_op jit(solution)/shard_map/ppermute | solution.py:154
  59.4 0.7 copy-start.4
  61.3 1.0 copy-start.3
  64.1 0.8 copy-start
  112.9 12.9 %all-to-all-start.4 = ((f32[32,1,128]{2,1,0:T(1,128)}), f32[32,1,128]{2,1,0:T(1,128)S(1)}, u32[]{:S(2)}, u32[]{:S(2)}) async-start(f32[32,1,128]{2,1,0:T(1,128)} %reshape.38), calls=%async_computation.4 | async-start | bytes 32768 | tf_op jit(solution)/shard_map/all_to_all | solution.py:21

commit v3 on v2

--- a/solution.py
+++ b/solution.py
@@ -13,12 +13,17 @@
 LMAX = 4
 HD = 64
 SLAB = 32
+LANES = 128
 GRP = ("x", "core")
 PLANE = ("x", "core", "y")
 
 
 def exchange(array, axes):
     return lax.all_to_all(array, axes, split_axis=0, concat_axis=0, tiled=True)
+
+
+def on_chip(*arrays):
+    return [pltpu.with_memory_space_constraint(array, pltpu.VMEM) for array in arrays]
 
 
 def attend_step(step, per, place_ref, cells_ref, counts_ref, query_ref, kv_ref, out_ref):
@@ -64,12 +69,11 @@
     blocks, _, width = query.shape
     return pl.pallas_call(
         functools.partial(attend_kernel, per),
-        out_shape=jax.ShapeDtypeStruct((parts, blocks, BLK // parts, width), jnp.bfloat16),
+        out_shape=pltpu.VMEM((parts, blocks, BLK // parts, width), jnp.bfloat16),
         in_specs=[pl.BlockSpec(memory_space=pltpu.SMEM)] * 3
         + [pl.BlockSpec(memory_space=pltpu.VMEM)] * 2,
-        out_specs=pl.BlockSpec(memory_space=pltpu.VMEM),
         name="attend",
-    )(place, cells, counts, query, kv)
+    )(place, cells, counts, *on_chip(query, kv))
 
 
 def flux_kernel(stream_ref, gain_ref, up_ref, flux_ref, out_ref):
@@ -85,26 +89,29 @@
     flux = lax.dot_general(
         flux_ref[...], hidden, (((1,), (1,)), ((), ())), preferred_element_type=jnp.float32
     )
-    for block in range(out_ref.shape[0]):
-        few = out_ref.shape[2]
-        out_ref[block] = flux[:, block * few : (block + 1) * few]
+    blocks = out_ref.shape[0]
+    few = flux.shape[1] // blocks
+    for block in range(blocks):
+        piece = flux[:, block * few : (block + 1) * few]
+        out_ref[block] = jnp.concatenate([piece] * (LANES // few), axis=1)
 
 
 def wall_flux(stream, norm_gain, up_weight, flux_weight, blocks):
-    few = stream.shape[1] // blocks
     return pl.pallas_call(
         flux_kernel,
-        out_shape=jax.ShapeDtypeStruct((blocks, flux_weight.shape[0], few), jnp.float32),
+        out_shape=pltpu.VMEM((blocks, flux_weight.shape[0], LANES), jnp.float32),
+        in_specs=[pl.BlockSpec(memory_space=pltpu.VMEM)] * 4,
         name="wall_flux",
-    )(stream, norm_gain[None, :], up_weight, flux_weight)
+    )(*on_chip(stream, norm_gain[None, :], up_weight, flux_weight))
 
 
 def place_kernel(y_ref, flux_ref, out_ref):
-    _, halves, n_y, both, few = flux_ref.shape
-    comps = out_ref.shape[0]
-    mine = flux_ref[y_ref[0]]
+    _, halves, n_y, both, _ = flux_ref.shape
+    comps, rows = out_ref.shape
+    few = rows * comps // (halves * n_y * both)
+    mine = flux_ref.at[y_ref[0]]
     pieces = [
-        mine[half, low, top * comps : (top + 1) * comps]
+        mine[half, low, top * comps : (top + 1) * comps, :few]
         for top in range(both // comps)
         for low in range(n_y)
         for half in range(halves)
@@ -112,16 +119,16 @@
     out_ref[...] = jnp.concatenate(pieces, axis=1)
 
 
-def place_flux(flux, comps, y):
+def place_flux(flux, comps, rows, y):
     return pl.pallas_call(
         place_kernel,
-        out_shape=jax.ShapeDtypeStruct((comps, flux[0].size // comps), jnp.float32),
+        out_shape=jax.ShapeDtypeStruct((comps, rows), jnp.float32),
         in_specs=[
             pl.BlockSpec(memory_space=pltpu.SMEM),
             pl.BlockSpec(memory_space=pltpu.VMEM),
         ],
         name="place_flux",
-    )(y, flux)
+    )(y, *on_chip(flux))
 
 
 def body(
@@ -144,13 +151,13 @@
     query = exchange(query.reshape(grp * n_y, hi * SLAB, width), PLANE)
     query = query.reshape(grp, n_y, hi, SLAB, width).transpose(0, 2, 1, 3, 4)
     query = query.reshape(n_z, n_y * SLAB, width)
-    query, anchors = lax.optimization_barrier((query, anchor_states))
     query = exchange(query, "z")
-    along = [anchors] + [
-        lax.ppermute(anchors, "x", [((i + far) % n_x, i) for i in range(n_x)])
-        for far in range(1, n_x)
-    ]
-    along = jnp.concatenate(along, axis=0)
+    up = [((i + 1) % n_x, i) for i in range(n_x)]
+    down = [(i, (i + 1) % n_x) for i in range(n_x)]
+    one_up = lax.ppermute(anchor_states, "x", up)
+    one_down = lax.ppermute(anchor_states, "x", down)
+    two_up = lax.ppermute(one_up, "x", up)
+    along = jnp.concatenate([anchor_states, one_up, two_up, one_down], axis=0)
     across = lax.ppermute(along, "core", [(0, 1), (1, 0)])
     weights = jnp.concatenate([key_weight, value_weight], axis=1)
     kv = jnp.concatenate(
@@ -167,12 +174,14 @@
         stream.reshape(grp, -1, width), norm_gain, up_weight, flux_weight, n_z
     )
     comps = flux_weight.shape[0]
-    few = flux.shape[2]
-    flux = exchange(flux, "z").reshape(grp, 1, hi * comps, few)
-    flux = jnp.broadcast_to(flux, (grp, n_y, hi * comps, few))
-    flux = exchange(flux.reshape(grp * n_y, hi * comps, few), PLANE)
+    flux = exchange(flux, "z").reshape(grp, 1, hi * comps, LANES)
+    flux = jnp.broadcast_to(flux, (grp, n_y, hi * comps, LANES))
+    flux = exchange(flux.reshape(grp * n_y, hi * comps, LANES), PLANE)
     return place_flux(
-        flux.reshape(n_x, 2, n_y, hi * comps, few), comps, lax.axis_index("y").reshape(1)
+        flux.reshape(n_x, 2, n_y, hi * comps, LANES),
+        comps,
+        panel_query.shape[0],
+        lax.axis_index("y").reshape(1),
     )
 
 

time: 130 us -> 120 us (0.923)
  blocking collectives: 57.4 us -> 36.9 us
  starting transfers between devices: 30.3 us -> 43.2 us
  Pallas kernels: 12.1 us -> 7.85 us
  waiting for transfers between devices: 19 us -> 22.4 us
  other arithmetic: 2.05 us -> 0.7 us
  local copies, waits for them, and re-layouts: 7.49 us -> 6.15 us
    all_to_all x3 -> x2, blocking collectives: 57.4 us -> 36.9 us  [exchange(): return lax.all_to_all(array, axes, split_axis=0, concat_axis=0, tiled=True)]
    all_to_all x2 -> x3, starting transfers between devices: 19.6 us -> 29.5 us  [exchange(): return lax.all_to_all(array, axes, split_axis=0, concat_axis=0, tiled=True)]
    all_to_all x2 -> x3, waiting for transfers between devices: 7.01 us -> 14.7 us  [exchange(): return lax.all_to_all(array, axes, split_axis=0, concat_axis=0, tiled=True)]
    pallas_call x3, Pallas kernels: 12.1 us -> 7.85 us  [the longest x1 6.32 us: attend(): pl.pallas_call(functools.partial(attend_kernel, per), out_shape=pltpu.VME...]
    ppermute x3, waiting for transfers between devices: 12 us -> 7.74 us  [the longest x1 4.66 us: body(): one_down = lax.ppermute(anchor_states, 'x', down)]
    unnamed x18 -> x20, local copies, waits for them, and re-layouts: 5.3 us -> 2.92 us
    ppermute x3, starting transfers between devices: 8.15 us -> 9.93 us  [the longest x1 4.65 us: body(): one_up = lax.ppermute(anchor_states, 'x', up)]
  transfers between devices with their start and end apart: 6 -> 7, of which waited for: 3 -> 5; matrix products, arithmetic and copies ran while one was open for 2% -> 4% of each run, Pallas kernels for 0% -> 0%
where the time goes in v3:
time: 120 us
  starting transfers between devices  43.2 us (36%)
  blocking collectives  36.9 us (31%)
  waiting for transfers between devices  22.4 us (19%)
  Pallas kernels  7.85 us (7%)
  local copies, waits for them, and re-layouts  6.15 us (5%)
  matrix products  2.1 us (2%)
    all_to_all x2, blocking collectives, exchange(): return lax.all_to_all(array, axes, split_axis=0, concat_axis=0, tiled=True)  36.9 us
    all_to_all x3, starting transfers between devices, exchange(): return lax.all_to_all(array, axes, split_axis=0, concat_axis=0, tiled=True)  29.5 us
    all_to_all x3, waiting for transfers between devices, exchange(): return lax.all_to_all(array, axes, split_axis=0, concat_axis=0, tiled=True)  14.7 us
    pallas_call x1, Pallas kernels, attend(): pl.pallas_call(functools.partial(attend_kernel, per), out_shape=pltpu.VME...  6.32 us
    ppermute x1, waiting for transfers between devices, body(): one_down = lax.ppermute(anchor_states, 'x', down)  4.66 us
    ppermute x1, starting transfers between devices, body(): one_up = lax.ppermute(anchor_states, 'x', up)  4.65 us
    ppermute x1, starting transfers between devices, body(): across = lax.ppermute(along, 'core', [(0, 1), (1, 0)])  3.78 us
    ppermute x1, starting transfers between devices, body(): two_up = lax.ppermute(one_up, 'x', up)  3.16 us
  transfers between devices with their start and end apart: 7, of which 5 were waited for; matrix products, arithmetic and copies ran while one was open for 4% of the time, Pallas kernels for 0%

profile of v3, /device:TPU:1, one launch (start us, length us, event | category | flops | bytes accessed | tf_op | source)
XLA Modules:
  0.0 119.6 jit_solution(1384605844511193708)
XLA Ops:
  0.0 1.1 copy.16
  1.1 0.9 copy.14
  2.1 10.6 %all-to-all-start = ((bf16[32,64,128]{2,1,0:T(8,128)(2,1)}), bf16[32,64,128]{2,1,0:T(8,128)(2,1)S(1)}, u32[]{:S(2)}, u32[]{:S(2)}) async-start(bf16[32,64,128]{2,1,0:T(8,128)(2,1)} %bitcast.4), calls=%async_computation | async-start | bytes 1048576 | tf_op jit(solution)/shard_map/all_to_all | solution.py:22
  12.7 4.6 %collective-permute-start = (bf16[128,1024]{1,0:T(8,128)(2,1)S(1)}, bf16[128,1024]{1,0:T(8,128)(2,1)S(1)}, u32[]{:S(2)}, u32[]{:S(2)}) collective-permute-start(bf16[128,1024]{1,0:T(8,128)(2,1)S(1)} %copy-done.3), channel_id=1, source_target_pairs={{128,0},{256,128},{384,256},{0,384},{129,1},{257,129},{385,257},{1... | collective-permute-start | bytes 786440 | tf_op jit(solution)/shard_map/ppermute | solution.py:157
  17.3 6.5 %all-to-all-done = bf16[32,64,128]{2,1,0:T(8,128)(2,1)S(1)} async-done(((bf16[32,64,128]{2,1,0:T(8,128)(2,1)}), bf16[32,64,128]{2,1,0:T(8,128)(2,1)S(1)}, u32[]{:S(2)}, u32[]{:S(2)}) %all-to-all-start) | async-done | bytes 524320 | tf_op jit(solution)/shard_map/all_to_all | solution.py:22
  23.8 0.9 copy.15
  24.7 13.0 %all-to-all-start.1 = ((bf16[16,128,128]{2,1,0:T(8,128)(2,1)}), bf16[16,128,128]{2,1,0:T(8,128)(2,1)S(1)}, u32[]{:S(2)}, u32[]{:S(2)}) async-start(bf16[16,128,128]{2,1,0:T(8,128)(2,1)} %bitcast.7), calls=%async_computation.1 | async-start | bytes 1048576 | tf_op jit(solution)/shard_map/all_to_all | solution.py:22
  37.6 3.2 %collective-permute-start.1 = (bf16[128,1024]{1,0:T(8,128)(2,1)S(1)}, bf16[128,1024]{1,0:T(8,128)(2,1)S(1)}, u32[]{:S(2)}, u32[]{:S(2)}) collective-permute-start(bf16[128,1024]{1,0:T(8,128)(2,1)S(1)} %collective-permute-done), channel_id=1, source_target_pairs={{128,0},{256,128},{384,256},{0,384},{129,1},{257,129},{385,257},{1... | collective-permute-start | bytes 786440 | tf_op jit(solution)/shard_map/ppermute | solution.py:159
  40.8 2.1 %collective-permute-start.2 = (bf16[128,1024]{1,0:T(8,128)(2,1)S(1)}, bf16[128,1024]{1,0:T(8,128)(2,1)S(1)}, u32[]{:S(2)}, u32[]{:S(2)}) collective-permute-start(bf16[128,1024]{1,0:T(8,128)(2,1)S(1)} %copy-done.3), channel_id=1, source_target_pairs={{0,128},{128,256},{256,384},{384,0},{1,129},{129,257},{257,385},{3... | collective-permute-start | bytes 786440 | tf_op jit(solution)/shard_map/ppermute | solution.py:158
  43.0 3.1 %collective-permute-done.1 = bf16[128,1024]{1,0:T(8,128)(2,1)S(1)} collective-permute-done((bf16[128,1024]{1,0:T(8,128)(2,1)S(1)}, bf16[128,1024]{1,0:T(8,128)(2,1)S(1)}, u32[]{:S(2)}, u32[]{:S(2)}) %collective-permute-start.1) | collective-permute-done | bytes 262176 | tf_op jit(solution)/shard_map/ppermute | solution.py:159
  46.1 4.7 %collective-permute-done.2 = bf16[128,1024]{1,0:T(8,128)(2,1)S(1)} collective-permute-done((bf16[128,1024]{1,0:T(8,128)(2,1)S(1)}, bf16[128,1024]{1,0:T(8,128)(2,1)S(1)}, u32[]{:S(2)}, u32[]{:S(2)}) %collective-permute-start.2) | collective-permute-done | bytes 262176 | tf_op jit(solution)/shard_map/ppermute | solution.py:158
  50.8 3.8 %collective-permute-start.3 = (bf16[512,1024]{1,0:T(8,128)(2,1)S(1)}, bf16[512,1024]{1,0:T(8,128)(2,1)}, u32[]{:S(2)}, u32[]{:S(2)}) collective-permute-start(bf16[512,1024]{1,0:T(8,128)(2,1)S(1)} %constant_dynamic-update-slice_fusion), channel_id=1, source_target_pairs={{0,64},{64,0},{1,65},{65,1},{2,66},{66,2},{3,67},{67,3},{4,68},{68... | collective-permute-start | bytes 3145736 | tf_op jit(solution)/shard_map/ppermute | solution.py:161
  54.6 0.7 copy-done.6
  55.4 0.7 reshape.30.refs_1_
  56.8 0.9 copy-done.5
  58.2 1.7 %convolution_convert_fusion = bf16[512,256]{1,0:T(8,128)(2,1)S(1)} fusion(bf16[512,1024]{1,0:T(8,128)(2,1)} %collective-permute-done.3, bf16[1024,256]{1,0:T(8,128)(2,1)S(1)} %constant_dynamic-update-slice_fusion.4), kind=kOutput, calls=%fused_computation | convolution fusion | flops 268566528 | bytes 1835008 | tf_op jit(solution)/shard_map/dot_general | solution.py:165
  60.5 6.3 %attend.1 = bf16[8,16,16,128]{3,2,1,0:T(8,128)(2,1)S(1)} custom-call(s32[2]{0:T(128)} %pad_add_fusion.refs_0_, s32[64]{0:T(128)} %reshape.30.refs_1_, s32[16]{0:T(128)} %refs_2_.1, bf16[16,128,128]{2,1,0:T(8,128)(2,1)S(1)} %all-to-all-done.1.refs_3_, bf16[1024,256]{1,0:T(8,128)(2,1)S(1)} %pad_maximum_fusion.refs_4_), custom_call_target="tpu_custom_call" | custom-call | tf_op jit(solution)/shard_map/attend/pallas_call | solution.py:70
  66.8 19.6 %all_to_all.25 = bf16[8,16,16,128]{3,2,1,0:T(8,128)(2,1)S(1)} all-to-all(bf16[8,16,16,128]{3,2,1,0:T(8,128)(2,1)S(1)} %attend.1), channel_id=1, replica_groups=mesh['x'=4,'core'=2,'z'=16,'y'=4] {'x','core'}, dimensions={0} | all-to-all | bytes 1048576 | tf_op jit(solution)/shard_map/all_to_all | solution.py:22
  86.4 0.9 wall_flux.1
  87.3 17.3 %all_to_all.26 = f32[16,4,128]{2,1,0:T(4,128)S(1)} all-to-all(f32[16,4,128]{2,1,0:T(4,128)S(1)} %wall_flux.1), channel_id=1, replica_groups=mesh['x'=4,'core'=2,'z'=16,'y'=4] {'z'}, dimensions={0} | all-to-all | bytes 65536 | tf_op jit(solution)/shard_map/all_to_all | solution.py:22
  104.6 0.7 broadcast_in_dim.12
  105.3 5.9 %all-to-all-start.4 = ((f32[32,8,128]{2,1,0:T(8,128)}), f32[32,8,128]{2,1,0:T(8,128)S(1)}, u32[]{:S(2)}, u32[]{:S(2)}) async-start(f32[32,8,128]{2,1,0:T(8,128)} %bitcast.11), calls=%async_computation.4 | async-start | bytes 262144 | tf_op jit(solution)/shard_map/all_to_all | solution.py:22
  111.2 7.7 %all-to-all-done.4 = f32[32,8,128]{2,1,0:T(8,128)S(1)} async-done(((f32[32,8,128]{2,1,0:T(8,128)}), f32[32,8,128]{2,1,0:T(8,128)S(1)}, u32[]{:S(2)}, u32[]{:S(2)}) %all-to-all-start.4) | async-done | bytes 131104 | tf_op jit(solution)/shard_map/all_to_all | solution.py:22
  118.9 0.7 place_flux.1
  (25 shorter events, 2.0 us)
Async XLA Ops:
  2.1 10.6 %copy-start.3 = (bf16[128,1024]{1,0:T(8,128)(2,1)S(1)}, bf16[128,1024]{1,0:T(8,128)(2,1)}, u32[]{:S(2)}) copy-start(bf16[128,1024]{1,0:T(8,128)(2,1)} %param.9) | copy-start | bytes 786436
  2.1 21.7 %all-to-all-start = ((bf16[32,64,128]{2,1,0:T(8,128)(2,1)}), bf16[32,64,128]{2,1,0:T(8,128)(2,1)S(1)}, u32[]{:S(2)}, u32[]{:S(2)}) async-start(bf16[32,64,128]{2,1,0:T(8,128)(2,1)} %bitcast.4), calls=%async_computation | async-start | bytes 1048576 | tf_op jit(solution)/shard_map/all_to_all | solution.py:22
  12.7 25.0 %collective-permute-start = (bf16[128,1024]{1,0:T(8,128)(2,1)S(1)}, bf16[128,1024]{1,0:T(8,128)(2,1)S(1)}, u32[]{:S(2)}, u32[]{:S(2)}) collective-permute-start(bf16[128,1024]{1,0:T(8,128)(2,1)S(1)} %copy-done.3), channel_id=1, source_target_pairs={{128,0},{256,128},{384,256},{0,384},{129,1},{257,129},{385,257},{1... | collective-permute-start | bytes 786440 | tf_op jit(solution)/shard_map/ppermute | solution.py:157
  24.7 35.8 %all-to-all-start.1 = ((bf16[16,128,128]{2,1,0:T(8,128)(2,1)}), bf16[16,128,128]{2,1,0:T(8,128)(2,1)S(1)}, u32[]{:S(2)}, u32[]{:S(2)}) async-start(bf16[16,128,128]{2,1,0:T(8,128)(2,1)} %bitcast.7), calls=%async_computation.1 | async-start | bytes 1048576 | tf_op jit(solution)/shard_map/all_to_all | solution.py:22
  37.6 8.4 %collective-permute-start.1 = (bf16[128,1024]{1,0:T(8,128)(2,1)S(1)}, bf16[128,1024]{1,0:T(8,128)(2,1)S(1)}, u32[]{:S(2)}, u32[]{:S(2)}) collective-permute-start(bf16[128,1024]{1,0:T(8,128)(2,1)S(1)} %collective-permute-done), channel_id=1, source_target_pairs={{128,0},{256,128},{384,256},{0,384},{129,1},{257,129},{385,257},{1... | collective-permute-start | bytes 786440 | tf_op jit(solution)/shard_map/ppermute | solution.py:159
  40.8 10.0 %collective-permute-start.2 = (bf16[128,1024]{1,0:T(8,128)(2,1)S(1)}, bf16[128,1024]{1,0:T(8,128)(2,1)S(1)}, u32[]{:S(2)}, u32[]{:S(2)}) collective-permute-start(bf16[128,1024]{1,0:T(8,128)(2,1)S(1)} %copy-done.3), channel_id=1, source_target_pairs={{0,128},{128,256},{256,384},{384,0},{1,129},{129,257},{257,385},{3... | collective-permute-start | bytes 786440 | tf_op jit(solution)/shard_map/ppermute | solution.py:158
  46.1 10.6 %copy-start.4 = (bf16[1024,128]{1,0:T(8,128)(2,1)S(1)}, bf16[1024,128]{1,0:T(8,128)(2,1)}, u32[]{:S(2)}) copy-start(bf16[1024,128]{1,0:T(8,128)(2,1)} %param.10) | copy-start | bytes 786436
  50.8 7.4 %collective-permute-start.3 = (bf16[512,1024]{1,0:T(8,128)(2,1)S(1)}, bf16[512,1024]{1,0:T(8,128)(2,1)}, u32[]{:S(2)}, u32[]{:S(2)}) collective-permute-start(bf16[512,1024]{1,0:T(8,128)(2,1)S(1)} %constant_dynamic-update-slice_fusion), channel_id=1, source_target_pairs={{0,64},{64,0},{1,65},{65,1},{2,66},{66,2},{3,67},{67,3},{4,68},{68... | collective-permute-start | bytes 3145736 | tf_op jit(solution)/shard_map/ppermute | solution.py:161
  54.6 0.7 copy-start.6
  56.7 1.0 copy-start.5
  59.9 26.5 %copy-start = (bf16[1024,512]{1,0:T(8,128)(2,1)S(1)}, bf16[1024,512]{1,0:T(8,128)(2,1)}, u32[]{:S(2)}) copy-start(bf16[1024,512]{1,0:T(8,128)(2,1)} %up_ref.1) | copy-start | bytes 3145732
  66.8 19.6 %copy-start.1 = (f32[1024]{0:T(1024)S(1)}, f32[1024]{0:T(1024)}, u32[]{:S(2)}) copy-start(f32[1024]{0:T(1024)} %param.15) | copy-start | bytes 12292
  66.8 19.6 %copy-start.2 = (bf16[4,512]{1,0:T(4,128)(2,1)S(1)}, bf16[4,512]{1,0:T(4,128)(2,1)}, u32[]{:S(2)}) copy-start(bf16[4,512]{1,0:T(4,128)(2,1)} %flux_ref.1) | copy-start | bytes 12292
  105.3 13.6 %all-to-all-start.4 = ((f32[32,8,128]{2,1,0:T(8,128)}), f32[32,8,128]{2,1,0:T(8,128)S(1)}, u32[]{:S(2)}, u32[]{:S(2)}) async-start(f32[32,8,128]{2,1,0:T(8,128)} %bitcast.11), calls=%async_computation.4 | async-start | bytes 262144 | tf_op jit(solution)/shard_map/all_to_all | solution.py:22

commit v4 on v3

v4 whole, which is shorter than its diff:
```python
import functools
import math

import jax
import jax.numpy as jnp
from jax import lax
from jax.experimental import pallas as pl
from jax.experimental.pallas import tpu as pltpu
from jax.sharding import Mesh
from jax.sharding import PartitionSpec as P

BLK = 128
LMAX = 4
HD = 64
SLAB = 32
LANES = 128
GRP = ("x", "core")
PLANE = ("x", "core", "y")


def exchange(array, axes):
    return lax.all_to_all(array, axes, split_axis=0, concat_axis=0, tiled=True)


def on_chip(*arrays):
    return [pltpu.with_memory_space_constraint(array, pltpu.VMEM) for array in arrays]


def specs(scalars, arrays):
    return [pl.BlockSpec(memory_space=pltpu.SMEM)] * scalars + [
        pl.BlockSpec(memory_space=pltpu.VMEM)
    ] * arrays


def project_kernel(place_ref, own_ref, up_ref, down_ref, two_ref, last_ref, across_ref, kv_ref,
                   anchors_ref, weights_ref):
    depth, width = weights_ref.shape[0], own_ref.shape[1]
    parts = depth // width
    rows = parts * BLK
    n_x = weights_ref.shape[1] // width
    pieces = [own_ref, up_ref, two_ref, down_ref]
    for far, ref in enumerate(pieces):
        for part in range(parts):
            lanes = slice(part * width, (part + 1) * width)
            anchors_ref[far * BLK : (far + 1) * BLK, lanes] = ref[part * BLK : (part + 1) * BLK, :]
            start = far * rows + part * BLK
            anchors_ref[(n_x + far) * BLK : (n_x + far + 1) * BLK, lanes] = across_ref[
                start : start + BLK, :
            ]
    for far, ref in enumerate(pieces):
        at = (place_ref[0] + far) % n_x
        lanes = pl.ds(pl.multiple_of(at * width, width), width)
        if ref is two_ref:
            held = ref.shape[0] - rows
            weights_ref[:held, lanes] = ref[rows:, :]
            weights_ref[held:, lanes] = last_ref[...]
        else:
            weights_ref[:, lanes] = ref[rows:, :]
    step = 2 * BLK
    for start in range(0, kv_ref.shape[0], step):
        kv_ref[start : start + step, :] = jnp.dot(
            anchors_ref[start : start + step, :],
            weights_ref[...],
            preferred_element_type=jnp.float32,
        ).astype(jnp.bfloat16)


def project(place, own, up, down, two, last, across, depth, n_x):
    width = own.shape[1]
    return pl.pallas_call(
        project_kernel,
        out_shape=pltpu.VMEM((2 * n_x * BLK, n_x * width), jnp.bfloat16),
        in_specs=specs(1, 6),
        scratch_shapes=[
            pltpu.VMEM((2 * n_x * BLK, depth), jnp.bfloat16),
            pltpu.VMEM((depth, n_x * width), jnp.bfloat16),
        ],
        name="project",
    )(place, own, up, down, two, last, across)


def attend_step(step, per, place_ref, cells_ref, counts_ref, query_ref, kv_ref, keep_ref, send_ref):
    rows, width = query_ref.shape[1:]
    half = rows // 2
    cells = kv_ref.shape[0] // BLK
    quad = 2 * LANES
    heads = quad // HD
    head_of = lax.broadcasted_iota(jnp.int32, (rows, quad), 1) // HD
    for item in range(per):
        block = step * per + item
        picked = []
        for slot in range(LMAX):
            cell = jnp.clip(cells_ref[block * LMAX + slot], 0, cells - 1)
            far = (cell // 2 - place_ref[0] + cells) % (cells // 2)
            row = far + (cells // 2) * ((cell + place_ref[1]) % 2)
            picked.append(pl.multiple_of(row * BLK, BLK))
        slot_of = lax.broadcasted_iota(jnp.int32, (1, LMAX * BLK), 1) // BLK
        bias = jnp.where(slot_of < counts_ref[block], 0.0, -jnp.inf)

        def gathered(first, start):
            lanes = [slice(first + far * quad + start, first + far * quad + start + LANES)
                     for far in range(2)]
            return jnp.concatenate(
                [
                    jnp.concatenate([kv_ref[pl.ds(row, BLK), part] for part in lanes], axis=1)
                    for row in picked
                ],
                axis=0,
            )

        for lane in range(0, width, quad):
            query = query_ref[block, :, lane : lane + quad].astype(jnp.float32)
            scaled = query * (1.0 / math.sqrt(HD))
            each = jnp.concatenate(
                [jnp.where(head_of == head, scaled, 0.0) for head in range(heads)], axis=0
            ).astype(jnp.bfloat16)
            scores = lax.dot_general(
                each,
                gathered(2 * lane, 0),
                (((1,), (1,)), ((), ())),
                preferred_element_type=jnp.float32,
            )
            scores = scores + bias
            top = jnp.max(scores, axis=-1, keepdims=True)
            expo = jnp.exp(scores - top)
            total = jnp.sum(expo, axis=-1, keepdims=True)
            summed = jnp.dot(
                expo.astype(jnp.bfloat16),
                gathered(2 * lane, LANES),
                preferred_element_type=jnp.float32,
            )
            summed = summed / total
            attended = summed[:rows]
            for head in range(1, heads):
                attended = jnp.where(
                    head_of == head, summed[head * rows : (head + 1) * rows], attended
                )
            attended = attended.astype(jnp.bfloat16).astype(jnp.float32)
            stream = (query + attended).astype(jnp.bfloat16)
            low, high = stream[:half], stream[half:]
            keep_ref[block, :, lane : lane + quad] = jnp.where(place_ref[1] == 0, low, high)
            send_ref[block, :, lane : lane + quad] = jnp.where(place_ref[1] == 0, high, low)


def attend_kernel(per, *refs):
    steps = refs[3].shape[0] // per
    lax.fori_loop(0, steps, lambda step, _: attend_step(step, per, *refs), None)


def attend(query, kv, place, cells, counts, per):
    blocks, rows, width = query.shape
    return pl.pallas_call(
        functools.partial(attend_kernel, per),
        out_shape=[pltpu.VMEM((blocks, rows // 2, width), jnp.bfloat16)] * 2,
        in_specs=specs(3, 2),
        name="attend",
    )(place, cells, counts, *on_chip(query, kv))


def flux_kernel(place_ref, mine_ref, other_ref, gain_ref, up_ref, flux_ref, out_ref):
    rows = mine_ref.shape[0]
    core = place_ref[1]
    n_x = gain_ref.shape[0] // 2
    mine = mine_ref[...].astype(jnp.float32)
    other = other_ref[...].astype(jnp.float32)
    squares = jnp.sum(mine * mine, axis=-1, keepdims=True) + jnp.sum(
        other * other, axis=-1, keepdims=True
    )
    scale = lax.rsqrt(squares / (mine.shape[1] + other.shape[1]) + 1e-06)
    hidden = jnp.zeros((rows, up_ref.shape[2]), jnp.float32)
    for stream, at in ((mine, core), (other, 1 - core)):
        gain = jnp.concatenate([gain_ref[2 * x + at] for x in range(n_x)], axis=1)
        weights = jnp.concatenate([up_ref[2 * x + at] for x in range(n_x)], axis=0)
        normed = (stream * scale * gain).astype(jnp.bfloat16)
        hidden = hidden + jnp.dot(normed, weights, preferred_element_type=jnp.float32)
    hidden = jax.nn.gelu(hidden).astype(jnp.bfloat16)
    flux = lax.dot_general(
        flux_ref[...], hidden, (((1,), (1,)), ((), ())), preferred_element_type=jnp.float32
    )
    blocks = out_ref.shape[0]
    few = rows // blocks
    for block in range(blocks):
        piece = flux[:, block * few : (block + 1) * few]
        out_ref[block] = jnp.concatenate([piece] * (LANES // few), axis=1)


def wall_flux(place, mine, other, norm_gain, up_weight, flux_weight, blocks):
    groups = norm_gain.shape[0] // LANES
    return pl.pallas_call(
        flux_kernel,
        out_shape=pltpu.VMEM((blocks, flux_weight.shape[0], LANES), jnp.float32),
        in_specs=specs(1, 5),
        name="wall_flux",
    )(
        place,
        *on_chip(
            mine,
            other,
            norm_gain.reshape(groups, 1, LANES),
            up_weight.reshape(groups, LANES, -1),
            flux_weight,
        ),
    )


def place_kernel(y_ref, flux_ref, out_ref):
    n_x, halves, n_y, both, _ = flux_ref.shape
    comps = out_ref.shape[0]
    few = SLAB // n_x
    core = y_ref[0] // (n_y // halves)
    even = y_ref[0] % (n_y // halves) == 0
    pieces = []
    for top in range(both // comps):
        for low in range(n_y):
            for x in range(n_x):
                piece = flux_ref[x, core, low, top * comps : (top + 1) * comps]
                pieces.append(jnp.where(even, piece[:, :few], piece[:, few : 2 * few]))
    out_ref[...] = jnp.concatenate(pieces, axis=1)


def place_flux(flux, comps, rows, y):
    return pl.pallas_call(
        place_kernel,
        out_shape=jax.ShapeDtypeStruct((comps, rows), jnp.float32),
        in_specs=specs(1, 1),
        name="place_flux",
    )(y, *on_chip(flux))


def body(
    sizes,
    anchor_states,
    key_weight,
    value_weight,
    panel_query,
    cell_list,
    cell_count,
    norm_gain,
    up_weight,
    flux_weight,
):
    n_x, n_z, n_y = sizes
    grp = 2 * n_x
    depth, width = key_weight.shape
    few = SLAB // n_x
    half = n_x * width
    hi = n_z // grp
    query = panel_query.reshape(hi, n_y, n_x, few, n_x, 2, width).transpose(2, 5, 1, 0, 3, 4, 6)
    query = exchange(query.reshape(grp * n_y, hi * few, half), PLANE)
    query = query.reshape(grp, n_y, hi, few, half).transpose(0, 2, 1, 3, 4)
    query = exchange(query.reshape(n_z, n_y * few, half), "z")
    weights = jnp.concatenate([key_weight, value_weight], axis=1)
    cut = depth // (2 * width)
    anchors = anchor_states.reshape(BLK, cut, 2 * width).transpose(1, 0, 2)
    rows = cut * BLK
    own = jnp.concatenate([anchors.reshape(rows, 2 * width), weights], axis=0)
    up = [((i + 1) % n_x, i) for i in range(n_x)]
    down = [(i, (i + 1) % n_x) for i in range(n_x)]
    one_up = lax.ppermute(own, "x", up)
    one_down = lax.ppermute(own, "x", down)
    middle = own.shape[0] // 2
    two = lax.ppermute(one_up[:middle], "x", up)
    last = lax.ppermute(one_down[middle:], "x", down)
    two, last = lax.optimization_barrier((two, last))
    along = jnp.concatenate([own[:rows], one_up[:rows], two[:rows], one_down[:rows]], axis=0)
    across = lax.ppermute(along, "core", [(0, 1), (1, 0)])
    place = jnp.stack([lax.axis_index("x"), lax.axis_index("core")]).astype(jnp.int32)
    kv = project(place, own, one_up, one_down, two, last, across, depth, n_x)
    keep, send = attend(query, kv, place, cell_list.reshape(-1), cell_count, 2)
    other = lax.ppermute(send, "core", [(0, 1), (1, 0)])
    flux = wall_flux(
        place,
        keep.reshape(-1, half),
        other.reshape(-1, half),
        norm_gain,
        up_weight,
        flux_weight,
        n_z,
    )
    comps = flux_weight.shape[0]
    flux = exchange(flux, "z").reshape(grp, 1, hi * comps, LANES)
    flux = jnp.broadcast_to(flux, (grp, n_y, hi * comps, LANES))
    flux = exchange(flux.reshape(grp * n_y, hi * comps, LANES), PLANE)
    return place_flux(
        flux.reshape(n_x, 2, n_y, hi * comps, LANES),
        comps,
        panel_query.shape[0],
        lax.axis_index("y").reshape(1),
    )


def solution(mesh):
    grp, wide = mesh.devices.shape
    sizes = (grp // 2, 16, wide // 16)
    fine = Mesh(mesh.devices.reshape(grp // 2, 2, 16, wide // 16), ("x", "core", "z", "y"))
    rows = ("z", "y", "x", "core")
    in_specs = (
        P(rows, None),
        P(None, GRP),
        P(None, GRP),
        P(rows, None),
        P(("z", "y"), None),
        P(("z", "y")),
        P(),
        P(),
        P(),
    )
    return jax.shard_map(
        functools.partial(body, sizes),
        mesh=fine,
        in_specs=in_specs,
        out_specs=P(None, rows),
        check_vma=False,
    )
```

time: 120 us -> 137 us (1.14)
  blocking collectives: 36.9 us -> 48.8 us
  Pallas kernels: 7.85 us -> 19.5 us
  waiting for transfers between devices: 22.4 us -> 19.5 us
  starting transfers between devices: 43.2 us -> 41.1 us
  matrix products: 2.1 us -> 0 us
  other arithmetic: 0.7 us -> 2.76 us
  local copies, waits for them, and re-layouts: 6.15 us -> 4.78 us
    all_to_all x2, blocking collectives: 36.9 us -> 48.8 us  [exchange(): return lax.all_to_all(array, axes, split_axis=0, concat_axis=0, tiled=True)]
    pallas_call x1 -> x2, Pallas kernels: 6.32 us -> 17.3 us  [the longest x1 12.5 us: attend(): pl.pallas_call(functools.partial(attend_kernel, per), out_shape=[pltpu.VM...]
    all_to_all x3 -> x2, starting transfers between devices: 29.5 us -> 20.2 us  [exchange(): return lax.all_to_all(array, axes, split_axis=0, concat_axis=0, tiled=True)]
    ppermute x3 -> x5, starting transfers between devices: 9.93 us -> 17.1 us  [the longest x1 5.22 us: body(): one_up = lax.ppermute(own, 'x', up)]
    all_to_all x3 -> x2, waiting for transfers between devices: 14.7 us -> 7.67 us  [exchange(): return lax.all_to_all(array, axes, split_axis=0, concat_axis=0, tiled=True)]
    ppermute x3 -> x5, waiting for transfers between devices: 7.74 us -> 10.6 us  [the longest x1 6.24 us: body(): two = lax.ppermute(one_up[:middle], 'x', up)]
    concatenate x1 -> x2, other arithmetic: 0.04 us -> 2.16 us  [the longest x1 1.11 us: body(): own = jnp.concatenate([anchors.reshape(rows, 2 * width), weights], axis=0)]
    dot_general x2 -> x0, matrix products: 2.1 us -> none  [body(): jnp.dot(part, weights, preferred_element_type=jnp.float32)]
  transfers between devices with their start and end apart: 7 -> 8, of which waited for: 5 -> 5; matrix products, arithmetic and copies ran while one was open for 4% -> 3% of each run, Pallas kernels for 0% -> 4%
where the time goes in v4:
time: 137 us
  blocking collectives  48.8 us (36%)
  starting transfers between devices  41.1 us (30%)
  waiting for transfers between devices  19.5 us (14%)
  Pallas kernels  19.5 us (14%)
  local copies, waits for them, and re-layouts  4.78 us (3%)
  other arithmetic  2.76 us (2%)
    all_to_all x2, blocking collectives, exchange(): return lax.all_to_all(array, axes, split_axis=0, concat_axis=0, tiled=True)  48.8 us
    all_to_all x2, starting transfers between devices, exchange(): return lax.all_to_all(array, axes, split_axis=0, concat_axis=0, tiled=True)  20.2 us
    pallas_call x1, Pallas kernels, attend(): pl.pallas_call(functools.partial(attend_kernel, per), out_shape=[pltpu.VM...  12.5 us
    all_to_all x2, waiting for transfers between devices, exchange(): return lax.all_to_all(array, axes, split_axis=0, concat_axis=0, tiled=True)  7.67 us
    ppermute x1, waiting for transfers between devices, body(): two = lax.ppermute(one_up[:middle], 'x', up)  6.24 us
    ppermute x1, starting transfers between devices, body(): one_up = lax.ppermute(own, 'x', up)  5.22 us
    pallas_call x1, Pallas kernels, project(): pl.pallas_call(project_kernel, out_shape=pltpu.VMEM((2 * n_x * BLK, n_x *...  4.81 us
    ppermute x1, starting transfers between devices, body(): other = lax.ppermute(send, 'core', [(0, 1), (1, 0)])  4.58 us
  transfers between devices with their start and end apart: 8, of which 5 were waited for; matrix products, arithmetic and copies ran while one was open for 3% of the time, Pallas kernels for 4%

profile of v4, /device:TPU:1, one launch (start us, length us, event | category | flops | bytes accessed | tf_op | source)
XLA Modules:
  0.0 136.7 jit_solution(16580372272667617594)
XLA Ops:
  0.0 1.0 copy.21
  1.0 1.1 maximum_maximum_fusion.own_ref
  2.2 5.2 %collective-permute-start = (bf16[1536,256]{1,0:T(8,128)(2,1)S(1)}, bf16[1536,256]{1,0:T(8,128)(2,1)S(1)}, u32[]{:S(2)}, u32[]{:S(2)}) collective-permute-start(bf16[1536,256]{1,0:T(8,128)(2,1)S(1)} %maximum_maximum_fusion.own_ref), channel_id=1, source_target_pairs={{128,0},{256,128},{384,256},{0,384},{129,1},{257,129},{385,257},{1... | collective-permute-start | bytes 2359304 | tf_op jit(solution)/shard_map/ppermute | solution.py:259
  7.4 1.9 %collective-permute-start.1 = (bf16[1536,256]{1,0:T(8,128)(2,1)S(1)}, bf16[1536,256]{1,0:T(8,128)(2,1)S(1)}, u32[]{:S(2)}, u32[]{:S(2)}) collective-permute-start(bf16[1536,256]{1,0:T(8,128)(2,1)S(1)} %maximum_maximum_fusion.own_ref), channel_id=1, source_target_pairs={{0,128},{128,256},{256,384},{384,0},{1,129},{129,257},{257,385},{3... | collective-permute-start | bytes 2359304 | tf_op jit(solution)/shard_map/ppermute | solution.py:260
  9.5 28.4 %all_to_all.20 = bf16[32,16,512]{2,1,0:T(8,128)(2,1)S(1)} all-to-all(bf16[32,16,512]{2,1,0:T(8,128)(2,1)S(1)} %bitcast.34), channel_id=1, replica_groups=mesh['x'=4,'core'=2,'z'=16,'y'=4] {'x','core','y'}, dimensions={0} | all-to-all | bytes 1048576 | tf_op jit(solution)/shard_map/all_to_all | solution.py:22
  37.8 0.9 copy.17
  38.7 14.9 %all-to-all-start.1 = ((bf16[16,32,512]{2,1,0:T(8,128)(2,1)}), bf16[16,32,512]{2,1,0:T(8,128)(2,1)S(1)}, u32[]{:S(2)}, u32[]{:S(2)}) async-start(bf16[16,32,512]{2,1,0:T(8,128)(2,1)} %bitcast.32), calls=%async_computation.1 | async-start | bytes 1048576 | tf_op jit(solution)/shard_map/all_to_all | solution.py:22
  53.7 2.1 %collective-permute-start.2 = (bf16[768,256]{1,0:T(8,128)(2,1)S(1)}, bf16[768,256]{1,0:T(8,128)(2,1)S(1)}, u32[]{:S(2)}, u32[]{:S(2)}) collective-permute-start(bf16[768,256]{1,0:T(8,128)(2,1)S(1)} %slice.20), channel_id=1, source_target_pairs={{128,0},{256,128},{384,256},{0,384},{129,1},{257,129},{385,257},{1... | collective-permute-start | bytes 1179656 | tf_op jit(solution)/shard_map/ppermute | solution.py:262
  55.8 3.4 %collective-permute-start.3 = (bf16[768,256]{1,0:T(8,128)(2,1)S(1)}, bf16[768,256]{1,0:T(8,128)(2,1)}, u32[]{:S(2)}, u32[]{:S(2)}) collective-permute-start(bf16[768,256]{1,0:T(8,128)(2,1)S(1)} %slice.21), channel_id=1, source_target_pairs={{0,128},{128,256},{256,384},{384,0},{1,129},{129,257},{257,385},{3... | collective-permute-start | bytes 1179656 | tf_op jit(solution)/shard_map/ppermute | solution.py:263
  59.2 6.2 %collective-permute-done.2.two_ref = bf16[768,256]{1,0:T(8,128)(2,1)S(1)} collective-permute-done((bf16[768,256]{1,0:T(8,128)(2,1)S(1)}, bf16[768,256]{1,0:T(8,128)(2,1)S(1)}, u32[]{:S(2)}, u32[]{:S(2)}) %collective-permute-start.2) | collective-permute-done | bytes 393248 | tf_op jit(solution)/shard_map/ppermute | solution.py:262
  65.5 3.2 %collective-permute-done.3.last_ref = bf16[768,256]{1,0:T(8,128)(2,1)} collective-permute-done((bf16[768,256]{1,0:T(8,128)(2,1)S(1)}, bf16[768,256]{1,0:T(8,128)(2,1)}, u32[]{:S(2)}, u32[]{:S(2)}) %collective-permute-start.3) | collective-permute-done | bytes 393248 | tf_op jit(solution)/shard_map/ppermute | solution.py:263
  68.7 1.1 pad_maximum_fusion
  69.7 3.8 %collective-permute-start.4 = (bf16[2048,256]{1,0:T(8,128)(2,1)}, bf16[2048,256]{1,0:T(8,128)(2,1)}, u32[]{:S(2)}, u32[]{:S(2)}) collective-permute-start(bf16[2048,256]{1,0:T(8,128)(2,1)} %pad_maximum_fusion), channel_id=1, source_target_pairs={{0,64},{64,0},{1,65},{65,1},{2,66},{66,2},{3,67},{67,3},{4,68},{68... | collective-permute-start | bytes 3145736 | tf_op jit(solution)/shard_map/ppermute | solution.py:266
  74.9 1.3 collective-permute-done.4.across_ref
  76.1 4.8 %project.1.refs_4_ = bf16[1024,1024]{1,0:T(8,128)(2,1)S(1)} custom-call(s32[2]{0:T(128)} %pad_add_fusion.place_ref.refs_0_, bf16[1536,256]{1,0:T(8,128)(2,1)} %copy-done.3, bf16[1536,256]{1,0:T(8,128)(2,1)} %copy-done.4, bf16[1536,256]{1,0:T(8,128)(2,1)} %copy-done.5, bf16[768,256]{1,0:T(8,128)(2,1)} %copy-done.6, ...), custom_call_target="tpu_custom_call" | custom-call | tf_op jit(solution)/shard_map/project/pallas_call | solution.py:70
  81.0 12.5 %attend.1 = (bf16[16,16,512]{2,1,0:T(8,128)(2,1)S(1)}, bf16[16,16,512]{2,1,0:T(8,128)(2,1)S(1)}) custom-call(s32[2]{0:T(128)} %pad_add_fusion.place_ref.refs_0_, s32[64]{0:T(128)} %reshape.45.refs_1_, s32[16]{0:T(128)} %refs_2_.1, bf16[16,32,512]{2,1,0:T(8,128)(2,1)S(1)} %all-to-all-done.1.refs_3_, bf16[1024,1024]{1,0:T(8,128)(2,1)S(1)} %project.1.refs_4_), custom_call_target="tpu_custom_call" | custom-call | tf_op jit(solution)/shard_map/attend/pallas_call | solution.py:152
  93.5 4.6 %collective-permute-start.5 = (bf16[16,16,512]{2,1,0:T(8,128)(2,1)S(1)}, bf16[16,16,512]{2,1,0:T(8,128)(2,1)S(1)}, u32[]{:S(2)}, u32[]{:S(2)}) collective-permute-start(bf16[16,16,512]{2,1,0:T(8,128)(2,1)S(1)} %get-tuple-element.12), channel_id=1, source_target_pairs={{0,64},{64,0},{1,65},{65,1},{2,66},{66,2},{3,67},{67,3},{4,68},{68... | collective-permute-start | bytes 786440 | tf_op jit(solution)/shard_map/ppermute | solution.py:270
  98.1 1.1 collective-permute-done.5
  99.2 1.2 copy-done
  100.4 1.5 %wall_flux.1 = f32[16,4,128]{2,1,0:T(4,128)S(1)} custom-call(s32[2]{0:T(128)} %pad_add_fusion.place_ref.refs_0_, bf16[256,512]{1,0:T(8,128)(2,1)S(1)} %bitcast.27, bf16[256,512]{1,0:T(8,128)(2,1)S(1)} %bitcast.28, f32[8,1,128]{2,1,0:T(1,128)S(1)} %bitcast.29, bf16[8,128,512]{2,1,0:T(8,128)(2,1)S(1)} %bitcast.25, bf16[4,512]{1,0:T(4,128)(2,1)S(1)} %copy-done.2), custom_call_target="tpu_custom_call" | custom-call | tf_op jit(solution)/shard_map/wall_flux/pallas_call | solution.py:189
  101.9 20.4 %all_to_all.21 = f32[16,4,128]{2,1,0:T(4,128)S(1)} all-to-all(f32[16,4,128]{2,1,0:T(4,128)S(1)} %wall_flux.1), channel_id=1, replica_groups=mesh['x'=4,'core'=2,'z'=16,'y'=4] {'z'}, dimensions={0} | all-to-all | bytes 65536 | tf_op jit(solution)/shard_map/all_to_all | solution.py:22
  123.0 5.3 %all-to-all-start.3 = ((f32[32,8,128]{2,1,0:T(8,128)}), f32[32,8,128]{2,1,0:T(8,128)S(1)}, u32[]{:S(2)}, u32[]{:S(2)}) async-start(f32[32,8,128]{2,1,0:T(8,128)} %bitcast.17), calls=%async_computation.3 | async-start | bytes 262144 | tf_op jit(solution)/shard_map/all_to_all | solution.py:22
  128.3 7.7 %all-to-all-done.3 = f32[32,8,128]{2,1,0:T(8,128)S(1)} async-done(((f32[32,8,128]{2,1,0:T(8,128)}), f32[32,8,128]{2,1,0:T(8,128)S(1)}, u32[]{:S(2)}, u32[]{:S(2)}) %all-to-all-start.3) | async-done | bytes 131104 | tf_op jit(solution)/shard_map/all_to_all | solution.py:22
  136.0 0.8 place_flux.1
  (30 shorter events, 2.3 us)
Async XLA Ops:
  0.0 9.3 %copy-start.7 = (bf16[256,1024]{1,0:T(8,128)(2,1)S(1)}, bf16[256,1024]{1,0:T(8,128)(2,1)}, u32[]{:S(2)}) copy-start(bf16[256,1024]{1,0:T(8,128)(2,1)} %param.12) | copy-start | bytes 1572868
  2.1 36.5 %copy-start.3 = (bf16[1536,256]{1,0:T(8,128)(2,1)}, bf16[1536,256]{1,0:T(8,128)(2,1)S(1)}, u32[]{:S(2)}) copy-start(bf16[1536,256]{1,0:T(8,128)(2,1)S(1)} %maximum_maximum_fusion.own_ref) | copy-start | bytes 2359300
  2.2 51.5 %collective-permute-start = (bf16[1536,256]{1,0:T(8,128)(2,1)S(1)}, bf16[1536,256]{1,0:T(8,128)(2,1)S(1)}, u32[]{:S(2)}, u32[]{:S(2)}) collective-permute-start(bf16[1536,256]{1,0:T(8,128)(2,1)S(1)} %maximum_maximum_fusion.own_ref), channel_id=1, source_target_pairs={{128,0},{256,128},{384,256},{0,384},{129,1},{257,129},{385,257},{1... | collective-permute-start | bytes 2359304 | tf_op jit(solution)/shard_map/ppermute | solution.py:259
  7.4 48.4 %collective-permute-start.1 = (bf16[1536,256]{1,0:T(8,128)(2,1)S(1)}, bf16[1536,256]{1,0:T(8,128)(2,1)S(1)}, u32[]{:S(2)}, u32[]{:S(2)}) collective-permute-start(bf16[1536,256]{1,0:T(8,128)(2,1)S(1)} %maximum_maximum_fusion.own_ref), channel_id=1, source_target_pairs={{0,128},{128,256},{256,384},{384,0},{1,129},{129,257},{257,385},{3... | collective-permute-start | bytes 2359304 | tf_op jit(solution)/shard_map/ppermute | solution.py:260
  38.7 42.3 %all-to-all-start.1 = ((bf16[16,32,512]{2,1,0:T(8,128)(2,1)}), bf16[16,32,512]{2,1,0:T(8,128)(2,1)S(1)}, u32[]{:S(2)}, u32[]{:S(2)}) async-start(bf16[16,32,512]{2,1,0:T(8,128)(2,1)} %bitcast.32), calls=%async_computation.1 | async-start | bytes 1048576 | tf_op jit(solution)/shard_map/all_to_all | solution.py:22
  53.6 16.1 %copy-start.4 = (bf16[1536,256]{1,0:T(8,128)(2,1)}, bf16[1536,256]{1,0:T(8,128)(2,1)S(1)}, u32[]{:S(2)}) copy-start(bf16[1536,256]{1,0:T(8,128)(2,1)S(1)} %collective-permute-done.up_ref) | copy-start | bytes 2359300
  53.7 19.9 %copy-start.8 = (s32[16,4]{0,1:T(4,128)S(1)}, s32[16,4]{0,1:T(4,128)}, u32[]{:S(2)}) copy-start(s32[16,4]{0,1:T(4,128)} %param.13) | copy-start | bytes 772
  53.7 11.8 %collective-permute-start.2 = (bf16[768,256]{1,0:T(8,128)(2,1)S(1)}, bf16[768,256]{1,0:T(8,128)(2,1)S(1)}, u32[]{:S(2)}, u32[]{:S(2)}) collective-permute-start(bf16[768,256]{1,0:T(8,128)(2,1)S(1)} %slice.20), channel_id=1, source_target_pairs={{128,0},{256,128},{384,256},{0,384},{129,1},{257,129},{385,257},{1... | collective-permute-start | bytes 1179656 | tf_op jit(solution)/shard_map/ppermute | solution.py:262
  55.8 14.0 %copy-start.5 = (bf16[1536,256]{1,0:T(8,128)(2,1)}, bf16[1536,256]{1,0:T(8,128)(2,1)S(1)}, u32[]{:S(2)}) copy-start(bf16[1536,256]{1,0:T(8,128)(2,1)S(1)} %collective-permute-done.1.down_ref) | copy-start | bytes 2359300
  55.8 12.9 %collective-permute-start.3 = (bf16[768,256]{1,0:T(8,128)(2,1)S(1)}, bf16[768,256]{1,0:T(8,128)(2,1)}, u32[]{:S(2)}, u32[]{:S(2)}) collective-permute-start(bf16[768,256]{1,0:T(8,128)(2,1)S(1)} %slice.21), channel_id=1, source_target_pairs={{0,128},{128,256},{256,384},{384,0},{1,129},{129,257},{257,385},{3... | collective-permute-start | bytes 1179656 | tf_op jit(solution)/shard_map/ppermute | solution.py:263
  65.5 10.7 %copy-start.6 = (bf16[768,256]{1,0:T(8,128)(2,1)}, bf16[768,256]{1,0:T(8,128)(2,1)S(1)}, u32[]{:S(2)}) copy-start(bf16[768,256]{1,0:T(8,128)(2,1)S(1)} %collective-permute-done.2.two_ref) | copy-start | bytes 1179652
  69.7 6.4 %collective-permute-start.4 = (bf16[2048,256]{1,0:T(8,128)(2,1)}, bf16[2048,256]{1,0:T(8,128)(2,1)}, u32[]{:S(2)}, u32[]{:S(2)}) collective-permute-start(bf16[2048,256]{1,0:T(8,128)(2,1)} %pad_maximum_fusion), channel_id=1, source_target_pairs={{0,64},{64,0},{1,65},{65,1},{2,66},{66,2},{3,67},{67,3},{4,68},{68... | collective-permute-start | bytes 3145736 | tf_op jit(solution)/shard_map/ppermute | solution.py:266
  81.0 18.2 %copy-start.1 = (f32[1024]{0:T(1024)S(1)}, f32[1024]{0:T(1024)}, u32[]{:S(2)}) copy-start(f32[1024]{0:T(1024)} %param.15) | copy-start | bytes 12292
  81.0 18.2 %copy-start.2 = (bf16[4,512]{1,0:T(4,128)(2,1)S(1)}, bf16[4,512]{1,0:T(4,128)(2,1)}, u32[]{:S(2)}) copy-start(bf16[4,512]{1,0:T(4,128)(2,1)} %flux_ref.1) | copy-start | bytes 12292
  93.5 5.7 %collective-permute-start.5 = (bf16[16,16,512]{2,1,0:T(8,128)(2,1)S(1)}, bf16[16,16,512]{2,1,0:T(8,128)(2,1)S(1)}, u32[]{:S(2)}, u32[]{:S(2)}) collective-permute-start(bf16[16,16,512]{2,1,0:T(8,128)(2,1)S(1)} %get-tuple-element.12), channel_id=1, source_target_pairs={{0,64},{64,0},{1,65},{65,1},{2,66},{66,2},{3,67},{67,3},{4,68},{68... | collective-permute-start | bytes 786440 | tf_op jit(solution)/shard_map/ppermute | solution.py:270
  99.2 1.2 copy-start
  123.0 12.9 %all-to-all-start.3 = ((f32[32,8,128]{2,1,0:T(8,128)}), f32[32,8,128]{2,1,0:T(8,128)S(1)}, u32[]{:S(2)}, u32[]{:S(2)}) async-start(f32[32,8,128]{2,1,0:T(8,128)} %bitcast.17), calls=%async_computation.3 | async-start | bytes 262144 | tf_op jit(solution)/shard_map/all_to_all | solution.py:22

commit v5 on v3

--- a/solution.py
+++ b/solution.py
@@ -24,6 +24,29 @@
 
 def on_chip(*arrays):
     return [pltpu.with_memory_space_constraint(array, pltpu.VMEM) for array in arrays]
+
+
+def split_kernel(query_ref, out_ref):
+    chunks, rows, width = out_ref.shape
+    groups = query_ref.shape[1] // width
+    low = chunks // groups
+    for chunk in range(chunks):
+        lane = chunk // low * width
+        for top in range(rows // SLAB):
+            row = (top * low + chunk % low) * SLAB
+            out_ref[chunk, top * SLAB : (top + 1) * SLAB, :] = query_ref[
+                row : row + SLAB, lane : lane + width
+            ]
+
+
+def split_query(query, groups, low):
+    rows, width = query.shape
+    return pl.pallas_call(
+        split_kernel,
+        out_shape=pltpu.VMEM((groups * low, rows // low, width // groups), query.dtype),
+        in_specs=[pl.BlockSpec(memory_space=pltpu.VMEM)],
+        name="split_query",
+    )(query)
 
 
 def attend_step(step, per, place_ref, cells_ref, counts_ref, query_ref, kv_ref, out_ref):
@@ -105,11 +128,11 @@
     )(*on_chip(stream, norm_gain[None, :], up_weight, flux_weight))
 
 
-def place_kernel(y_ref, flux_ref, out_ref):
+def place_kernel(place_ref, flux_ref, out_ref):
     _, halves, n_y, both, _ = flux_ref.shape
     comps, rows = out_ref.shape
     few = rows * comps // (halves * n_y * both)
-    mine = flux_ref.at[y_ref[0]]
+    mine = flux_ref.at[place_ref[2]]
     pieces = [
         mine[half, low, top * comps : (top + 1) * comps, :few]
         for top in range(both // comps)
@@ -119,7 +142,7 @@
     out_ref[...] = jnp.concatenate(pieces, axis=1)
 
 
-def place_flux(flux, comps, rows, y):
+def place_flux(place, flux, comps, rows):
     return pl.pallas_call(
         place_kernel,
         out_shape=jax.ShapeDtypeStruct((comps, rows), jnp.float32),
@@ -128,7 +151,7 @@
             pl.BlockSpec(memory_space=pltpu.VMEM),
         ],
         name="place_flux",
-    )(y, *on_chip(flux))
+    )(place, *on_chip(flux))
 
 
 def body(
@@ -147,8 +170,7 @@
     grp = 2 * n_x
     width = key_weight.shape[1]
     hi = n_z // grp
-    query = panel_query.reshape(hi, n_y, SLAB, grp, width).transpose(3, 1, 0, 2, 4)
-    query = exchange(query.reshape(grp * n_y, hi * SLAB, width), PLANE)
+    query = exchange(split_query(panel_query, grp, n_y), PLANE)
     query = query.reshape(grp, n_y, hi, SLAB, width).transpose(0, 2, 1, 3, 4)
     query = query.reshape(n_z, n_y * SLAB, width)
     query = exchange(query, "z")
@@ -167,8 +189,8 @@
         ],
         axis=0,
     )
-    place = jnp.stack([lax.axis_index("x"), lax.axis_index("core")]).astype(jnp.int32)
-    stream = attend(query, kv, place, cell_list.reshape(-1), cell_count, grp, 4)
+    place = jnp.stack([lax.axis_index(axis) for axis in PLANE]).astype(jnp.int32)
+    stream = attend(query, kv, place, cell_list.reshape(-1), cell_count, grp, 16)
     stream = exchange(stream, GRP)
     flux = wall_flux(
         stream.reshape(grp, -1, width), norm_gain, up_weight, flux_weight, n_z
@@ -178,10 +200,7 @@
     flux = jnp.broadcast_to(flux, (grp, n_y, hi * comps, LANES))
     flux = exchange(flux.reshape(grp * n_y, hi * comps, LANES), PLANE)
     return place_flux(
-        flux.reshape(n_x, 2, n_y, hi * comps, LANES),
-        comps,
-        panel_query.shape[0],
-        lax.axis_index("y").reshape(1),
+        place, flux.reshape(n_x, 2, n_y, hi * comps, LANES), comps, panel_query.shape[0]
     )
 
 

time: 120 us -> 119 us (level)
  blocking collectives: 36.9 us -> 49.8 us
  waiting for transfers between devices: 22.4 us -> 14.9 us
  starting transfers between devices: 43.2 us -> 37.3 us
  local copies, waits for them, and re-layouts: 6.15 us -> 3.38 us
  Pallas kernels: 7.85 us -> 9.88 us
    all_to_all x2 -> x3, blocking collectives: 36.9 us -> 49.8 us  [exchange(): return lax.all_to_all(array, axes, split_axis=0, concat_axis=0, tiled=True)]
    all_to_all x3 -> x2, waiting for transfers between devices: 14.7 us -> 7.17 us  [exchange(): return lax.all_to_all(array, axes, split_axis=0, concat_axis=0, tiled=True)]
    all_to_all x3 -> x2, starting transfers between devices: 29.5 us -> 23.5 us  [exchange(): return lax.all_to_all(array, axes, split_axis=0, concat_axis=0, tiled=True)]
    pallas_call x0 -> x1, Pallas kernels: none -> 1.93 us  [split_query(): pl.pallas_call(split_kernel, out_shape=pltpu.VMEM((groups * low, rows //...]
    transpose x2 -> x0, local copies, waits for them, and re-layouts: 1.81 us -> none  [the longest x1 0.92 us: body(): panel_query.reshape(hi, n_y, SLAB, grp, width).transpose(3, 1, 0, 2, 4)]
    unnamed x20 -> x19, local copies, waits for them, and re-layouts: 2.92 us -> 1.79 us
  transfers between devices with their start and end apart: 7 -> 6, of which waited for: 5 -> 4; matrix products, arithmetic and copies ran while one was open for 4% -> 4% of each run, Pallas kernels for 0% -> 0%
where the time goes in v5:
time: 119 us; the launch traced here: 118 us
  blocking collectives  49.8 us (42%)
  starting transfers between devices  37.3 us (31%)
  waiting for transfers between devices  14.9 us (13%)
  Pallas kernels  9.88 us (8%)
  local copies, waits for them, and re-layouts  3.38 us (3%)
  matrix products  2.1 us (2%)
    all_to_all x3, blocking collectives, exchange(): return lax.all_to_all(array, axes, split_axis=0, concat_axis=0, tiled=True)  49.8 us
    all_to_all x2, starting transfers between devices, exchange(): return lax.all_to_all(array, axes, split_axis=0, concat_axis=0, tiled=True)  23.5 us
    all_to_all x2, waiting for transfers between devices, exchange(): return lax.all_to_all(array, axes, split_axis=0, concat_axis=0, tiled=True)  7.17 us
    pallas_call x1, Pallas kernels, attend(): pl.pallas_call(functools.partial(attend_kernel, per), out_shape=pltpu.VME...  5.77 us
    ppermute x1, waiting for transfers between devices, body(): one_down = lax.ppermute(anchor_states, 'x', down)  4.66 us
    ppermute x1, starting transfers between devices, body(): one_up = lax.ppermute(anchor_states, 'x', up)  4.65 us
    ppermute x1, starting transfers between devices, body(): across = lax.ppermute(along, 'core', [(0, 1), (1, 0)])  3.78 us
    ppermute x1, starting transfers between devices, body(): two_up = lax.ppermute(one_up, 'x', up)  3.16 us
  transfers between devices with their start and end apart: 6, of which 4 were waited for; matrix products, arithmetic and copies ran while one was open for 4% of the time, Pallas kernels for 0%

profile of v5, /device:TPU:1, one launch (start us, length us, event | category | flops | bytes accessed | tf_op | source)
XLA Modules:
  0.0 118.1 jit_solution(6426497635479942977)
XLA Ops:
  0.0 1.9 %split_query.1 = bf16[32,64,128]{2,1,0:T(8,128)(2,1)} custom-call(bf16[256,1024]{1,0:T(8,128)(2,1)} %query_ref.1), custom_call_target="tpu_custom_call" | custom-call | tf_op jit(solution)/shard_map/split_query/pallas_call | solution.py:44
  1.9 10.6 %all-to-all-start = ((bf16[32,64,128]{2,1,0:T(8,128)(2,1)}), bf16[32,64,128]{2,1,0:T(8,128)(2,1)S(1)}, u32[]{:S(2)}, u32[]{:S(2)}) async-start(bf16[32,64,128]{2,1,0:T(8,128)(2,1)} %split_query.1), calls=%async_computation | async-start | bytes 1048576 | tf_op jit(solution)/shard_map/all_to_all | solution.py:22
  12.5 4.6 %collective-permute-start = (bf16[128,1024]{1,0:T(8,128)(2,1)S(1)}, bf16[128,1024]{1,0:T(8,128)(2,1)S(1)}, u32[]{:S(2)}, u32[]{:S(2)}) collective-permute-start(bf16[128,1024]{1,0:T(8,128)(2,1)S(1)} %copy-done.3), channel_id=1, source_target_pairs={{128,0},{256,128},{384,256},{0,384},{129,1},{257,129},{385,257},{1... | collective-permute-start | bytes 786440 | tf_op jit(solution)/shard_map/ppermute | solution.py:179
  17.2 6.5 %all-to-all-done = bf16[32,64,128]{2,1,0:T(8,128)(2,1)S(1)} async-done(((bf16[32,64,128]{2,1,0:T(8,128)(2,1)}), bf16[32,64,128]{2,1,0:T(8,128)(2,1)S(1)}, u32[]{:S(2)}, u32[]{:S(2)}) %all-to-all-start) | async-done | bytes 524320 | tf_op jit(solution)/shard_map/all_to_all | solution.py:22
  23.6 0.9 copy.13
  24.5 13.0 %all-to-all-start.1 = ((bf16[16,128,128]{2,1,0:T(8,128)(2,1)}), bf16[16,128,128]{2,1,0:T(8,128)(2,1)S(1)}, u32[]{:S(2)}, u32[]{:S(2)}) async-start(bf16[16,128,128]{2,1,0:T(8,128)(2,1)} %bitcast.5), calls=%async_computation.1 | async-start | bytes 1048576 | tf_op jit(solution)/shard_map/all_to_all | solution.py:22
  37.5 3.2 %collective-permute-start.1 = (bf16[128,1024]{1,0:T(8,128)(2,1)S(1)}, bf16[128,1024]{1,0:T(8,128)(2,1)S(1)}, u32[]{:S(2)}, u32[]{:S(2)}) collective-permute-start(bf16[128,1024]{1,0:T(8,128)(2,1)S(1)} %collective-permute-done), channel_id=1, source_target_pairs={{128,0},{256,128},{384,256},{0,384},{129,1},{257,129},{385,257},{1... | collective-permute-start | bytes 786440 | tf_op jit(solution)/shard_map/ppermute | solution.py:181
  40.7 2.1 %collective-permute-start.2 = (bf16[128,1024]{1,0:T(8,128)(2,1)S(1)}, bf16[128,1024]{1,0:T(8,128)(2,1)S(1)}, u32[]{:S(2)}, u32[]{:S(2)}) collective-permute-start(bf16[128,1024]{1,0:T(8,128)(2,1)S(1)} %copy-done.3), channel_id=1, source_target_pairs={{0,128},{128,256},{256,384},{384,0},{1,129},{129,257},{257,385},{3... | collective-permute-start | bytes 786440 | tf_op jit(solution)/shard_map/ppermute | solution.py:180
  42.9 3.1 %collective-permute-done.1 = bf16[128,1024]{1,0:T(8,128)(2,1)S(1)} collective-permute-done((bf16[128,1024]{1,0:T(8,128)(2,1)S(1)}, bf16[128,1024]{1,0:T(8,128)(2,1)S(1)}, u32[]{:S(2)}, u32[]{:S(2)}) %collective-permute-start.1) | collective-permute-done | bytes 262176 | tf_op jit(solution)/shard_map/ppermute | solution.py:181
  46.0 4.7 %collective-permute-done.2 = bf16[128,1024]{1,0:T(8,128)(2,1)S(1)} collective-permute-done((bf16[128,1024]{1,0:T(8,128)(2,1)S(1)}, bf16[128,1024]{1,0:T(8,128)(2,1)S(1)}, u32[]{:S(2)}, u32[]{:S(2)}) %collective-permute-start.2) | collective-permute-done | bytes 262176 | tf_op jit(solution)/shard_map/ppermute | solution.py:180
  50.7 3.8 %collective-permute-start.3 = (bf16[512,1024]{1,0:T(8,128)(2,1)S(1)}, bf16[512,1024]{1,0:T(8,128)(2,1)}, u32[]{:S(2)}, u32[]{:S(2)}) collective-permute-start(bf16[512,1024]{1,0:T(8,128)(2,1)S(1)} %constant_dynamic-update-slice_fusion), channel_id=1, source_target_pairs={{0,64},{64,0},{1,65},{65,1},{2,66},{66,2},{3,67},{67,3},{4,68},{68... | collective-permute-start | bytes 3145736 | tf_op jit(solution)/shard_map/ppermute | solution.py:183
  54.5 0.7 copy-done.6
  55.2 0.6 reshape.20.refs_1_
  55.8 0.6 pad_add_fusion.refs_0_.place_ref
  56.5 0.9 copy-done.5
  57.5 0.4 convolution_convert_fusion.1
  57.9 1.7 %convolution_convert_fusion = bf16[512,256]{1,0:T(8,128)(2,1)S(1)} fusion(bf16[512,1024]{1,0:T(8,128)(2,1)} %collective-permute-done.3, bf16[1024,256]{1,0:T(8,128)(2,1)S(1)} %constant_dynamic-update-slice_fusion.4), kind=kOutput, calls=%fused_computation | convolution fusion | flops 268566528 | bytes 1835008 | tf_op jit(solution)/shard_map/dot_general | solution.py:187
  59.6 0.7 all-to-all-done.1.refs_3_
  60.3 5.8 %attend.1 = bf16[8,16,16,128]{3,2,1,0:T(8,128)(2,1)S(1)} custom-call(s32[3]{0:T(128)} %pad_add_fusion.refs_0_.place_ref, s32[64]{0:T(128)} %reshape.20.refs_1_, s32[16]{0:T(128)} %refs_2_.1, bf16[16,128,128]{2,1,0:T(8,128)(2,1)S(1)} %all-to-all-done.1.refs_3_, bf16[1024,256]{1,0:T(8,128)(2,1)S(1)} %pad_maximum_fusion.refs_4_), custom_call_target="tpu_custom_call" | custom-call | tf_op jit(solution)/shard_map/attend/pallas_call | solution.py:93
  66.1 19.6 %all_to_all.25 = bf16[8,16,16,128]{3,2,1,0:T(8,128)(2,1)S(1)} all-to-all(bf16[8,16,16,128]{3,2,1,0:T(8,128)(2,1)S(1)} %attend.1), channel_id=1, replica_groups=mesh['x'=4,'core'=2,'z'=16,'y'=4] {'x','core'}, dimensions={0} | all-to-all | bytes 1048576 | tf_op jit(solution)/shard_map/all_to_all | solution.py:22
  85.7 0.9 wall_flux.1
  86.6 17.3 %all_to_all.26 = f32[16,4,128]{2,1,0:T(4,128)S(1)} all-to-all(f32[16,4,128]{2,1,0:T(4,128)S(1)} %wall_flux.1), channel_id=1, replica_groups=mesh['x'=4,'core'=2,'z'=16,'y'=4] {'z'}, dimensions={0} | all-to-all | bytes 65536 | tf_op jit(solution)/shard_map/all_to_all | solution.py:22
  103.9 12.9 %all_to_all.27 = f32[32,8,128]{2,1,0:T(8,128)S(1)} all-to-all(f32[32,8,128]{2,1,0:T(8,128)S(1)} %bitcast.20), channel_id=1, replica_groups=mesh['x'=4,'core'=2,'z'=16,'y'=4] {'x','core','y'}, dimensions={0} | all-to-all | bytes 262144 | tf_op jit(solution)/shard_map/all_to_all | solution.py:22
  116.8 1.3 %place_flux.1 = f32[4,256]{1,0:T(4,128)} custom-call(s32[3]{0:T(128)} %pad_add_fusion.refs_0_.place_ref, f32[4,2,4,8,128]{4,3,2,1,0:T(8,128)S(1)} %bitcast.17), custom_call_target="tpu_custom_call" | custom-call | tf_op jit(solution)/shard_map/place_flux/pallas_call | solution.py:146
  (23 shorter events, 0.4 us)
Async XLA Ops:
  1.9 10.6 %copy-start.3 = (bf16[128,1024]{1,0:T(8,128)(2,1)S(1)}, bf16[128,1024]{1,0:T(8,128)(2,1)}, u32[]{:S(2)}) copy-start(bf16[128,1024]{1,0:T(8,128)(2,1)} %param.9) | copy-start | bytes 786436
  1.9 21.7 %all-to-all-start = ((bf16[32,64,128]{2,1,0:T(8,128)(2,1)}), bf16[32,64,128]{2,1,0:T(8,128)(2,1)S(1)}, u32[]{:S(2)}, u32[]{:S(2)}) async-start(bf16[32,64,128]{2,1,0:T(8,128)(2,1)} %split_query.1), calls=%async_computation | async-start | bytes 1048576 | tf_op jit(solution)/shard_map/all_to_all | solution.py:22
  12.5 25.0 %collective-permute-start = (bf16[128,1024]{1,0:T(8,128)(2,1)S(1)}, bf16[128,1024]{1,0:T(8,128)(2,1)S(1)}, u32[]{:S(2)}, u32[]{:S(2)}) collective-permute-start(bf16[128,1024]{1,0:T(8,128)(2,1)S(1)} %copy-done.3), channel_id=1, source_target_pairs={{128,0},{256,128},{384,256},{0,384},{129,1},{257,129},{385,257},{1... | collective-permute-start | bytes 786440 | tf_op jit(solution)/shard_map/ppermute | solution.py:179
  24.5 35.8 %all-to-all-start.1 = ((bf16[16,128,128]{2,1,0:T(8,128)(2,1)}), bf16[16,128,128]{2,1,0:T(8,128)(2,1)S(1)}, u32[]{:S(2)}, u32[]{:S(2)}) async-start(bf16[16,128,128]{2,1,0:T(8,128)(2,1)} %bitcast.5), calls=%async_computation.1 | async-start | bytes 1048576 | tf_op jit(solution)/shard_map/all_to_all | solution.py:22
  37.5 8.4 %collective-permute-start.1 = (bf16[128,1024]{1,0:T(8,128)(2,1)S(1)}, bf16[128,1024]{1,0:T(8,128)(2,1)S(1)}, u32[]{:S(2)}, u32[]{:S(2)}) collective-permute-start(bf16[128,1024]{1,0:T(8,128)(2,1)S(1)} %collective-permute-done), channel_id=1, source_target_pairs={{128,0},{256,128},{384,256},{0,384},{129,1},{257,129},{385,257},{1... | collective-permute-start | bytes 786440 | tf_op jit(solution)/shard_map/ppermute | solution.py:181
  40.7 10.0 %collective-permute-start.2 = (bf16[128,1024]{1,0:T(8,128)(2,1)S(1)}, bf16[128,1024]{1,0:T(8,128)(2,1)S(1)}, u32[]{:S(2)}, u32[]{:S(2)}) collective-permute-start(bf16[128,1024]{1,0:T(8,128)(2,1)S(1)} %copy-done.3), channel_id=1, source_target_pairs={{0,128},{128,256},{256,384},{384,0},{1,129},{129,257},{257,385},{3... | collective-permute-start | bytes 786440 | tf_op jit(solution)/shard_map/ppermute | solution.py:180
  46.0 10.5 %copy-start.4 = (bf16[1024,128]{1,0:T(8,128)(2,1)S(1)}, bf16[1024,128]{1,0:T(8,128)(2,1)}, u32[]{:S(2)}) copy-start(bf16[1024,128]{1,0:T(8,128)(2,1)} %param.10) | copy-start | bytes 786436
  50.7 7.2 %collective-permute-start.3 = (bf16[512,1024]{1,0:T(8,128)(2,1)S(1)}, bf16[512,1024]{1,0:T(8,128)(2,1)}, u32[]{:S(2)}, u32[]{:S(2)}) collective-permute-start(bf16[512,1024]{1,0:T(8,128)(2,1)S(1)} %constant_dynamic-update-slice_fusion), channel_id=1, source_target_pairs={{0,64},{64,0},{1,65},{65,1},{2,66},{66,2},{3,67},{67,3},{4,68},{68... | collective-permute-start | bytes 3145736 | tf_op jit(solution)/shard_map/ppermute | solution.py:183
  54.5 0.7 copy-start.6
  56.4 1.0 copy-start.5
  59.6 26.1 %copy-start = (bf16[1024,512]{1,0:T(8,128)(2,1)S(1)}, bf16[1024,512]{1,0:T(8,128)(2,1)}, u32[]{:S(2)}) copy-start(bf16[1024,512]{1,0:T(8,128)(2,1)} %up_ref.1) | copy-start | bytes 3145732
  66.1 19.6 %copy-start.1 = (f32[1024]{0:T(1024)S(1)}, f32[1024]{0:T(1024)}, u32[]{:S(2)}) copy-start(f32[1024]{0:T(1024)} %param.15) | copy-start | bytes 12292
  66.1 19.6 %copy-start.2 = (bf16[4,512]{1,0:T(4,128)(2,1)S(1)}, bf16[4,512]{1,0:T(4,128)(2,1)}, u32[]{:S(2)}) copy-start(bf16[4,512]{1,0:T(4,128)(2,1)} %flux_ref.1) | copy-start | bytes 12292

commit v6 on v3

--- a/solution.py
+++ b/solution.py
@@ -26,9 +26,10 @@
     return [pltpu.with_memory_space_constraint(array, pltpu.VMEM) for array in arrays]
 
 
-def attend_step(step, per, place_ref, cells_ref, counts_ref, query_ref, kv_ref, out_ref):
+def attend_step(step, per, cells_ref, counts_ref, query_ref, kv_ref, out_ref):
     parts, _, part_rows, width = out_ref.shape
     cells = kv_ref.shape[0] // BLK
+    x, core = lax.axis_index("x"), lax.axis_index("core")
     first = lax.broadcasted_iota(jnp.int32, (BLK, width), 1) < HD
     for item in range(per):
         block = step * per + item
@@ -39,9 +40,9 @@
         ).astype(jnp.bfloat16)
         picked = []
         for slot in range(LMAX):
-            cell = jnp.clip(cells_ref[block * LMAX + slot], 0, cells - 1)
-            far = (cell // 2 - place_ref[0] + cells) % (cells // 2)
-            row = far + (cells // 2) * ((cell + place_ref[1]) % 2)
+            cell = jnp.clip(cells_ref[slot, block], 0, cells - 1)
+            far = (cell // 2 - x + cells) % (cells // 2)
+            row = far + (cells // 2) * ((cell + core) % 2)
             picked.append(pl.multiple_of(row * BLK, BLK))
         keys = jnp.concatenate([kv_ref[pl.ds(row, BLK), :width] for row in picked], axis=0)
         values = jnp.concatenate([kv_ref[pl.ds(row, BLK), width:] for row in picked], axis=0)
@@ -61,19 +62,19 @@
 
 
 def attend_kernel(per, *refs):
-    steps = refs[3].shape[0] // per
+    steps = refs[2].shape[0] // per
     lax.fori_loop(0, steps, lambda step, _: attend_step(step, per, *refs), None)
 
 
-def attend(query, kv, place, cells, counts, parts, per):
+def attend(query, kv, cells, counts, parts, per):
     blocks, _, width = query.shape
     return pl.pallas_call(
         functools.partial(attend_kernel, per),
         out_shape=pltpu.VMEM((parts, blocks, BLK // parts, width), jnp.bfloat16),
-        in_specs=[pl.BlockSpec(memory_space=pltpu.SMEM)] * 3
+        in_specs=[pl.BlockSpec(memory_space=pltpu.SMEM)] * 2
         + [pl.BlockSpec(memory_space=pltpu.VMEM)] * 2,
         name="attend",
-    )(place, cells, counts, *on_chip(query, kv))
+    )(cells, counts, *on_chip(query, kv))
 
 
 def flux_kernel(stream_ref, gain_ref, up_ref, flux_ref, out_ref):
@@ -105,11 +106,11 @@
     )(*on_chip(stream, norm_gain[None, :], up_weight, flux_weight))
 
 
-def place_kernel(y_ref, flux_ref, out_ref):
+def place_kernel(flux_ref, out_ref):
     _, halves, n_y, both, _ = flux_ref.shape
     comps, rows = out_ref.shape
     few = rows * comps // (halves * n_y * both)
-    mine = flux_ref.at[y_ref[0]]
+    mine = flux_ref.at[lax.axis_index("y")]
     pieces = [
         mine[half, low, top * comps : (top + 1) * comps, :few]
         for top in range(both // comps)
@@ -119,16 +120,13 @@
     out_ref[...] = jnp.concatenate(pieces, axis=1)
 
 
-def place_flux(flux, comps, rows, y):
+def place_flux(flux, comps, rows):
     return pl.pallas_call(
         place_kernel,
         out_shape=jax.ShapeDtypeStruct((comps, rows), jnp.float32),
-        in_specs=[
-            pl.BlockSpec(memory_space=pltpu.SMEM),
-            pl.BlockSpec(memory_space=pltpu.VMEM),
-        ],
+        in_specs=[pl.BlockSpec(memory_space=pltpu.VMEM)],
         name="place_flux",
-    )(y, *on_chip(flux))
+    )(*on_chip(flux))
 
 
 def body(
@@ -167,8 +165,7 @@
         ],
         axis=0,
     )
-    place = jnp.stack([lax.axis_index("x"), lax.axis_index("core")]).astype(jnp.int32)
-    stream = attend(query, kv, place, cell_list.reshape(-1), cell_count, grp, 4)
+    stream = attend(query, kv, cell_list.T, cell_count, grp, 16)
     stream = exchange(stream, GRP)
     flux = wall_flux(
         stream.reshape(grp, -1, width), norm_gain, up_weight, flux_weight, n_z
@@ -178,10 +175,7 @@
     flux = jnp.broadcast_to(flux, (grp, n_y, hi * comps, LANES))
     flux = exchange(flux.reshape(grp * n_y, hi * comps, LANES), PLANE)
     return place_flux(
-        flux.reshape(n_x, 2, n_y, hi * comps, LANES),
-        comps,
-        panel_query.shape[0],
-        lax.axis_index("y").reshape(1),
+        flux.reshape(n_x, 2, n_y, hi * comps, LANES), comps, panel_query.shape[0]
     )
 
 

time: 120 us -> 118 us (0.983)
  blocking collectives: 36.9 us -> 49.8 us
  starting transfers between devices: 43.2 us -> 37.4 us
  waiting for transfers between devices: 22.4 us -> 18.9 us
  local copies, waits for them, and re-layouts: 6.15 us -> 3.14 us
  matrix products: 2.1 us -> 0.88 us
    all_to_all x2 -> x3, blocking collectives: 36.9 us -> 49.8 us  [exchange(): return lax.all_to_all(array, axes, split_axis=0, concat_axis=0, tiled=True)]
    all_to_all x3 -> x2, starting transfers between devices: 29.5 us -> 23.6 us  [exchange(): return lax.all_to_all(array, axes, split_axis=0, concat_axis=0, tiled=True)]
    all_to_all x3 -> x2, waiting for transfers between devices: 14.7 us -> 9.44 us  [exchange(): return lax.all_to_all(array, axes, split_axis=0, concat_axis=0, tiled=True)]
    ppermute x1, waiting for transfers between devices: 0.01 us -> 1.67 us  [body(): across = lax.ppermute(along, 'core', [(0, 1), (1, 0)])]
    unnamed x20 -> x17, local copies, waits for them, and re-layouts: 2.92 us -> 1.27 us
    dot_general x2, matrix products: 2.1 us -> 0.88 us  [body(): jnp.dot(part, weights, preferred_element_type=jnp.float32)]
  transfers between devices with their start and end apart: 7 -> 6, of which waited for: 5 -> 5; matrix products, arithmetic and copies ran while one was open for 4% -> 2% of each run, Pallas kernels for 0% -> 0%
where the time goes in v6:
time: 118 us
  blocking collectives  49.8 us (42%)
  starting transfers between devices  37.4 us (32%)
  waiting for transfers between devices  18.9 us (16%)
  Pallas kernels  7.4 us (6%)
  local copies, waits for them, and re-layouts  3.14 us (3%)
    all_to_all x3, blocking collectives, exchange(): return lax.all_to_all(array, axes, split_axis=0, concat_axis=0, tiled=True)  49.8 us
    all_to_all x2, starting transfers between devices, exchange(): return lax.all_to_all(array, axes, split_axis=0, concat_axis=0, tiled=True)  23.6 us
    all_to_all x2, waiting for transfers between devices, exchange(): return lax.all_to_all(array, axes, split_axis=0, concat_axis=0, tiled=True)  9.44 us
    pallas_call x1, Pallas kernels, attend(): pl.pallas_call(functools.partial(attend_kernel, per), out_shape=pltpu.VME...  5.87 us
    ppermute x1, waiting for transfers between devices, body(): one_down = lax.ppermute(anchor_states, 'x', down)  4.66 us
    ppermute x1, starting transfers between devices, body(): one_up = lax.ppermute(anchor_states, 'x', up)  4.65 us
    ppermute x1, starting transfers between devices, body(): across = lax.ppermute(along, 'core', [(0, 1), (1, 0)])  3.91 us
    ppermute x1, starting transfers between devices, body(): two_up = lax.ppermute(one_up, 'x', up)  3.16 us
  transfers between devices with their start and end apart: 6, of which 5 were waited for; matrix products, arithmetic and copies ran while one was open for 2% of the time, Pallas kernels for 0%

profile of v6, /device:TPU:1, one launch (start us, length us, event | category | flops | bytes accessed | tf_op | source)
XLA Modules:
  0.0 117.7 jit_solution(4390119035943370665)
XLA Ops:
  0.0 1.1 copy.13
  1.1 0.9 copy.11
  2.1 10.6 %all-to-all-start = ((bf16[32,64,128]{2,1,0:T(8,128)(2,1)}), bf16[32,64,128]{2,1,0:T(8,128)(2,1)S(1)}, u32[]{:S(2)}, u32[]{:S(2)}) async-start(bf16[32,64,128]{2,1,0:T(8,128)(2,1)} %bitcast.2), calls=%async_computation | async-start | bytes 1048576 | tf_op jit(solution)/shard_map/all_to_all | solution.py:22
  12.7 4.6 %collective-permute-start = (bf16[128,1024]{1,0:T(8,128)(2,1)S(1)}, bf16[128,1024]{1,0:T(8,128)(2,1)S(1)}, u32[]{:S(2)}, u32[]{:S(2)}) collective-permute-start(bf16[128,1024]{1,0:T(8,128)(2,1)S(1)} %copy-done.3), channel_id=1, source_target_pairs={{128,0},{256,128},{384,256},{0,384},{129,1},{257,129},{385,257},{1... | collective-permute-start | bytes 786440 | tf_op jit(solution)/shard_map/ppermute | solution.py:155
  17.3 6.5 %all-to-all-done = bf16[32,64,128]{2,1,0:T(8,128)(2,1)S(1)} async-done(((bf16[32,64,128]{2,1,0:T(8,128)(2,1)}), bf16[32,64,128]{2,1,0:T(8,128)(2,1)S(1)}, u32[]{:S(2)}, u32[]{:S(2)}) %all-to-all-start) | async-done | bytes 524320 | tf_op jit(solution)/shard_map/all_to_all | solution.py:22
  23.8 0.9 copy.12
  24.6 13.0 %all-to-all-start.1 = ((bf16[16,128,128]{2,1,0:T(8,128)(2,1)}), bf16[16,128,128]{2,1,0:T(8,128)(2,1)S(1)}, u32[]{:S(2)}, u32[]{:S(2)}) async-start(bf16[16,128,128]{2,1,0:T(8,128)(2,1)} %bitcast.5), calls=%async_computation.1 | async-start | bytes 1048576 | tf_op jit(solution)/shard_map/all_to_all | solution.py:22
  37.6 3.2 %collective-permute-start.1 = (bf16[128,1024]{1,0:T(8,128)(2,1)S(1)}, bf16[128,1024]{1,0:T(8,128)(2,1)S(1)}, u32[]{:S(2)}, u32[]{:S(2)}) collective-permute-start(bf16[128,1024]{1,0:T(8,128)(2,1)S(1)} %collective-permute-done), channel_id=1, source_target_pairs={{128,0},{256,128},{384,256},{0,384},{129,1},{257,129},{385,257},{1... | collective-permute-start | bytes 786440 | tf_op jit(solution)/shard_map/ppermute | solution.py:157
  40.8 2.1 %collective-permute-start.2 = (bf16[128,1024]{1,0:T(8,128)(2,1)S(1)}, bf16[128,1024]{1,0:T(8,128)(2,1)S(1)}, u32[]{:S(2)}, u32[]{:S(2)}) collective-permute-start(bf16[128,1024]{1,0:T(8,128)(2,1)S(1)} %copy-done.3), channel_id=1, source_target_pairs={{0,128},{128,256},{256,384},{384,0},{1,129},{129,257},{257,385},{3... | collective-permute-start | bytes 786440 | tf_op jit(solution)/shard_map/ppermute | solution.py:156
  43.0 3.1 %collective-permute-done.1 = bf16[128,1024]{1,0:T(8,128)(2,1)S(1)} collective-permute-done((bf16[128,1024]{1,0:T(8,128)(2,1)S(1)}, bf16[128,1024]{1,0:T(8,128)(2,1)S(1)}, u32[]{:S(2)}, u32[]{:S(2)}) %collective-permute-start.1) | collective-permute-done | bytes 262176 | tf_op jit(solution)/shard_map/ppermute | solution.py:157
  46.1 4.7 %collective-permute-done.2 = bf16[128,1024]{1,0:T(8,128)(2,1)S(1)} collective-permute-done((bf16[128,1024]{1,0:T(8,128)(2,1)S(1)}, bf16[128,1024]{1,0:T(8,128)(2,1)S(1)}, u32[]{:S(2)}, u32[]{:S(2)}) %collective-permute-start.2) | collective-permute-done | bytes 262176 | tf_op jit(solution)/shard_map/ppermute | solution.py:156
  50.8 3.9 %collective-permute-start.3 = (bf16[512,1024]{1,0:T(8,128)(2,1)S(1)}, bf16[512,1024]{1,0:T(8,128)(2,1)S(1)}, u32[]{:S(2)}, u32[]{:S(2)}) collective-permute-start(bf16[512,1024]{1,0:T(8,128)(2,1)S(1)} %constant_dynamic-update-slice_fusion), channel_id=1, source_target_pairs={{0,64},{64,0},{1,65},{65,1},{2,66},{66,2},{3,67},{67,3},{4,68},{68... | collective-permute-start | bytes 3145736 | tf_op jit(solution)/shard_map/ppermute | solution.py:159
  54.8 0.1 constant_dynamic-update-slice_fusion.4
  54.8 0.4 convolution_convert_fusion.1
  55.3 1.7 %collective-permute-done.3 = bf16[512,1024]{1,0:T(8,128)(2,1)S(1)} collective-permute-done((bf16[512,1024]{1,0:T(8,128)(2,1)S(1)}, bf16[512,1024]{1,0:T(8,128)(2,1)S(1)}, u32[]{:S(2)}, u32[]{:S(2)}) %collective-permute-start.3) | collective-permute-done | bytes 1048608 | tf_op jit(solution)/shard_map/ppermute | solution.py:159
  57.0 0.4 convolution_convert_fusion
  57.5 3.0 %all-to-all-done.1.refs_2_ = bf16[16,128,128]{2,1,0:T(8,128)(2,1)S(1)} async-done(((bf16[16,128,128]{2,1,0:T(8,128)(2,1)}), bf16[16,128,128]{2,1,0:T(8,128)(2,1)S(1)}, u32[]{:S(2)}, u32[]{:S(2)}) %all-to-all-start.1) | async-done | bytes 524320 | tf_op jit(solution)/shard_map/all_to_all | solution.py:22
  60.4 5.9 %attend.1 = bf16[8,16,16,128]{3,2,1,0:T(8,128)(2,1)S(1)} custom-call(s32[4,16]{1,0:T(4,128)} %bitcast.28, s32[16]{0:T(128)} %refs_1_.1, bf16[16,128,128]{2,1,0:T(8,128)(2,1)S(1)} %all-to-all-done.1.refs_2_, bf16[1024,256]{1,0:T(8,128)(2,1)S(1)} %pad_maximum_fusion.refs_3_), custom_call_target="tpu_custom_call" | custom-call | tf_op jit(solution)/shard_map/attend/pallas_call | solution.py:71
  66.3 0.0 copy-start.2
  66.3 19.6 %all_to_all.25 = bf16[8,16,16,128]{3,2,1,0:T(8,128)(2,1)S(1)} all-to-all(bf16[8,16,16,128]{3,2,1,0:T(8,128)(2,1)S(1)} %attend.1), channel_id=1, replica_groups=mesh['x'=4,'core'=2,'z'=16,'y'=4] {'x','core'}, dimensions={0} | all-to-all | bytes 1048576 | tf_op jit(solution)/shard_map/all_to_all | solution.py:22
  85.9 0.9 wall_flux.1
  86.8 17.3 %all_to_all.26 = f32[16,4,128]{2,1,0:T(4,128)S(1)} all-to-all(f32[16,4,128]{2,1,0:T(4,128)S(1)} %wall_flux.1), channel_id=1, replica_groups=mesh['x'=4,'core'=2,'z'=16,'y'=4] {'z'}, dimensions={0} | all-to-all | bytes 65536 | tf_op jit(solution)/shard_map/all_to_all | solution.py:22
  104.1 12.9 %all_to_all.27 = f32[32,8,128]{2,1,0:T(8,128)S(1)} all-to-all(f32[32,8,128]{2,1,0:T(8,128)S(1)} %bitcast.25), channel_id=1, replica_groups=mesh['x'=4,'core'=2,'z'=16,'y'=4] {'x','core','y'}, dimensions={0} | all-to-all | bytes 262144 | tf_op jit(solution)/shard_map/all_to_all | solution.py:22
  117.0 0.7 place_flux.1
  (19 shorter events, 0.2 us)
Async XLA Ops:
  2.1 10.6 %copy-start.3 = (bf16[128,1024]{1,0:T(8,128)(2,1)S(1)}, bf16[128,1024]{1,0:T(8,128)(2,1)}, u32[]{:S(2)}) copy-start(bf16[128,1024]{1,0:T(8,128)(2,1)} %param.9) | copy-start | bytes 786436
  2.1 21.7 %all-to-all-start = ((bf16[32,64,128]{2,1,0:T(8,128)(2,1)}), bf16[32,64,128]{2,1,0:T(8,128)(2,1)S(1)}, u32[]{:S(2)}, u32[]{:S(2)}) async-start(bf16[32,64,128]{2,1,0:T(8,128)(2,1)} %bitcast.2), calls=%async_computation | async-start | bytes 1048576 | tf_op jit(solution)/shard_map/all_to_all | solution.py:22
  12.7 25.0 %collective-permute-start = (bf16[128,1024]{1,0:T(8,128)(2,1)S(1)}, bf16[128,1024]{1,0:T(8,128)(2,1)S(1)}, u32[]{:S(2)}, u32[]{:S(2)}) collective-permute-start(bf16[128,1024]{1,0:T(8,128)(2,1)S(1)} %copy-done.3), channel_id=1, source_target_pairs={{128,0},{256,128},{384,256},{0,384},{129,1},{257,129},{385,257},{1... | collective-permute-start | bytes 786440 | tf_op jit(solution)/shard_map/ppermute | solution.py:155
  24.6 35.8 %all-to-all-start.1 = ((bf16[16,128,128]{2,1,0:T(8,128)(2,1)}), bf16[16,128,128]{2,1,0:T(8,128)(2,1)S(1)}, u32[]{:S(2)}, u32[]{:S(2)}) async-start(bf16[16,128,128]{2,1,0:T(8,128)(2,1)} %bitcast.5), calls=%async_computation.1 | async-start | bytes 1048576 | tf_op jit(solution)/shard_map/all_to_all | solution.py:22
  37.6 8.4 %collective-permute-start.1 = (bf16[128,1024]{1,0:T(8,128)(2,1)S(1)}, bf16[128,1024]{1,0:T(8,128)(2,1)S(1)}, u32[]{:S(2)}, u32[]{:S(2)}) collective-permute-start(bf16[128,1024]{1,0:T(8,128)(2,1)S(1)} %collective-permute-done), channel_id=1, source_target_pairs={{128,0},{256,128},{384,256},{0,384},{129,1},{257,129},{385,257},{1... | collective-permute-start | bytes 786440 | tf_op jit(solution)/shard_map/ppermute | solution.py:157
  40.8 10.0 %collective-permute-start.2 = (bf16[128,1024]{1,0:T(8,128)(2,1)S(1)}, bf16[128,1024]{1,0:T(8,128)(2,1)S(1)}, u32[]{:S(2)}, u32[]{:S(2)}) collective-permute-start(bf16[128,1024]{1,0:T(8,128)(2,1)S(1)} %copy-done.3), channel_id=1, source_target_pairs={{0,128},{128,256},{256,384},{384,0},{1,129},{129,257},{257,385},{3... | collective-permute-start | bytes 786440 | tf_op jit(solution)/shard_map/ppermute | solution.py:156
  46.1 8.6 %copy-start.4 = (bf16[1024,128]{1,0:T(8,128)(2,1)S(1)}, bf16[1024,128]{1,0:T(8,128)(2,1)}, u32[]{:S(2)}) copy-start(bf16[1024,128]{1,0:T(8,128)(2,1)} %param.10) | copy-start | bytes 786436
  50.8 4.0 %copy-start.5 = (bf16[1024,128]{1,0:T(8,128)(2,1)S(1)}, bf16[1024,128]{1,0:T(8,128)(2,1)}, u32[]{:S(2)}) copy-start(bf16[1024,128]{1,0:T(8,128)(2,1)} %param.11) | copy-start | bytes 786436
  50.8 6.2 %collective-permute-start.3 = (bf16[512,1024]{1,0:T(8,128)(2,1)S(1)}, bf16[512,1024]{1,0:T(8,128)(2,1)S(1)}, u32[]{:S(2)}, u32[]{:S(2)}) collective-permute-start(bf16[512,1024]{1,0:T(8,128)(2,1)S(1)} %constant_dynamic-update-slice_fusion), channel_id=1, source_target_pairs={{0,64},{64,0},{1,65},{65,1},{2,66},{66,2},{3,67},{67,3},{4,68},{68... | collective-permute-start | bytes 3145736 | tf_op jit(solution)/shard_map/ppermute | solution.py:159
  60.4 25.5 %copy-start = (bf16[1024,512]{1,0:T(8,128)(2,1)S(1)}, bf16[1024,512]{1,0:T(8,128)(2,1)}, u32[]{:S(2)}) copy-start(bf16[1024,512]{1,0:T(8,128)(2,1)} %up_ref.1) | copy-start | bytes 3145732
  66.3 19.6 %copy-start.1 = (f32[1024]{0:T(1024)S(1)}, f32[1024]{0:T(1024)}, u32[]{:S(2)}) copy-start(f32[1024]{0:T(1024)} %param.15) | copy-start | bytes 12292
  66.3 19.6 %copy-start.2 = (bf16[4,512]{1,0:T(4,128)(2,1)S(1)}, bf16[4,512]{1,0:T(4,128)(2,1)}, u32[]{:S(2)}) copy-start(bf16[4,512]{1,0:T(4,128)(2,1)} %flux_ref.1) | copy-start | bytes 12292

commit v7 on v6

--- a/solution.py
+++ b/solution.py
@@ -31,6 +31,7 @@
     cells = kv_ref.shape[0] // BLK
     x, core = lax.axis_index("x"), lax.axis_index("core")
     first = lax.broadcasted_iota(jnp.int32, (BLK, width), 1) < HD
+    ones = jnp.ones((LMAX * BLK, width), jnp.bfloat16)
     for item in range(per):
         block = step * per + item
         query = query_ref[block].astype(jnp.float32)
@@ -53,9 +54,12 @@
         scores = scores + jnp.where(slot_of < counts_ref[block], 0.0, -jnp.inf)
         top = jnp.max(scores, axis=-1, keepdims=True)
         expo = jnp.exp(scores - top)
-        total = jnp.sum(expo, axis=-1, keepdims=True)
-        summed = jnp.dot(expo.astype(jnp.bfloat16), values, preferred_element_type=jnp.float32)
-        summed = summed / total
+        summed = jnp.dot(
+            expo.astype(jnp.bfloat16),
+            jnp.concatenate([values, ones], axis=1),
+            preferred_element_type=jnp.float32,
+        )
+        summed = summed[:, :width] / summed[:, width:]
         attended = jnp.where(first, summed[:BLK], summed[BLK:]).astype(jnp.bfloat16)
         stream = query + attended.astype(jnp.float32)
         out_ref[:, block] = stream.astype(jnp.bfloat16).reshape(parts, part_rows, width)

time: 118 us -> 116 us (0.983)
  Pallas kernels: 7.4 us -> 5.1 us
    pallas_call x1, Pallas kernels: 5.87 us -> 3.57 us  [attend(): pl.pallas_call(functools.partial(attend_kernel, per), out_shape=pltpu.VME...]
where the time goes in v7:
time: 116 us; the launch traced here: 115 us
  blocking collectives  49.8 us (43%)
  starting transfers between devices  37.4 us (32%)
  waiting for transfers between devices  18.9 us (16%)
  Pallas kernels  5.1 us (4%)
  local copies, waits for them, and re-layouts  3.14 us (3%)
    all_to_all x3, blocking collectives, exchange(): return lax.all_to_all(array, axes, split_axis=0, concat_axis=0, tiled=True)  49.8 us
    all_to_all x2, starting transfers between devices, exchange(): return lax.all_to_all(array, axes, split_axis=0, concat_axis=0, tiled=True)  23.6 us
    all_to_all x2, waiting for transfers between devices, exchange(): return lax.all_to_all(array, axes, split_axis=0, concat_axis=0, tiled=True)  9.44 us
    ppermute x1, waiting for transfers between devices, body(): one_down = lax.ppermute(anchor_states, 'x', down)  4.66 us
    ppermute x1, starting transfers between devices, body(): one_up = lax.ppermute(anchor_states, 'x', up)  4.65 us
    ppermute x1, starting transfers between devices, body(): across = lax.ppermute(along, 'core', [(0, 1), (1, 0)])  3.91 us
    pallas_call x1, Pallas kernels, attend(): pl.pallas_call(functools.partial(attend_kernel, per), out_shape=pltpu.VME...  3.57 us
    ppermute x1, starting transfers between devices, body(): two_up = lax.ppermute(one_up, 'x', up)  3.16 us
  transfers between devices with their start and end apart: 6, of which 5 were waited for; matrix products, arithmetic and copies ran while one was open for 2% of the time, Pallas kernels for 0%

profile of v7, /device:TPU:1, one launch (start us, length us, event | category | flops | bytes accessed | tf_op | source)
XLA Modules:
  0.0 115.4 jit_solution(2774120503833873188)
XLA Ops:
  0.0 1.1 copy.13
  1.1 0.9 copy.11
  2.1 10.6 %all-to-all-start = ((bf16[32,64,128]{2,1,0:T(8,128)(2,1)}), bf16[32,64,128]{2,1,0:T(8,128)(2,1)S(1)}, u32[]{:S(2)}, u32[]{:S(2)}) async-start(bf16[32,64,128]{2,1,0:T(8,128)(2,1)} %bitcast.2), calls=%async_computation | async-start | bytes 1048576 | tf_op jit(solution)/shard_map/all_to_all | solution.py:22
  12.7 4.6 %collective-permute-start = (bf16[128,1024]{1,0:T(8,128)(2,1)S(1)}, bf16[128,1024]{1,0:T(8,128)(2,1)S(1)}, u32[]{:S(2)}, u32[]{:S(2)}) collective-permute-start(bf16[128,1024]{1,0:T(8,128)(2,1)S(1)} %copy-done.3), channel_id=1, source_target_pairs={{128,0},{256,128},{384,256},{0,384},{129,1},{257,129},{385,257},{1... | collective-permute-start | bytes 786440 | tf_op jit(solution)/shard_map/ppermute | solution.py:159
  17.3 6.5 %all-to-all-done = bf16[32,64,128]{2,1,0:T(8,128)(2,1)S(1)} async-done(((bf16[32,64,128]{2,1,0:T(8,128)(2,1)}), bf16[32,64,128]{2,1,0:T(8,128)(2,1)S(1)}, u32[]{:S(2)}, u32[]{:S(2)}) %all-to-all-start) | async-done | bytes 524320 | tf_op jit(solution)/shard_map/all_to_all | solution.py:22
  23.8 0.9 copy.12
  24.6 13.0 %all-to-all-start.1 = ((bf16[16,128,128]{2,1,0:T(8,128)(2,1)}), bf16[16,128,128]{2,1,0:T(8,128)(2,1)S(1)}, u32[]{:S(2)}, u32[]{:S(2)}) async-start(bf16[16,128,128]{2,1,0:T(8,128)(2,1)} %bitcast.5), calls=%async_computation.1 | async-start | bytes 1048576 | tf_op jit(solution)/shard_map/all_to_all | solution.py:22
  37.6 3.2 %collective-permute-start.1 = (bf16[128,1024]{1,0:T(8,128)(2,1)S(1)}, bf16[128,1024]{1,0:T(8,128)(2,1)S(1)}, u32[]{:S(2)}, u32[]{:S(2)}) collective-permute-start(bf16[128,1024]{1,0:T(8,128)(2,1)S(1)} %collective-permute-done), channel_id=1, source_target_pairs={{128,0},{256,128},{384,256},{0,384},{129,1},{257,129},{385,257},{1... | collective-permute-start | bytes 786440 | tf_op jit(solution)/shard_map/ppermute | solution.py:161
  40.8 2.1 %collective-permute-start.2 = (bf16[128,1024]{1,0:T(8,128)(2,1)S(1)}, bf16[128,1024]{1,0:T(8,128)(2,1)S(1)}, u32[]{:S(2)}, u32[]{:S(2)}) collective-permute-start(bf16[128,1024]{1,0:T(8,128)(2,1)S(1)} %copy-done.3), channel_id=1, source_target_pairs={{0,128},{128,256},{256,384},{384,0},{1,129},{129,257},{257,385},{3... | collective-permute-start | bytes 786440 | tf_op jit(solution)/shard_map/ppermute | solution.py:160
  43.0 3.1 %collective-permute-done.1 = bf16[128,1024]{1,0:T(8,128)(2,1)S(1)} collective-permute-done((bf16[128,1024]{1,0:T(8,128)(2,1)S(1)}, bf16[128,1024]{1,0:T(8,128)(2,1)S(1)}, u32[]{:S(2)}, u32[]{:S(2)}) %collective-permute-start.1) | collective-permute-done | bytes 262176 | tf_op jit(solution)/shard_map/ppermute | solution.py:161
  46.1 4.7 %collective-permute-done.2 = bf16[128,1024]{1,0:T(8,128)(2,1)S(1)} collective-permute-done((bf16[128,1024]{1,0:T(8,128)(2,1)S(1)}, bf16[128,1024]{1,0:T(8,128)(2,1)S(1)}, u32[]{:S(2)}, u32[]{:S(2)}) %collective-permute-start.2) | collective-permute-done | bytes 262176 | tf_op jit(solution)/shard_map/ppermute | solution.py:160
  50.8 3.9 %collective-permute-start.3 = (bf16[512,1024]{1,0:T(8,128)(2,1)S(1)}, bf16[512,1024]{1,0:T(8,128)(2,1)S(1)}, u32[]{:S(2)}, u32[]{:S(2)}) collective-permute-start(bf16[512,1024]{1,0:T(8,128)(2,1)S(1)} %constant_dynamic-update-slice_fusion), channel_id=1, source_target_pairs={{0,64},{64,0},{1,65},{65,1},{2,66},{66,2},{3,67},{67,3},{4,68},{68... | collective-permute-start | bytes 3145736 | tf_op jit(solution)/shard_map/ppermute | solution.py:163
  54.8 0.1 constant_dynamic-update-slice_fusion.4
  54.8 0.4 convolution_convert_fusion.1
  55.3 1.7 %collective-permute-done.3 = bf16[512,1024]{1,0:T(8,128)(2,1)S(1)} collective-permute-done((bf16[512,1024]{1,0:T(8,128)(2,1)S(1)}, bf16[512,1024]{1,0:T(8,128)(2,1)S(1)}, u32[]{:S(2)}, u32[]{:S(2)}) %collective-permute-start.3) | collective-permute-done | bytes 1048608 | tf_op jit(solution)/shard_map/ppermute | solution.py:163
  57.0 0.4 convolution_convert_fusion
  57.5 3.0 %all-to-all-done.1.refs_2_ = bf16[16,128,128]{2,1,0:T(8,128)(2,1)S(1)} async-done(((bf16[16,128,128]{2,1,0:T(8,128)(2,1)}), bf16[16,128,128]{2,1,0:T(8,128)(2,1)S(1)}, u32[]{:S(2)}, u32[]{:S(2)}) %all-to-all-start.1) | async-done | bytes 524320 | tf_op jit(solution)/shard_map/all_to_all | solution.py:22
  60.4 3.6 %attend.1 = bf16[8,16,16,128]{3,2,1,0:T(8,128)(2,1)S(1)} custom-call(s32[4,16]{1,0:T(4,128)} %bitcast.28, s32[16]{0:T(128)} %refs_1_.1, bf16[16,128,128]{2,1,0:T(8,128)(2,1)S(1)} %all-to-all-done.1.refs_2_, bf16[1024,256]{1,0:T(8,128)(2,1)S(1)} %pad_maximum_fusion.refs_3_), custom_call_target="tpu_custom_call" | custom-call | tf_op jit(solution)/shard_map/attend/pallas_call | solution.py:75
  64.0 0.0 copy-start.1
  64.0 19.6 %all_to_all.25 = bf16[8,16,16,128]{3,2,1,0:T(8,128)(2,1)S(1)} all-to-all(bf16[8,16,16,128]{3,2,1,0:T(8,128)(2,1)S(1)} %attend.1), channel_id=1, replica_groups=mesh['x'=4,'core'=2,'z'=16,'y'=4] {'x','core'}, dimensions={0} | all-to-all | bytes 1048576 | tf_op jit(solution)/shard_map/all_to_all | solution.py:22
  83.7 0.9 wall_flux.1
  84.5 17.3 %all_to_all.26 = f32[16,4,128]{2,1,0:T(4,128)S(1)} all-to-all(f32[16,4,128]{2,1,0:T(4,128)S(1)} %wall_flux.1), channel_id=1, replica_groups=mesh['x'=4,'core'=2,'z'=16,'y'=4] {'z'}, dimensions={0} | all-to-all | bytes 65536 | tf_op jit(solution)/shard_map/all_to_all | solution.py:22
  101.8 12.9 %all_to_all.27 = f32[32,8,128]{2,1,0:T(8,128)S(1)} all-to-all(f32[32,8,128]{2,1,0:T(8,128)S(1)} %bitcast.25), channel_id=1, replica_groups=mesh['x'=4,'core'=2,'z'=16,'y'=4] {'x','core','y'}, dimensions={0} | all-to-all | bytes 262144 | tf_op jit(solution)/shard_map/all_to_all | solution.py:22
  114.7 0.7 place_flux.1
  (19 shorter events, 0.2 us)
Async XLA Ops:
  2.1 10.6 %copy-start.3 = (bf16[128,1024]{1,0:T(8,128)(2,1)S(1)}, bf16[128,1024]{1,0:T(8,128)(2,1)}, u32[]{:S(2)}) copy-start(bf16[128,1024]{1,0:T(8,128)(2,1)} %param.9) | copy-start | bytes 786436
  2.1 21.7 %all-to-all-start = ((bf16[32,64,128]{2,1,0:T(8,128)(2,1)}), bf16[32,64,128]{2,1,0:T(8,128)(2,1)S(1)}, u32[]{:S(2)}, u32[]{:S(2)}) async-start(bf16[32,64,128]{2,1,0:T(8,128)(2,1)} %bitcast.2), calls=%async_computation | async-start | bytes 1048576 | tf_op jit(solution)/shard_map/all_to_all | solution.py:22
  12.7 25.0 %collective-permute-start = (bf16[128,1024]{1,0:T(8,128)(2,1)S(1)}, bf16[128,1024]{1,0:T(8,128)(2,1)S(1)}, u32[]{:S(2)}, u32[]{:S(2)}) collective-permute-start(bf16[128,1024]{1,0:T(8,128)(2,1)S(1)} %copy-done.3), channel_id=1, source_target_pairs={{128,0},{256,128},{384,256},{0,384},{129,1},{257,129},{385,257},{1... | collective-permute-start | bytes 786440 | tf_op jit(solution)/shard_map/ppermute | solution.py:159
  24.6 35.8 %all-to-all-start.1 = ((bf16[16,128,128]{2,1,0:T(8,128)(2,1)}), bf16[16,128,128]{2,1,0:T(8,128)(2,1)S(1)}, u32[]{:S(2)}, u32[]{:S(2)}) async-start(bf16[16,128,128]{2,1,0:T(8,128)(2,1)} %bitcast.5), calls=%async_computation.1 | async-start | bytes 1048576 | tf_op jit(solution)/shard_map/all_to_all | solution.py:22
  37.6 8.4 %collective-permute-start.1 = (bf16[128,1024]{1,0:T(8,128)(2,1)S(1)}, bf16[128,1024]{1,0:T(8,128)(2,1)S(1)}, u32[]{:S(2)}, u32[]{:S(2)}) collective-permute-start(bf16[128,1024]{1,0:T(8,128)(2,1)S(1)} %collective-permute-done), channel_id=1, source_target_pairs={{128,0},{256,128},{384,256},{0,384},{129,1},{257,129},{385,257},{1... | collective-permute-start | bytes 786440 | tf_op jit(solution)/shard_map/ppermute | solution.py:161
  40.8 10.0 %collective-permute-start.2 = (bf16[128,1024]{1,0:T(8,128)(2,1)S(1)}, bf16[128,1024]{1,0:T(8,128)(2,1)S(1)}, u32[]{:S(2)}, u32[]{:S(2)}) collective-permute-start(bf16[128,1024]{1,0:T(8,128)(2,1)S(1)} %copy-done.3), channel_id=1, source_target_pairs={{0,128},{128,256},{256,384},{384,0},{1,129},{129,257},{257,385},{3... | collective-permute-start | bytes 786440 | tf_op jit(solution)/shard_map/ppermute | solution.py:160
  46.1 8.6 %copy-start.4 = (bf16[1024,128]{1,0:T(8,128)(2,1)S(1)}, bf16[1024,128]{1,0:T(8,128)(2,1)}, u32[]{:S(2)}) copy-start(bf16[1024,128]{1,0:T(8,128)(2,1)} %param.10) | copy-start | bytes 786436
  50.8 4.0 %copy-start.5 = (bf16[1024,128]{1,0:T(8,128)(2,1)S(1)}, bf16[1024,128]{1,0:T(8,128)(2,1)}, u32[]{:S(2)}) copy-start(bf16[1024,128]{1,0:T(8,128)(2,1)} %param.11) | copy-start | bytes 786436
  50.8 6.2 %collective-permute-start.3 = (bf16[512,1024]{1,0:T(8,128)(2,1)S(1)}, bf16[512,1024]{1,0:T(8,128)(2,1)S(1)}, u32[]{:S(2)}, u32[]{:S(2)}) collective-permute-start(bf16[512,1024]{1,0:T(8,128)(2,1)S(1)} %constant_dynamic-update-slice_fusion), channel_id=1, source_target_pairs={{0,64},{64,0},{1,65},{65,1},{2,66},{66,2},{3,67},{67,3},{4,68},{68... | collective-permute-start | bytes 3145736 | tf_op jit(solution)/shard_map/ppermute | solution.py:163
  60.4 23.2 %copy-start = (bf16[1024,512]{1,0:T(8,128)(2,1)S(1)}, bf16[1024,512]{1,0:T(8,128)(2,1)}, u32[]{:S(2)}) copy-start(bf16[1024,512]{1,0:T(8,128)(2,1)} %up_ref.1) | copy-start | bytes 3145732
  64.0 19.6 %copy-start.1 = (f32[1024]{0:T(1024)S(1)}, f32[1024]{0:T(1024)}, u32[]{:S(2)}) copy-start(f32[1024]{0:T(1024)} %param.15) | copy-start | bytes 12292
  64.0 19.6 %copy-start.2 = (bf16[4,512]{1,0:T(4,128)(2,1)S(1)}, bf16[4,512]{1,0:T(4,128)(2,1)}, u32[]{:S(2)}) copy-start(bf16[4,512]{1,0:T(4,128)(2,1)} %flux_ref.1) | copy-start | bytes 12292

commit v8 on v7

--- a/solution.py
+++ b/solution.py
@@ -24,6 +24,25 @@
 
 def on_chip(*arrays):
     return [pltpu.with_memory_space_constraint(array, pltpu.VMEM) for array in arrays]
+
+
+def project_kernel(along_ref, across_ref, keys_ref, values_ref, kv_ref):
+    rows, width = along_ref.shape[0], keys_ref.shape[1]
+    for start, ref in ((0, along_ref), (rows, across_ref)):
+        for lane, weights_ref in ((0, keys_ref), (width, values_ref)):
+            kv_ref[start : start + rows, lane : lane + width] = jnp.dot(
+                ref[...], weights_ref[...], preferred_element_type=jnp.float32
+            ).astype(jnp.bfloat16)
+
+
+def project(along, across, keys, values):
+    return pl.pallas_call(
+        project_kernel,
+        out_shape=pltpu.VMEM((2 * along.shape[0], 2 * keys.shape[1]), jnp.bfloat16),
+        in_specs=[pl.BlockSpec(memory_space=pltpu.VMEM)] * 4,
+        cost_estimate=pl.CostEstimate(flops=0, transcendentals=0, bytes_accessed=0),
+        name="project",
+    )(along, across, *on_chip(keys, values))
 
 
 def attend_step(step, per, cells_ref, counts_ref, query_ref, kv_ref, out_ref):
@@ -153,22 +172,17 @@
     query = exchange(query.reshape(grp * n_y, hi * SLAB, width), PLANE)
     query = query.reshape(grp, n_y, hi, SLAB, width).transpose(0, 2, 1, 3, 4)
     query = query.reshape(n_z, n_y * SLAB, width)
+    query, anchors = lax.optimization_barrier((query, anchor_states))
     query = exchange(query, "z")
     up = [((i + 1) % n_x, i) for i in range(n_x)]
     down = [(i, (i + 1) % n_x) for i in range(n_x)]
-    one_up = lax.ppermute(anchor_states, "x", up)
-    one_down = lax.ppermute(anchor_states, "x", down)
+    one_up = lax.ppermute(anchors, "x", up)
+    one_down = lax.ppermute(anchors, "x", down)
+    one_up, one_down = lax.optimization_barrier((one_up, one_down))
     two_up = lax.ppermute(one_up, "x", up)
-    along = jnp.concatenate([anchor_states, one_up, two_up, one_down], axis=0)
+    along = jnp.concatenate([anchors, one_up, two_up, one_down], axis=0)
     across = lax.ppermute(along, "core", [(0, 1), (1, 0)])
-    weights = jnp.concatenate([key_weight, value_weight], axis=1)
-    kv = jnp.concatenate(
-        [
-            jnp.dot(part, weights, preferred_element_type=jnp.float32).astype(jnp.bfloat16)
-            for part in (along, across)
-        ],
-        axis=0,
-    )
+    kv = project(along, across, key_weight, value_weight)
     stream = attend(query, kv, cell_list.T, cell_count, grp, 16)
     stream = exchange(stream, GRP)
     flux = wall_flux(

time: 116 us -> 121 us (1.043)
  blocking collectives: 49.8 us -> 68.3 us
  starting transfers between devices: 37.4 us -> 25.8 us
  waiting for transfers between devices: 18.9 us -> 16 us
  Pallas kernels: 5.1 us -> 7.89 us
    all_to_all x3 -> x4, blocking collectives: 49.8 us -> 68.3 us  [exchange(): return lax.all_to_all(array, axes, split_axis=0, concat_axis=0, tiled=True)]
    all_to_all x2 -> x1, starting transfers between devices: 23.6 us -> 13.8 us  [exchange(): return lax.all_to_all(array, axes, split_axis=0, concat_axis=0, tiled=True)]
    all_to_all x2 -> x1, waiting for transfers between devices: 9.44 us -> 0.01 us  [exchange(): return lax.all_to_all(array, axes, split_axis=0, concat_axis=0, tiled=True)]
    ppermute x2, waiting for transfers between devices: 4.66 us -> 7.8 us  [the longest x1 4.67 us: body(): one_down = lax.ppermute(anchors, 'x', down)]
    pallas_call x0 -> x1, Pallas kernels: none -> 2.78 us  [project(): pl.pallas_call(project_kernel, out_shape=pltpu.VMEM((2 * along.shape[0],...]
    ppermute x1, waiting for transfers between devices: 3.08 us -> 5.84 us  [body(): two_up = lax.ppermute(one_up, 'x', up)]
    ppermute x2, starting transfers between devices: 6.77 us -> 5.28 us  [the longest x1 3.14 us: body(): one_up = lax.ppermute(anchors, 'x', up)]
    ppermute x1, starting transfers between devices: 3.16 us -> 1.91 us  [body(): two_up = lax.ppermute(one_up, 'x', up)]
  transfers between devices with their start and end apart: 6 -> 5, of which waited for: 5 -> 4; matrix products, arithmetic and copies ran while one was open for 2% -> 0% of each run, Pallas kernels for 0% -> 2%
where the time goes in v8:
time: 121 us
  blocking collectives  68.3 us (56%)
  starting transfers between devices  25.8 us (21%)
  waiting for transfers between devices  16 us (13%)
  Pallas kernels  7.89 us (7%)
  local copies, waits for them, and re-layouts  2.24 us (2%)
    all_to_all x4, blocking collectives, exchange(): return lax.all_to_all(array, axes, split_axis=0, concat_axis=0, tiled=True)  68.3 us
    all_to_all x1, starting transfers between devices, exchange(): return lax.all_to_all(array, axes, split_axis=0, concat_axis=0, tiled=True)  13.8 us
    ppermute x1, waiting for transfers between devices, body(): two_up = lax.ppermute(one_up, 'x', up)  5.84 us
    ppermute x1, starting transfers between devices, body(): across = lax.ppermute(along, 'core', [(0, 1), (1, 0)])  4.83 us
    ppermute x1, waiting for transfers between devices, body(): one_down = lax.ppermute(anchors, 'x', down)  4.67 us
    pallas_call x1, Pallas kernels, attend(): pl.pallas_call(functools.partial(attend_kernel, per), out_shape=pltpu.VME...  3.57 us
    ppermute x1, starting transfers between devices, body(): one_up = lax.ppermute(anchors, 'x', up)  3.14 us
    ppermute x1, waiting for transfers between devices, body(): one_up = lax.ppermute(anchors, 'x', up)  3.13 us
  transfers between devices with their start and end apart: 5, of which 4 were waited for; matrix products, arithmetic and copies ran while one was open for 0% of the time, Pallas kernels for 2%

profile of v8, /device:TPU:1, one launch (start us, length us, event | category | flops | bytes accessed | tf_op | source)
XLA Modules:
  0.0 120.5 jit_solution(8853532582044227577)
XLA Ops:
  0.0 1.1 copy.13
  1.1 0.1 copy.11
  1.3 20.7 %all_to_all.25 = bf16[32,64,128]{2,1,0:T(8,128)(2,1)S(1)} all-to-all(bf16[32,64,128]{2,1,0:T(8,128)(2,1)S(1)} %bitcast.19), channel_id=1, replica_groups=mesh['x'=4,'core'=2,'z'=16,'y'=4] {'x','core','y'}, dimensions={0} | all-to-all | bytes 1048576 | tf_op jit(solution)/shard_map/all_to_all | solution.py:22
  21.9 0.9 copy.12
  22.8 13.8 %all-to-all-start.1 = ((bf16[16,128,128]{2,1,0:T(8,128)(2,1)}), bf16[16,128,128]{2,1,0:T(8,128)(2,1)S(1)}, u32[]{:S(2)}, u32[]{:S(2)}) async-start(bf16[16,128,128]{2,1,0:T(8,128)(2,1)} %bitcast.5), calls=%async_computation.1 | async-start | bytes 1048576 | tf_op jit(solution)/shard_map/all_to_all | solution.py:22
  36.6 3.1 %collective-permute-start = (bf16[128,1024]{1,0:T(8,128)(2,1)S(1)}, bf16[128,1024]{1,0:T(8,128)(2,1)S(1)}, u32[]{:S(2)}, u32[]{:S(2)}) collective-permute-start(bf16[128,1024]{1,0:T(8,128)(2,1)S(1)} %copy-done.6), channel_id=1, source_target_pairs={{128,0},{256,128},{384,256},{0,384},{129,1},{257,129},{385,257},{1... | collective-permute-start | bytes 786440 | tf_op jit(solution)/shard_map/ppermute | solution.py:179
  39.8 2.1 %collective-permute-start.1 = (bf16[128,1024]{1,0:T(8,128)(2,1)S(1)}, bf16[128,1024]{1,0:T(8,128)(2,1)S(1)}, u32[]{:S(2)}, u32[]{:S(2)}) collective-permute-start(bf16[128,1024]{1,0:T(8,128)(2,1)S(1)} %copy-done.6), channel_id=1, source_target_pairs={{0,128},{128,256},{256,384},{384,0},{1,129},{129,257},{257,385},{3... | collective-permute-start | bytes 786440 | tf_op jit(solution)/shard_map/ppermute | solution.py:180
  41.9 3.1 %collective-permute-done = bf16[128,1024]{1,0:T(8,128)(2,1)S(1)} collective-permute-done((bf16[128,1024]{1,0:T(8,128)(2,1)S(1)}, bf16[128,1024]{1,0:T(8,128)(2,1)S(1)}, u32[]{:S(2)}, u32[]{:S(2)}) %collective-permute-start) | collective-permute-done | bytes 262176 | tf_op jit(solution)/shard_map/ppermute | solution.py:179
  45.1 4.7 %collective-permute-done.1 = bf16[128,1024]{1,0:T(8,128)(2,1)S(1)} collective-permute-done((bf16[128,1024]{1,0:T(8,128)(2,1)S(1)}, bf16[128,1024]{1,0:T(8,128)(2,1)S(1)}, u32[]{:S(2)}, u32[]{:S(2)}) %collective-permute-start.1) | collective-permute-done | bytes 262176 | tf_op jit(solution)/shard_map/ppermute | solution.py:180
  49.7 1.9 %collective-permute-start.2 = (bf16[128,1024]{1,0:T(8,128)(2,1)S(1)}, bf16[128,1024]{1,0:T(8,128)(2,1)S(1)}, u32[]{:S(2)}, u32[]{:S(2)}) collective-permute-start(bf16[128,1024]{1,0:T(8,128)(2,1)S(1)} %collective-permute-done), channel_id=1, source_target_pairs={{128,0},{256,128},{384,256},{0,384},{129,1},{257,129},{385,257},{1... | collective-permute-start | bytes 786440 | tf_op jit(solution)/shard_map/ppermute | solution.py:182
  51.7 5.8 %collective-permute-done.2 = bf16[128,1024]{1,0:T(8,128)(2,1)S(1)} collective-permute-done((bf16[128,1024]{1,0:T(8,128)(2,1)S(1)}, bf16[128,1024]{1,0:T(8,128)(2,1)S(1)}, u32[]{:S(2)}, u32[]{:S(2)}) %collective-permute-start.2) | collective-permute-done | bytes 262176 | tf_op jit(solution)/shard_map/ppermute | solution.py:182
  57.6 0.0 copy-start.1
  57.6 0.0 copy-start.2
  57.6 4.8 %collective-permute-start.3 = (bf16[512,1024]{1,0:T(8,128)(2,1)S(1)}, bf16[512,1024]{1,0:T(8,128)(2,1)}, u32[]{:S(2)}, u32[]{:S(2)}) collective-permute-start(bf16[512,1024]{1,0:T(8,128)(2,1)S(1)} %constant_dynamic-update-slice_fusion.along_ref), channel_id=1, source_target_pairs={{0,64},{64,0},{1,65},{65,1},{2,66},{66,2},{3,67},{67,3},{4,68},{68... | collective-permute-start | bytes 3145736 | tf_op jit(solution)/shard_map/ppermute | solution.py:184
  62.5 2.4 %collective-permute-done.3.across_ref = bf16[512,1024]{1,0:T(8,128)(2,1)} collective-permute-done((bf16[512,1024]{1,0:T(8,128)(2,1)S(1)}, bf16[512,1024]{1,0:T(8,128)(2,1)}, u32[]{:S(2)}, u32[]{:S(2)}) %collective-permute-start.3) | collective-permute-done | bytes 1048608 | tf_op jit(solution)/shard_map/ppermute | solution.py:184
  64.9 2.8 %project.1.refs_3_ = bf16[1024,256]{1,0:T(8,128)(2,1)S(1)} custom-call(bf16[512,1024]{1,0:T(8,128)(2,1)} %copy-done.5, bf16[512,1024]{1,0:T(8,128)(2,1)} %collective-permute-done.3.across_ref, bf16[1024,128]{1,0:T(8,128)(2,1)S(1)} %copy-done.1, bf16[1024,128]{1,0:T(8,128)(2,1)S(1)} %copy-done.2), custom_call_target="tpu_custom_call" | custom-call | tf_op jit(solution)/shard_map/project/pallas_call | solution.py:39
  67.7 0.0 copy-start
  67.7 3.6 %attend.1 = bf16[8,16,16,128]{3,2,1,0:T(8,128)(2,1)S(1)} custom-call(s32[4,16]{1,0:T(4,128)} %bitcast.25, s32[16]{0:T(128)} %refs_1_.1, bf16[16,128,128]{2,1,0:T(8,128)(2,1)S(1)} %all-to-all-done.1.refs_2_, bf16[1024,256]{1,0:T(8,128)(2,1)S(1)} %project.1.refs_3_), custom_call_target="tpu_custom_call" | custom-call | tf_op jit(solution)/shard_map/attend/pallas_call | solution.py:94
  71.3 0.0 copy-start.3
  71.3 12.3 %all_to_all.26 = bf16[8,16,16,128]{3,2,1,0:T(8,128)(2,1)S(1)} all-to-all(bf16[8,16,16,128]{3,2,1,0:T(8,128)(2,1)S(1)} %attend.1), channel_id=1, replica_groups=mesh['x'=4,'core'=2,'z'=16,'y'=4] {'x','core'}, dimensions={0} | all-to-all | bytes 1048576 | tf_op jit(solution)/shard_map/all_to_all | solution.py:22
  83.6 0.9 wall_flux.1
  84.5 22.5 %all_to_all.27 = f32[16,4,128]{2,1,0:T(4,128)S(1)} all-to-all(f32[16,4,128]{2,1,0:T(4,128)S(1)} %wall_flux.1), channel_id=1, replica_groups=mesh['x'=4,'core'=2,'z'=16,'y'=4] {'z'}, dimensions={0} | all-to-all | bytes 65536 | tf_op jit(solution)/shard_map/all_to_all | solution.py:22
  107.0 12.9 %all_to_all.28 = f32[32,8,128]{2,1,0:T(8,128)S(1)} all-to-all(f32[32,8,128]{2,1,0:T(8,128)S(1)} %bitcast.22), channel_id=1, replica_groups=mesh['x'=4,'core'=2,'z'=16,'y'=4] {'x','core','y'}, dimensions={0} | all-to-all | bytes 262144 | tf_op jit(solution)/shard_map/all_to_all | solution.py:22
  119.8 0.7 place_flux.1
  (16 shorter events, 0.1 us)
Async XLA Ops:
  22.8 13.8 %copy-start.6 = (bf16[128,1024]{1,0:T(8,128)(2,1)S(1)}, bf16[128,1024]{1,0:T(8,128)(2,1)}, u32[]{:S(2)}) copy-start(bf16[128,1024]{1,0:T(8,128)(2,1)} %param.9) | copy-start | bytes 786436
  22.8 44.9 %all-to-all-start.1 = ((bf16[16,128,128]{2,1,0:T(8,128)(2,1)}), bf16[16,128,128]{2,1,0:T(8,128)(2,1)S(1)}, u32[]{:S(2)}, u32[]{:S(2)}) async-start(bf16[16,128,128]{2,1,0:T(8,128)(2,1)} %bitcast.5), calls=%async_computation.1 | async-start | bytes 1048576 | tf_op jit(solution)/shard_map/all_to_all | solution.py:22
  36.6 8.4 %collective-permute-start = (bf16[128,1024]{1,0:T(8,128)(2,1)S(1)}, bf16[128,1024]{1,0:T(8,128)(2,1)S(1)}, u32[]{:S(2)}, u32[]{:S(2)}) collective-permute-start(bf16[128,1024]{1,0:T(8,128)(2,1)S(1)} %copy-done.6), channel_id=1, source_target_pairs={{128,0},{256,128},{384,256},{0,384},{129,1},{257,129},{385,257},{1... | collective-permute-start | bytes 786440 | tf_op jit(solution)/shard_map/ppermute | solution.py:179
  39.8 10.0 %collective-permute-start.1 = (bf16[128,1024]{1,0:T(8,128)(2,1)S(1)}, bf16[128,1024]{1,0:T(8,128)(2,1)S(1)}, u32[]{:S(2)}, u32[]{:S(2)}) collective-permute-start(bf16[128,1024]{1,0:T(8,128)(2,1)S(1)} %copy-done.6), channel_id=1, source_target_pairs={{0,128},{128,256},{256,384},{384,0},{1,129},{129,257},{257,385},{3... | collective-permute-start | bytes 786440 | tf_op jit(solution)/shard_map/ppermute | solution.py:180
  49.7 7.8 %collective-permute-start.2 = (bf16[128,1024]{1,0:T(8,128)(2,1)S(1)}, bf16[128,1024]{1,0:T(8,128)(2,1)S(1)}, u32[]{:S(2)}, u32[]{:S(2)}) collective-permute-start(bf16[128,1024]{1,0:T(8,128)(2,1)S(1)} %collective-permute-done), channel_id=1, source_target_pairs={{128,0},{256,128},{384,256},{0,384},{129,1},{257,129},{385,257},{1... | collective-permute-start | bytes 786440 | tf_op jit(solution)/shard_map/ppermute | solution.py:182
  57.6 7.3 %copy-start.1 = (bf16[1024,128]{1,0:T(8,128)(2,1)S(1)}, bf16[1024,128]{1,0:T(8,128)(2,1)}, u32[]{:S(2)}) copy-start(bf16[1024,128]{1,0:T(8,128)(2,1)} %keys_ref.1) | copy-start | bytes 786436
  57.6 7.3 %copy-start.2 = (bf16[1024,128]{1,0:T(8,128)(2,1)S(1)}, bf16[1024,128]{1,0:T(8,128)(2,1)}, u32[]{:S(2)}) copy-start(bf16[1024,128]{1,0:T(8,128)(2,1)} %values_ref.1) | copy-start | bytes 786436
  57.6 7.2 %copy-start.5 = (bf16[512,1024]{1,0:T(8,128)(2,1)}, bf16[512,1024]{1,0:T(8,128)(2,1)S(1)}, u32[]{:S(2)}) copy-start(bf16[512,1024]{1,0:T(8,128)(2,1)S(1)} %constant_dynamic-update-slice_fusion.along_ref) | copy-start | bytes 3145732
  57.6 7.2 %collective-permute-start.3 = (bf16[512,1024]{1,0:T(8,128)(2,1)S(1)}, bf16[512,1024]{1,0:T(8,128)(2,1)}, u32[]{:S(2)}, u32[]{:S(2)}) collective-permute-start(bf16[512,1024]{1,0:T(8,128)(2,1)S(1)} %constant_dynamic-update-slice_fusion.along_ref), channel_id=1, source_target_pairs={{0,64},{64,0},{1,65},{65,1},{2,66},{66,2},{3,67},{67,3},{4,68},{68... | collective-permute-start | bytes 3145736 | tf_op jit(solution)/shard_map/ppermute | solution.py:184
  67.7 15.9 %copy-start = (bf16[1024,512]{1,0:T(8,128)(2,1)S(1)}, bf16[1024,512]{1,0:T(8,128)(2,1)}, u32[]{:S(2)}) copy-start(bf16[1024,512]{1,0:T(8,128)(2,1)} %up_ref.1) | copy-start | bytes 3145732
  71.3 12.3 %copy-start.3 = (f32[1024]{0:T(1024)S(1)}, f32[1024]{0:T(1024)}, u32[]{:S(2)}) copy-start(f32[1024]{0:T(1024)} %param.15) | copy-start | bytes 12292
  71.3 12.3 %copy-start.4 = (bf16[4,512]{1,0:T(4,128)(2,1)S(1)}, bf16[4,512]{1,0:T(4,128)(2,1)}, u32[]{:S(2)}) copy-start(bf16[4,512]{1,0:T(4,128)(2,1)} %flux_ref.1) | copy-start | bytes 12292

commit v9 on v7

--- a/solution.py
+++ b/solution.py
@@ -24,6 +24,33 @@
 
 def on_chip(*arrays):
     return [pltpu.with_memory_space_constraint(array, pltpu.VMEM) for array in arrays]
+
+
+def split_kernel(query_ref, out_ref):
+    chunks, rows, width = out_ref.shape
+    low = query_ref.shape[0] // rows
+    for chunk in range(chunks):
+        lane = chunk // low * width
+        for top in range(rows // SLAB):
+            row = (top * low + chunk % low) * SLAB
+            out_ref[chunk, top * SLAB : (top + 1) * SLAB, :] = query_ref[
+                row : row + SLAB, lane : lane + width
+            ]
+
+
+def split_query(query, groups, low):
+    rows, width = query.shape
+    steps = 2
+    return pl.pallas_call(
+        split_kernel,
+        out_shape=jax.ShapeDtypeStruct((groups * low, rows // low, width // groups), query.dtype),
+        grid=(steps,),
+        in_specs=[pl.BlockSpec((rows, width // steps), lambda i: (0, i))],
+        out_specs=pl.BlockSpec(
+            (groups * low // steps, rows // low, width // groups), lambda i: (i, 0, 0)
+        ),
+        name="split_query",
+    )(query)
 
 
 def attend_step(step, per, cells_ref, counts_ref, query_ref, kv_ref, out_ref):
@@ -149,8 +176,7 @@
     grp = 2 * n_x
     width = key_weight.shape[1]
     hi = n_z // grp
-    query = panel_query.reshape(hi, n_y, SLAB, grp, width).transpose(3, 1, 0, 2, 4)
-    query = exchange(query.reshape(grp * n_y, hi * SLAB, width), PLANE)
+    query = exchange(split_query(panel_query, grp, n_y), PLANE)
     query = query.reshape(grp, n_y, hi, SLAB, width).transpose(0, 2, 1, 3, 4)
     query = query.reshape(n_z, n_y * SLAB, width)
     query = exchange(query, "z")

time: 116 us -> 116 us (level)
  local copies, waits for them, and re-layouts: 3.14 us -> 1.08 us
  Pallas kernels: 5.1 us -> 6.89 us
    pallas_call x0 -> x1, Pallas kernels: none -> 1.79 us  [split_query(): pl.pallas_call(split_kernel, out_shape=jax.ShapeDtypeStruct((groups * low...]
    transpose x2 -> x0, local copies, waits for them, and re-layouts: 1.78 us -> none  [the longest x1 0.92 us: body(): panel_query.reshape(hi, n_y, SLAB, grp, width).transpose(3, 1, 0, 2, 4)]
where the time goes in v9:
time: 116 us; the launch traced here: 115 us
  blocking collectives  49.8 us (43%)
  starting transfers between devices  37.4 us (32%)
  waiting for transfers between devices  18.9 us (16%)
  Pallas kernels  6.89 us (6%)
    all_to_all x3, blocking collectives, exchange(): return lax.all_to_all(array, axes, split_axis=0, concat_axis=0, tiled=True)  49.8 us
    all_to_all x2, starting transfers between devices, exchange(): return lax.all_to_all(array, axes, split_axis=0, concat_axis=0, tiled=True)  23.5 us
    all_to_all x2, waiting for transfers between devices, exchange(): return lax.all_to_all(array, axes, split_axis=0, concat_axis=0, tiled=True)  9.44 us
    ppermute x1, waiting for transfers between devices, body(): one_down = lax.ppermute(anchor_states, 'x', down)  4.66 us
    ppermute x1, starting transfers between devices, body(): one_up = lax.ppermute(anchor_states, 'x', up)  4.65 us
    ppermute x1, starting transfers between devices, body(): across = lax.ppermute(along, 'core', [(0, 1), (1, 0)])  3.91 us
    pallas_call x1, Pallas kernels, attend(): pl.pallas_call(functools.partial(attend_kernel, per), out_shape=pltpu.VME...  3.57 us
    ppermute x1, starting transfers between devices, body(): two_up = lax.ppermute(one_up, 'x', up)  3.16 us
  transfers between devices with their start and end apart: 6, of which 5 were waited for; matrix products, arithmetic and copies ran while one was open for 2% of the time, Pallas kernels for 0%

profile of v9, /device:TPU:1, one launch (start us, length us, event | category | flops | bytes accessed | tf_op | source)
XLA Modules:
  0.0 115.1 jit_solution(12702933919218598900)
XLA Ops:
  0.0 1.8 %split_query.1 = bf16[32,64,128]{2,1,0:T(8,128)(2,1)} custom-call(bf16[256,1024]{1,0:T(8,128)(2,1)} %query_ref.1), custom_call_target="tpu_custom_call" | custom-call | tf_op jit(solution)/shard_map/split_query/pallas_call | solution.py:44
  1.8 10.6 %all-to-all-start = ((bf16[32,64,128]{2,1,0:T(8,128)(2,1)}), bf16[32,64,128]{2,1,0:T(8,128)(2,1)S(1)}, u32[]{:S(2)}, u32[]{:S(2)}) async-start(bf16[32,64,128]{2,1,0:T(8,128)(2,1)} %split_query.1), calls=%async_computation | async-start | bytes 1048576 | tf_op jit(solution)/shard_map/all_to_all | solution.py:22
  12.4 4.6 %collective-permute-start = (bf16[128,1024]{1,0:T(8,128)(2,1)S(1)}, bf16[128,1024]{1,0:T(8,128)(2,1)S(1)}, u32[]{:S(2)}, u32[]{:S(2)}) collective-permute-start(bf16[128,1024]{1,0:T(8,128)(2,1)S(1)} %copy-done.3), channel_id=1, source_target_pairs={{128,0},{256,128},{384,256},{0,384},{129,1},{257,129},{385,257},{1... | collective-permute-start | bytes 786440 | tf_op jit(solution)/shard_map/ppermute | solution.py:185
  17.0 6.5 %all-to-all-done = bf16[32,64,128]{2,1,0:T(8,128)(2,1)S(1)} async-done(((bf16[32,64,128]{2,1,0:T(8,128)(2,1)}), bf16[32,64,128]{2,1,0:T(8,128)(2,1)S(1)}, u32[]{:S(2)}, u32[]{:S(2)}) %all-to-all-start) | async-done | bytes 524320 | tf_op jit(solution)/shard_map/all_to_all | solution.py:22
  23.5 0.9 copy.10
  24.4 13.0 %all-to-all-start.1 = ((bf16[16,128,128]{2,1,0:T(8,128)(2,1)}), bf16[16,128,128]{2,1,0:T(8,128)(2,1)S(1)}, u32[]{:S(2)}, u32[]{:S(2)}) async-start(bf16[16,128,128]{2,1,0:T(8,128)(2,1)} %bitcast.3), calls=%async_computation.1 | async-start | bytes 1048576 | tf_op jit(solution)/shard_map/all_to_all | solution.py:22
  37.4 3.2 %collective-permute-start.1 = (bf16[128,1024]{1,0:T(8,128)(2,1)S(1)}, bf16[128,1024]{1,0:T(8,128)(2,1)S(1)}, u32[]{:S(2)}, u32[]{:S(2)}) collective-permute-start(bf16[128,1024]{1,0:T(8,128)(2,1)S(1)} %collective-permute-done), channel_id=1, source_target_pairs={{128,0},{256,128},{384,256},{0,384},{129,1},{257,129},{385,257},{1... | collective-permute-start | bytes 786440 | tf_op jit(solution)/shard_map/ppermute | solution.py:187
  40.5 2.1 %collective-permute-start.2 = (bf16[128,1024]{1,0:T(8,128)(2,1)S(1)}, bf16[128,1024]{1,0:T(8,128)(2,1)S(1)}, u32[]{:S(2)}, u32[]{:S(2)}) collective-permute-start(bf16[128,1024]{1,0:T(8,128)(2,1)S(1)} %copy-done.3), channel_id=1, source_target_pairs={{0,128},{128,256},{256,384},{384,0},{1,129},{129,257},{257,385},{3... | collective-permute-start | bytes 786440 | tf_op jit(solution)/shard_map/ppermute | solution.py:186
  42.7 3.1 %collective-permute-done.1 = bf16[128,1024]{1,0:T(8,128)(2,1)S(1)} collective-permute-done((bf16[128,1024]{1,0:T(8,128)(2,1)S(1)}, bf16[128,1024]{1,0:T(8,128)(2,1)S(1)}, u32[]{:S(2)}, u32[]{:S(2)}) %collective-permute-start.1) | collective-permute-done | bytes 262176 | tf_op jit(solution)/shard_map/ppermute | solution.py:187
  45.8 0.0 copy-start.4
  45.8 4.7 %collective-permute-done.2 = bf16[128,1024]{1,0:T(8,128)(2,1)S(1)} collective-permute-done((bf16[128,1024]{1,0:T(8,128)(2,1)S(1)}, bf16[128,1024]{1,0:T(8,128)(2,1)S(1)}, u32[]{:S(2)}, u32[]{:S(2)}) %collective-permute-start.2) | collective-permute-done | bytes 262176 | tf_op jit(solution)/shard_map/ppermute | solution.py:186
  50.5 0.0 copy-start.5
  50.5 3.9 %collective-permute-start.3 = (bf16[512,1024]{1,0:T(8,128)(2,1)S(1)}, bf16[512,1024]{1,0:T(8,128)(2,1)S(1)}, u32[]{:S(2)}, u32[]{:S(2)}) collective-permute-start(bf16[512,1024]{1,0:T(8,128)(2,1)S(1)} %constant_dynamic-update-slice_fusion), channel_id=1, source_target_pairs={{0,64},{64,0},{1,65},{65,1},{2,66},{66,2},{3,67},{67,3},{4,68},{68... | collective-permute-start | bytes 3145736 | tf_op jit(solution)/shard_map/ppermute | solution.py:189
  54.5 0.1 constant_dynamic-update-slice_fusion.4
  54.6 0.4 convolution_convert_fusion.1
  55.0 1.7 %collective-permute-done.3 = bf16[512,1024]{1,0:T(8,128)(2,1)S(1)} collective-permute-done((bf16[512,1024]{1,0:T(8,128)(2,1)S(1)}, bf16[512,1024]{1,0:T(8,128)(2,1)S(1)}, u32[]{:S(2)}, u32[]{:S(2)}) %collective-permute-start.3) | collective-permute-done | bytes 1048608 | tf_op jit(solution)/shard_map/ppermute | solution.py:189
  56.7 0.4 convolution_convert_fusion
  57.2 3.0 %all-to-all-done.1.refs_2_ = bf16[16,128,128]{2,1,0:T(8,128)(2,1)S(1)} async-done(((bf16[16,128,128]{2,1,0:T(8,128)(2,1)}), bf16[16,128,128]{2,1,0:T(8,128)(2,1)S(1)}, u32[]{:S(2)}, u32[]{:S(2)}) %all-to-all-start.1) | async-done | bytes 524320 | tf_op jit(solution)/shard_map/all_to_all | solution.py:22
  60.2 3.6 %attend.1 = bf16[8,16,16,128]{3,2,1,0:T(8,128)(2,1)S(1)} custom-call(s32[4,16]{1,0:T(4,128)} %bitcast.20, s32[16]{0:T(128)} %refs_1_.1, bf16[16,128,128]{2,1,0:T(8,128)(2,1)S(1)} %all-to-all-done.1.refs_2_, bf16[1024,256]{1,0:T(8,128)(2,1)S(1)} %pad_maximum_fusion.refs_3_), custom_call_target="tpu_custom_call" | custom-call | tf_op jit(solution)/shard_map/attend/pallas_call | solution.py:102
  63.8 19.6 %all_to_all.25 = bf16[8,16,16,128]{3,2,1,0:T(8,128)(2,1)S(1)} all-to-all(bf16[8,16,16,128]{3,2,1,0:T(8,128)(2,1)S(1)} %attend.1), channel_id=1, replica_groups=mesh['x'=4,'core'=2,'z'=16,'y'=4] {'x','core'}, dimensions={0} | all-to-all | bytes 1048576 | tf_op jit(solution)/shard_map/all_to_all | solution.py:22
  83.4 0.8 wall_flux.1
  84.2 17.3 %all_to_all.26 = f32[16,4,128]{2,1,0:T(4,128)S(1)} all-to-all(f32[16,4,128]{2,1,0:T(4,128)S(1)} %wall_flux.1), channel_id=1, replica_groups=mesh['x'=4,'core'=2,'z'=16,'y'=4] {'z'}, dimensions={0} | all-to-all | bytes 65536 | tf_op jit(solution)/shard_map/all_to_all | solution.py:22
  101.6 12.9 %all_to_all.27 = f32[32,8,128]{2,1,0:T(8,128)S(1)} all-to-all(f32[32,8,128]{2,1,0:T(8,128)S(1)} %bitcast.18), channel_id=1, replica_groups=mesh['x'=4,'core'=2,'z'=16,'y'=4] {'x','core','y'}, dimensions={0} | all-to-all | bytes 262144 | tf_op jit(solution)/shard_map/all_to_all | solution.py:22
  114.4 0.7 place_flux.1
  (18 shorter events, 0.2 us)
Async XLA Ops:
  1.8 10.6 %copy-start.3 = (bf16[128,1024]{1,0:T(8,128)(2,1)S(1)}, bf16[128,1024]{1,0:T(8,128)(2,1)}, u32[]{:S(2)}) copy-start(bf16[128,1024]{1,0:T(8,128)(2,1)} %param.9) | copy-start | bytes 786436
  1.8 21.7 %all-to-all-start = ((bf16[32,64,128]{2,1,0:T(8,128)(2,1)}), bf16[32,64,128]{2,1,0:T(8,128)(2,1)S(1)}, u32[]{:S(2)}, u32[]{:S(2)}) async-start(bf16[32,64,128]{2,1,0:T(8,128)(2,1)} %split_query.1), calls=%async_computation | async-start | bytes 1048576 | tf_op jit(solution)/shard_map/all_to_all | solution.py:22
  12.4 25.0 %collective-permute-start = (bf16[128,1024]{1,0:T(8,128)(2,1)S(1)}, bf16[128,1024]{1,0:T(8,128)(2,1)S(1)}, u32[]{:S(2)}, u32[]{:S(2)}) collective-permute-start(bf16[128,1024]{1,0:T(8,128)(2,1)S(1)} %copy-done.3), channel_id=1, source_target_pairs={{128,0},{256,128},{384,256},{0,384},{129,1},{257,129},{385,257},{1... | collective-permute-start | bytes 786440 | tf_op jit(solution)/shard_map/ppermute | solution.py:185
  24.4 35.8 %all-to-all-start.1 = ((bf16[16,128,128]{2,1,0:T(8,128)(2,1)}), bf16[16,128,128]{2,1,0:T(8,128)(2,1)S(1)}, u32[]{:S(2)}, u32[]{:S(2)}) async-start(bf16[16,128,128]{2,1,0:T(8,128)(2,1)} %bitcast.3), calls=%async_computation.1 | async-start | bytes 1048576 | tf_op jit(solution)/shard_map/all_to_all | solution.py:22
  37.4 8.4 %collective-permute-start.1 = (bf16[128,1024]{1,0:T(8,128)(2,1)S(1)}, bf16[128,1024]{1,0:T(8,128)(2,1)S(1)}, u32[]{:S(2)}, u32[]{:S(2)}) collective-permute-start(bf16[128,1024]{1,0:T(8,128)(2,1)S(1)} %collective-permute-done), channel_id=1, source_target_pairs={{128,0},{256,128},{384,256},{0,384},{129,1},{257,129},{385,257},{1... | collective-permute-start | bytes 786440 | tf_op jit(solution)/shard_map/ppermute | solution.py:187
  40.5 10.0 %collective-permute-start.2 = (bf16[128,1024]{1,0:T(8,128)(2,1)S(1)}, bf16[128,1024]{1,0:T(8,128)(2,1)S(1)}, u32[]{:S(2)}, u32[]{:S(2)}) collective-permute-start(bf16[128,1024]{1,0:T(8,128)(2,1)S(1)} %copy-done.3), channel_id=1, source_target_pairs={{0,128},{128,256},{256,384},{384,0},{1,129},{129,257},{257,385},{3... | collective-permute-start | bytes 786440 | tf_op jit(solution)/shard_map/ppermute | solution.py:186
  45.8 8.6 %copy-start.4 = (bf16[1024,128]{1,0:T(8,128)(2,1)S(1)}, bf16[1024,128]{1,0:T(8,128)(2,1)}, u32[]{:S(2)}) copy-start(bf16[1024,128]{1,0:T(8,128)(2,1)} %param.10) | copy-start | bytes 786436
  50.5 4.0 %copy-start.5 = (bf16[1024,128]{1,0:T(8,128)(2,1)S(1)}, bf16[1024,128]{1,0:T(8,128)(2,1)}, u32[]{:S(2)}) copy-start(bf16[1024,128]{1,0:T(8,128)(2,1)} %param.11) | copy-start | bytes 786436
  50.5 6.2 %collective-permute-start.3 = (bf16[512,1024]{1,0:T(8,128)(2,1)S(1)}, bf16[512,1024]{1,0:T(8,128)(2,1)S(1)}, u32[]{:S(2)}, u32[]{:S(2)}) collective-permute-start(bf16[512,1024]{1,0:T(8,128)(2,1)S(1)} %constant_dynamic-update-slice_fusion), channel_id=1, source_target_pairs={{0,64},{64,0},{1,65},{65,1},{2,66},{66,2},{3,67},{67,3},{4,68},{68... | collective-permute-start | bytes 3145736 | tf_op jit(solution)/shard_map/ppermute | solution.py:189
  60.2 23.2 %copy-start = (bf16[1024,512]{1,0:T(8,128)(2,1)S(1)}, bf16[1024,512]{1,0:T(8,128)(2,1)}, u32[]{:S(2)}) copy-start(bf16[1024,512]{1,0:T(8,128)(2,1)} %up_ref.1) | copy-start | bytes 3145732
  63.7 19.6 %copy-start.1 = (f32[1024]{0:T(1024)S(1)}, f32[1024]{0:T(1024)}, u32[]{:S(2)}) copy-start(f32[1024]{0:T(1024)} %param.15) | copy-start | bytes 12292
  63.8 19.6 %copy-start.2 = (bf16[4,512]{1,0:T(4,128)(2,1)S(1)}, bf16[4,512]{1,0:T(4,128)(2,1)}, u32[]{:S(2)}) copy-start(bf16[4,512]{1,0:T(4,128)(2,1)} %flux_ref.1) | copy-start | bytes 12292

commit v10 on v9

--- a/solution.py
+++ b/solution.py
@@ -86,8 +86,9 @@
             jnp.concatenate([values, ones], axis=1),
             preferred_element_type=jnp.float32,
         )
-        summed = summed[:, :width] / summed[:, width:]
-        attended = jnp.where(first, summed[:BLK], summed[BLK:]).astype(jnp.bfloat16)
+        mine = jnp.where(first, summed[:BLK, :width], summed[BLK:, :width])
+        total = jnp.where(first, summed[:BLK, width:], summed[BLK:, width:])
+        attended = (mine / total).astype(jnp.bfloat16)
         stream = query + attended.astype(jnp.float32)
         out_ref[:, block] = stream.astype(jnp.bfloat16).reshape(parts, part_rows, width)
 

time: 116 us -> 116 us (level)
  no operation moved by 1% of the time
where the time goes in v10:
time: 116 us; the launch traced here: 115 us
  blocking collectives  49.8 us (43%)
  starting transfers between devices  37.4 us (32%)
  waiting for transfers between devices  18.9 us (16%)
  Pallas kernels  6.9 us (6%)
    all_to_all x3, blocking collectives, exchange(): return lax.all_to_all(array, axes, split_axis=0, concat_axis=0, tiled=True)  49.8 us
    all_to_all x2, starting transfers between devices, exchange(): return lax.all_to_all(array, axes, split_axis=0, concat_axis=0, tiled=True)  23.5 us
    all_to_all x2, waiting for transfers between devices, exchange(): return lax.all_to_all(array, axes, split_axis=0, concat_axis=0, tiled=True)  9.44 us
    ppermute x1, waiting for transfers between devices, body(): one_down = lax.ppermute(anchor_states, 'x', down)  4.66 us
    ppermute x1, starting transfers between devices, body(): one_up = lax.ppermute(anchor_states, 'x', up)  4.65 us
    ppermute x1, starting transfers between devices, body(): across = lax.ppermute(along, 'core', [(0, 1), (1, 0)])  3.91 us
    pallas_call x1, Pallas kernels, attend(): pl.pallas_call(functools.partial(attend_kernel, per), out_shape=pltpu.VME...  3.58 us
    ppermute x1, starting transfers between devices, body(): two_up = lax.ppermute(one_up, 'x', up)  3.16 us
  transfers between devices with their start and end apart: 6, of which 5 were waited for; matrix products, arithmetic and copies ran while one was open for 2% of the time, Pallas kernels for 0%

profile of v10, /device:TPU:1, one launch (start us, length us, event | category | flops | bytes accessed | tf_op | source)
XLA Modules:
  0.0 115.1 jit_solution(10120007956987640563)
XLA Ops:
  0.0 1.8 %split_query.1 = bf16[32,64,128]{2,1,0:T(8,128)(2,1)} custom-call(bf16[256,1024]{1,0:T(8,128)(2,1)} %query_ref.1), custom_call_target="tpu_custom_call" | custom-call | tf_op jit(solution)/shard_map/split_query/pallas_call | solution.py:44
  1.8 10.6 %all-to-all-start = ((bf16[32,64,128]{2,1,0:T(8,128)(2,1)}), bf16[32,64,128]{2,1,0:T(8,128)(2,1)S(1)}, u32[]{:S(2)}, u32[]{:S(2)}) async-start(bf16[32,64,128]{2,1,0:T(8,128)(2,1)} %split_query.1), calls=%async_computation | async-start | bytes 1048576 | tf_op jit(solution)/shard_map/all_to_all | solution.py:22
  12.4 4.6 %collective-permute-start = (bf16[128,1024]{1,0:T(8,128)(2,1)S(1)}, bf16[128,1024]{1,0:T(8,128)(2,1)S(1)}, u32[]{:S(2)}, u32[]{:S(2)}) collective-permute-start(bf16[128,1024]{1,0:T(8,128)(2,1)S(1)} %copy-done.3), channel_id=1, source_target_pairs={{128,0},{256,128},{384,256},{0,384},{129,1},{257,129},{385,257},{1... | collective-permute-start | bytes 786440 | tf_op jit(solution)/shard_map/ppermute | solution.py:186
  17.0 6.5 %all-to-all-done = bf16[32,64,128]{2,1,0:T(8,128)(2,1)S(1)} async-done(((bf16[32,64,128]{2,1,0:T(8,128)(2,1)}), bf16[32,64,128]{2,1,0:T(8,128)(2,1)S(1)}, u32[]{:S(2)}, u32[]{:S(2)}) %all-to-all-start) | async-done | bytes 524320 | tf_op jit(solution)/shard_map/all_to_all | solution.py:22
  23.5 0.9 copy.10
  24.4 13.0 %all-to-all-start.1 = ((bf16[16,128,128]{2,1,0:T(8,128)(2,1)}), bf16[16,128,128]{2,1,0:T(8,128)(2,1)S(1)}, u32[]{:S(2)}, u32[]{:S(2)}) async-start(bf16[16,128,128]{2,1,0:T(8,128)(2,1)} %bitcast.3), calls=%async_computation.1 | async-start | bytes 1048576 | tf_op jit(solution)/shard_map/all_to_all | solution.py:22
  37.4 3.2 %collective-permute-start.1 = (bf16[128,1024]{1,0:T(8,128)(2,1)S(1)}, bf16[128,1024]{1,0:T(8,128)(2,1)S(1)}, u32[]{:S(2)}, u32[]{:S(2)}) collective-permute-start(bf16[128,1024]{1,0:T(8,128)(2,1)S(1)} %collective-permute-done), channel_id=1, source_target_pairs={{128,0},{256,128},{384,256},{0,384},{129,1},{257,129},{385,257},{1... | collective-permute-start | bytes 786440 | tf_op jit(solution)/shard_map/ppermute | solution.py:188
  40.5 2.1 %collective-permute-start.2 = (bf16[128,1024]{1,0:T(8,128)(2,1)S(1)}, bf16[128,1024]{1,0:T(8,128)(2,1)S(1)}, u32[]{:S(2)}, u32[]{:S(2)}) collective-permute-start(bf16[128,1024]{1,0:T(8,128)(2,1)S(1)} %copy-done.3), channel_id=1, source_target_pairs={{0,128},{128,256},{256,384},{384,0},{1,129},{129,257},{257,385},{3... | collective-permute-start | bytes 786440 | tf_op jit(solution)/shard_map/ppermute | solution.py:187
  42.7 3.1 %collective-permute-done.1 = bf16[128,1024]{1,0:T(8,128)(2,1)S(1)} collective-permute-done((bf16[128,1024]{1,0:T(8,128)(2,1)S(1)}, bf16[128,1024]{1,0:T(8,128)(2,1)S(1)}, u32[]{:S(2)}, u32[]{:S(2)}) %collective-permute-start.1) | collective-permute-done | bytes 262176 | tf_op jit(solution)/shard_map/ppermute | solution.py:188
  45.8 0.0 copy-start.4
  45.8 4.7 %collective-permute-done.2 = bf16[128,1024]{1,0:T(8,128)(2,1)S(1)} collective-permute-done((bf16[128,1024]{1,0:T(8,128)(2,1)S(1)}, bf16[128,1024]{1,0:T(8,128)(2,1)S(1)}, u32[]{:S(2)}, u32[]{:S(2)}) %collective-permute-start.2) | collective-permute-done | bytes 262176 | tf_op jit(solution)/shard_map/ppermute | solution.py:187
  50.5 0.0 copy-start.5
  50.5 3.9 %collective-permute-start.3 = (bf16[512,1024]{1,0:T(8,128)(2,1)S(1)}, bf16[512,1024]{1,0:T(8,128)(2,1)S(1)}, u32[]{:S(2)}, u32[]{:S(2)}) collective-permute-start(bf16[512,1024]{1,0:T(8,128)(2,1)S(1)} %constant_dynamic-update-slice_fusion), channel_id=1, source_target_pairs={{0,64},{64,0},{1,65},{65,1},{2,66},{66,2},{3,67},{67,3},{4,68},{68... | collective-permute-start | bytes 3145736 | tf_op jit(solution)/shard_map/ppermute | solution.py:190
  54.5 0.1 constant_dynamic-update-slice_fusion.4
  54.6 0.4 convolution_convert_fusion.1
  55.0 1.7 %collective-permute-done.3 = bf16[512,1024]{1,0:T(8,128)(2,1)S(1)} collective-permute-done((bf16[512,1024]{1,0:T(8,128)(2,1)S(1)}, bf16[512,1024]{1,0:T(8,128)(2,1)S(1)}, u32[]{:S(2)}, u32[]{:S(2)}) %collective-permute-start.3) | collective-permute-done | bytes 1048608 | tf_op jit(solution)/shard_map/ppermute | solution.py:190
  56.7 0.4 convolution_convert_fusion
  57.2 3.0 %all-to-all-done.1.refs_2_ = bf16[16,128,128]{2,1,0:T(8,128)(2,1)S(1)} async-done(((bf16[16,128,128]{2,1,0:T(8,128)(2,1)}), bf16[16,128,128]{2,1,0:T(8,128)(2,1)S(1)}, u32[]{:S(2)}, u32[]{:S(2)}) %all-to-all-start.1) | async-done | bytes 524320 | tf_op jit(solution)/shard_map/all_to_all | solution.py:22
  60.2 3.6 %attend.1 = bf16[8,16,16,128]{3,2,1,0:T(8,128)(2,1)S(1)} custom-call(s32[4,16]{1,0:T(4,128)} %bitcast.20, s32[16]{0:T(128)} %refs_1_.1, bf16[16,128,128]{2,1,0:T(8,128)(2,1)S(1)} %all-to-all-done.1.refs_2_, bf16[1024,256]{1,0:T(8,128)(2,1)S(1)} %pad_maximum_fusion.refs_3_), custom_call_target="tpu_custom_call" | custom-call | tf_op jit(solution)/shard_map/attend/pallas_call | solution.py:103
  63.8 19.6 %all_to_all.25 = bf16[8,16,16,128]{3,2,1,0:T(8,128)(2,1)S(1)} all-to-all(bf16[8,16,16,128]{3,2,1,0:T(8,128)(2,1)S(1)} %attend.1), channel_id=1, replica_groups=mesh['x'=4,'core'=2,'z'=16,'y'=4] {'x','core'}, dimensions={0} | all-to-all | bytes 1048576 | tf_op jit(solution)/shard_map/all_to_all | solution.py:22
  83.4 0.8 wall_flux.1
  84.2 17.3 %all_to_all.26 = f32[16,4,128]{2,1,0:T(4,128)S(1)} all-to-all(f32[16,4,128]{2,1,0:T(4,128)S(1)} %wall_flux.1), channel_id=1, replica_groups=mesh['x'=4,'core'=2,'z'=16,'y'=4] {'z'}, dimensions={0} | all-to-all | bytes 65536 | tf_op jit(solution)/shard_map/all_to_all | solution.py:22
  101.6 12.9 %all_to_all.27 = f32[32,8,128]{2,1,0:T(8,128)S(1)} all-to-all(f32[32,8,128]{2,1,0:T(8,128)S(1)} %bitcast.18), channel_id=1, replica_groups=mesh['x'=4,'core'=2,'z'=16,'y'=4] {'x','core','y'}, dimensions={0} | all-to-all | bytes 262144 | tf_op jit(solution)/shard_map/all_to_all | solution.py:22
  114.4 0.7 place_flux.1
  (18 shorter events, 0.2 us)
Async XLA Ops:
  1.8 10.6 %copy-start.3 = (bf16[128,1024]{1,0:T(8,128)(2,1)S(1)}, bf16[128,1024]{1,0:T(8,128)(2,1)}, u32[]{:S(2)}) copy-start(bf16[128,1024]{1,0:T(8,128)(2,1)} %param.9) | copy-start | bytes 786436
  1.8 21.7 %all-to-all-start = ((bf16[32,64,128]{2,1,0:T(8,128)(2,1)}), bf16[32,64,128]{2,1,0:T(8,128)(2,1)S(1)}, u32[]{:S(2)}, u32[]{:S(2)}) async-start(bf16[32,64,128]{2,1,0:T(8,128)(2,1)} %split_query.1), calls=%async_computation | async-start | bytes 1048576 | tf_op jit(solution)/shard_map/all_to_all | solution.py:22
  12.4 25.0 %collective-permute-start = (bf16[128,1024]{1,0:T(8,128)(2,1)S(1)}, bf16[128,1024]{1,0:T(8,128)(2,1)S(1)}, u32[]{:S(2)}, u32[]{:S(2)}) collective-permute-start(bf16[128,1024]{1,0:T(8,128)(2,1)S(1)} %copy-done.3), channel_id=1, source_target_pairs={{128,0},{256,128},{384,256},{0,384},{129,1},{257,129},{385,257},{1... | collective-permute-start | bytes 786440 | tf_op jit(solution)/shard_map/ppermute | solution.py:186
  24.4 35.8 %all-to-all-start.1 = ((bf16[16,128,128]{2,1,0:T(8,128)(2,1)}), bf16[16,128,128]{2,1,0:T(8,128)(2,1)S(1)}, u32[]{:S(2)}, u32[]{:S(2)}) async-start(bf16[16,128,128]{2,1,0:T(8,128)(2,1)} %bitcast.3), calls=%async_computation.1 | async-start | bytes 1048576 | tf_op jit(solution)/shard_map/all_to_all | solution.py:22
  37.4 8.4 %collective-permute-start.1 = (bf16[128,1024]{1,0:T(8,128)(2,1)S(1)}, bf16[128,1024]{1,0:T(8,128)(2,1)S(1)}, u32[]{:S(2)}, u32[]{:S(2)}) collective-permute-start(bf16[128,1024]{1,0:T(8,128)(2,1)S(1)} %collective-permute-done), channel_id=1, source_target_pairs={{128,0},{256,128},{384,256},{0,384},{129,1},{257,129},{385,257},{1... | collective-permute-start | bytes 786440 | tf_op jit(solution)/shard_map/ppermute | solution.py:188
  40.5 10.0 %collective-permute-start.2 = (bf16[128,1024]{1,0:T(8,128)(2,1)S(1)}, bf16[128,1024]{1,0:T(8,128)(2,1)S(1)}, u32[]{:S(2)}, u32[]{:S(2)}) collective-permute-start(bf16[128,1024]{1,0:T(8,128)(2,1)S(1)} %copy-done.3), channel_id=1, source_target_pairs={{0,128},{128,256},{256,384},{384,0},{1,129},{129,257},{257,385},{3... | collective-permute-start | bytes 786440 | tf_op jit(solution)/shard_map/ppermute | solution.py:187
  45.8 8.6 %copy-start.4 = (bf16[1024,128]{1,0:T(8,128)(2,1)S(1)}, bf16[1024,128]{1,0:T(8,128)(2,1)}, u32[]{:S(2)}) copy-start(bf16[1024,128]{1,0:T(8,128)(2,1)} %param.10) | copy-start | bytes 786436
  50.5 4.0 %copy-start.5 = (bf16[1024,128]{1,0:T(8,128)(2,1)S(1)}, bf16[1024,128]{1,0:T(8,128)(2,1)}, u32[]{:S(2)}) copy-start(bf16[1024,128]{1,0:T(8,128)(2,1)} %param.11) | copy-start | bytes 786436
  50.5 6.2 %collective-permute-start.3 = (bf16[512,1024]{1,0:T(8,128)(2,1)S(1)}, bf16[512,1024]{1,0:T(8,128)(2,1)S(1)}, u32[]{:S(2)}, u32[]{:S(2)}) collective-permute-start(bf16[512,1024]{1,0:T(8,128)(2,1)S(1)} %constant_dynamic-update-slice_fusion), channel_id=1, source_target_pairs={{0,64},{64,0},{1,65},{65,1},{2,66},{66,2},{3,67},{67,3},{4,68},{68... | collective-permute-start | bytes 3145736 | tf_op jit(solution)/shard_map/ppermute | solution.py:190
  60.2 23.2 %copy-start = (bf16[1024,512]{1,0:T(8,128)(2,1)S(1)}, bf16[1024,512]{1,0:T(8,128)(2,1)}, u32[]{:S(2)}) copy-start(bf16[1024,512]{1,0:T(8,128)(2,1)} %up_ref.1) | copy-start | bytes 3145732
  63.8 19.6 %copy-start.1 = (f32[1024]{0:T(1024)S(1)}, f32[1024]{0:T(1024)}, u32[]{:S(2)}) copy-start(f32[1024]{0:T(1024)} %param.15) | copy-start | bytes 12292
  63.8 19.6 %copy-start.2 = (bf16[4,512]{1,0:T(4,128)(2,1)S(1)}, bf16[4,512]{1,0:T(4,128)(2,1)}, u32[]{:S(2)}) copy-start(bf16[4,512]{1,0:T(4,128)(2,1)} %flux_ref.1) | copy-start | bytes 12292

commit v11 on v10

--- a/solution.py
+++ b/solution.py
@@ -110,23 +110,26 @@
 
 
 def flux_kernel(stream_ref, gain_ref, up_ref, flux_ref, out_ref):
-    groups = stream_ref.shape[0]
-    stream = jnp.concatenate(
-        [stream_ref[h].astype(jnp.float32) for h in range(groups)], axis=1
-    )
-    scale = lax.rsqrt(jnp.mean(stream * stream, axis=-1, keepdims=True) + 1e-06)
-    normed = (stream * scale * gain_ref[...]).astype(jnp.bfloat16)
-    hidden = jax.nn.gelu(
-        jnp.dot(normed, up_ref[...], preferred_element_type=jnp.float32)
-    ).astype(jnp.bfloat16)
-    flux = lax.dot_general(
-        flux_ref[...], hidden, (((1,), (1,)), ((), ())), preferred_element_type=jnp.float32
-    )
+    groups, rows, _ = stream_ref.shape
     blocks = out_ref.shape[0]
-    few = flux.shape[1] // blocks
-    for block in range(blocks):
-        piece = flux[:, block * few : (block + 1) * few]
-        out_ref[block] = jnp.concatenate([piece] * (LANES // few), axis=1)
+    few = rows // blocks
+    half = rows // 2
+    for start in range(0, rows, half):
+        stream = jnp.concatenate(
+            [stream_ref[h, start : start + half].astype(jnp.float32) for h in range(groups)],
+            axis=1,
+        )
+        scale = lax.rsqrt(jnp.mean(stream * stream, axis=-1, keepdims=True) + 1e-06)
+        normed = (stream * scale * gain_ref[...]).astype(jnp.bfloat16)
+        hidden = jax.nn.gelu(
+            jnp.dot(normed, up_ref[...], preferred_element_type=jnp.float32)
+        ).astype(jnp.bfloat16)
+        flux = lax.dot_general(
+            flux_ref[...], hidden, (((1,), (1,)), ((), ())), preferred_element_type=jnp.float32
+        )
+        for block in range(half // few):
+            piece = flux[:, block * few : (block + 1) * few]
+            out_ref[start // few + block] = jnp.concatenate([piece] * (LANES // few), axis=1)
 
 
 def wall_flux(stream, norm_gain, up_weight, flux_weight, blocks):

time: 116 us -> 116 us (level)
  no operation moved by 1% of the time
where the time goes in v11:
time: 116 us; the launch traced here: 115 us
  blocking collectives  49.8 us (43%)
  starting transfers between devices  37.4 us (32%)
  waiting for transfers between devices  18.9 us (16%)
  Pallas kernels  7.03 us (6%)
    all_to_all x3, blocking collectives, exchange(): return lax.all_to_all(array, axes, split_axis=0, concat_axis=0, tiled=True)  49.8 us
    all_to_all x2, starting transfers between devices, exchange(): return lax.all_to_all(array, axes, split_axis=0, concat_axis=0, tiled=True)  23.5 us
    all_to_all x2, waiting for transfers between devices, exchange(): return lax.all_to_all(array, axes, split_axis=0, concat_axis=0, tiled=True)  9.44 us
    ppermute x1, waiting for transfers between devices, body(): one_down = lax.ppermute(anchor_states, 'x', down)  4.66 us
    ppermute x1, starting transfers between devices, body(): one_up = lax.ppermute(anchor_states, 'x', up)  4.65 us
    ppermute x1, starting transfers between devices, body(): across = lax.ppermute(along, 'core', [(0, 1), (1, 0)])  3.91 us
    pallas_call x1, Pallas kernels, attend(): pl.pallas_call(functools.partial(attend_kernel, per), out_shape=pltpu.VME...  3.58 us
    ppermute x1, starting transfers between devices, body(): two_up = lax.ppermute(one_up, 'x', up)  3.16 us
  transfers between devices with their start and end apart: 6, of which 5 were waited for; matrix products, arithmetic and copies ran while one was open for 2% of the time, Pallas kernels for 0%

profile of v11, /device:TPU:1, one launch (start us, length us, event | category | flops | bytes accessed | tf_op | source)
XLA Modules:
  0.0 115.2 jit_solution(8853582589419212135)
XLA Ops:
  0.0 1.8 %split_query.1 = bf16[32,64,128]{2,1,0:T(8,128)(2,1)} custom-call(bf16[256,1024]{1,0:T(8,128)(2,1)} %query_ref.1), custom_call_target="tpu_custom_call" | custom-call | tf_op jit(solution)/shard_map/split_query/pallas_call | solution.py:44
  1.8 10.6 %all-to-all-start = ((bf16[32,64,128]{2,1,0:T(8,128)(2,1)}), bf16[32,64,128]{2,1,0:T(8,128)(2,1)S(1)}, u32[]{:S(2)}, u32[]{:S(2)}) async-start(bf16[32,64,128]{2,1,0:T(8,128)(2,1)} %split_query.1), calls=%async_computation | async-start | bytes 1048576 | tf_op jit(solution)/shard_map/all_to_all | solution.py:22
  12.4 4.6 %collective-permute-start = (bf16[128,1024]{1,0:T(8,128)(2,1)S(1)}, bf16[128,1024]{1,0:T(8,128)(2,1)S(1)}, u32[]{:S(2)}, u32[]{:S(2)}) collective-permute-start(bf16[128,1024]{1,0:T(8,128)(2,1)S(1)} %copy-done.3), channel_id=1, source_target_pairs={{128,0},{256,128},{384,256},{0,384},{129,1},{257,129},{385,257},{1... | collective-permute-start | bytes 786440 | tf_op jit(solution)/shard_map/ppermute | solution.py:189
  17.0 6.5 %all-to-all-done = bf16[32,64,128]{2,1,0:T(8,128)(2,1)S(1)} async-done(((bf16[32,64,128]{2,1,0:T(8,128)(2,1)}), bf16[32,64,128]{2,1,0:T(8,128)(2,1)S(1)}, u32[]{:S(2)}, u32[]{:S(2)}) %all-to-all-start) | async-done | bytes 524320 | tf_op jit(solution)/shard_map/all_to_all | solution.py:22
  23.5 0.9 copy.10
  24.4 13.0 %all-to-all-start.1 = ((bf16[16,128,128]{2,1,0:T(8,128)(2,1)}), bf16[16,128,128]{2,1,0:T(8,128)(2,1)S(1)}, u32[]{:S(2)}, u32[]{:S(2)}) async-start(bf16[16,128,128]{2,1,0:T(8,128)(2,1)} %bitcast.3), calls=%async_computation.1 | async-start | bytes 1048576 | tf_op jit(solution)/shard_map/all_to_all | solution.py:22
  37.4 3.2 %collective-permute-start.1 = (bf16[128,1024]{1,0:T(8,128)(2,1)S(1)}, bf16[128,1024]{1,0:T(8,128)(2,1)S(1)}, u32[]{:S(2)}, u32[]{:S(2)}) collective-permute-start(bf16[128,1024]{1,0:T(8,128)(2,1)S(1)} %collective-permute-done), channel_id=1, source_target_pairs={{128,0},{256,128},{384,256},{0,384},{129,1},{257,129},{385,257},{1... | collective-permute-start | bytes 786440 | tf_op jit(solution)/shard_map/ppermute | solution.py:191
  40.5 2.1 %collective-permute-start.2 = (bf16[128,1024]{1,0:T(8,128)(2,1)S(1)}, bf16[128,1024]{1,0:T(8,128)(2,1)S(1)}, u32[]{:S(2)}, u32[]{:S(2)}) collective-permute-start(bf16[128,1024]{1,0:T(8,128)(2,1)S(1)} %copy-done.3), channel_id=1, source_target_pairs={{0,128},{128,256},{256,384},{384,0},{1,129},{129,257},{257,385},{3... | collective-permute-start | bytes 786440 | tf_op jit(solution)/shard_map/ppermute | solution.py:190
  42.7 3.1 %collective-permute-done.1 = bf16[128,1024]{1,0:T(8,128)(2,1)S(1)} collective-permute-done((bf16[128,1024]{1,0:T(8,128)(2,1)S(1)}, bf16[128,1024]{1,0:T(8,128)(2,1)S(1)}, u32[]{:S(2)}, u32[]{:S(2)}) %collective-permute-start.1) | collective-permute-done | bytes 262176 | tf_op jit(solution)/shard_map/ppermute | solution.py:191
  45.8 0.0 copy-start.4
  45.8 4.7 %collective-permute-done.2 = bf16[128,1024]{1,0:T(8,128)(2,1)S(1)} collective-permute-done((bf16[128,1024]{1,0:T(8,128)(2,1)S(1)}, bf16[128,1024]{1,0:T(8,128)(2,1)S(1)}, u32[]{:S(2)}, u32[]{:S(2)}) %collective-permute-start.2) | collective-permute-done | bytes 262176 | tf_op jit(solution)/shard_map/ppermute | solution.py:190
  50.5 0.0 copy-start.5
  50.5 3.9 %collective-permute-start.3 = (bf16[512,1024]{1,0:T(8,128)(2,1)S(1)}, bf16[512,1024]{1,0:T(8,128)(2,1)S(1)}, u32[]{:S(2)}, u32[]{:S(2)}) collective-permute-start(bf16[512,1024]{1,0:T(8,128)(2,1)S(1)} %constant_dynamic-update-slice_fusion), channel_id=1, source_target_pairs={{0,64},{64,0},{1,65},{65,1},{2,66},{66,2},{3,67},{67,3},{4,68},{68... | collective-permute-start | bytes 3145736 | tf_op jit(solution)/shard_map/ppermute | solution.py:193
  54.5 0.1 constant_dynamic-update-slice_fusion.4
  54.6 0.4 convolution_convert_fusion.1
  55.0 1.7 %collective-permute-done.3 = bf16[512,1024]{1,0:T(8,128)(2,1)S(1)} collective-permute-done((bf16[512,1024]{1,0:T(8,128)(2,1)S(1)}, bf16[512,1024]{1,0:T(8,128)(2,1)S(1)}, u32[]{:S(2)}, u32[]{:S(2)}) %collective-permute-start.3) | collective-permute-done | bytes 1048608 | tf_op jit(solution)/shard_map/ppermute | solution.py:193
  56.7 0.4 convolution_convert_fusion
  57.2 3.0 %all-to-all-done.1.refs_2_ = bf16[16,128,128]{2,1,0:T(8,128)(2,1)S(1)} async-done(((bf16[16,128,128]{2,1,0:T(8,128)(2,1)}), bf16[16,128,128]{2,1,0:T(8,128)(2,1)S(1)}, u32[]{:S(2)}, u32[]{:S(2)}) %all-to-all-start.1) | async-done | bytes 524320 | tf_op jit(solution)/shard_map/all_to_all | solution.py:22
  60.2 3.6 %attend.1 = bf16[8,16,16,128]{3,2,1,0:T(8,128)(2,1)S(1)} custom-call(s32[4,16]{1,0:T(4,128)} %bitcast.20, s32[16]{0:T(128)} %refs_1_.1, bf16[16,128,128]{2,1,0:T(8,128)(2,1)S(1)} %all-to-all-done.1.refs_2_, bf16[1024,256]{1,0:T(8,128)(2,1)S(1)} %pad_maximum_fusion.refs_3_), custom_call_target="tpu_custom_call" | custom-call | tf_op jit(solution)/shard_map/attend/pallas_call | solution.py:103
  63.8 19.6 %all_to_all.25 = bf16[8,16,16,128]{3,2,1,0:T(8,128)(2,1)S(1)} all-to-all(bf16[8,16,16,128]{3,2,1,0:T(8,128)(2,1)S(1)} %attend.1), channel_id=1, replica_groups=mesh['x'=4,'core'=2,'z'=16,'y'=4] {'x','core'}, dimensions={0} | all-to-all | bytes 1048576 | tf_op jit(solution)/shard_map/all_to_all | solution.py:22
  83.4 1.0 wall_flux.1
  84.4 17.3 %all_to_all.26 = f32[16,4,128]{2,1,0:T(4,128)S(1)} all-to-all(f32[16,4,128]{2,1,0:T(4,128)S(1)} %wall_flux.1), channel_id=1, replica_groups=mesh['x'=4,'core'=2,'z'=16,'y'=4] {'z'}, dimensions={0} | all-to-all | bytes 65536 | tf_op jit(solution)/shard_map/all_to_all | solution.py:22
  101.7 12.9 %all_to_all.27 = f32[32,8,128]{2,1,0:T(8,128)S(1)} all-to-all(f32[32,8,128]{2,1,0:T(8,128)S(1)} %bitcast.18), channel_id=1, replica_groups=mesh['x'=4,'core'=2,'z'=16,'y'=4] {'x','core','y'}, dimensions={0} | all-to-all | bytes 262144 | tf_op jit(solution)/shard_map/all_to_all | solution.py:22
  114.6 0.7 place_flux.1
  (18 shorter events, 0.2 us)
Async XLA Ops:
  1.8 10.6 %copy-start.3 = (bf16[128,1024]{1,0:T(8,128)(2,1)S(1)}, bf16[128,1024]{1,0:T(8,128)(2,1)}, u32[]{:S(2)}) copy-start(bf16[128,1024]{1,0:T(8,128)(2,1)} %param.9) | copy-start | bytes 786436
  1.8 21.7 %all-to-all-start = ((bf16[32,64,128]{2,1,0:T(8,128)(2,1)}), bf16[32,64,128]{2,1,0:T(8,128)(2,1)S(1)}, u32[]{:S(2)}, u32[]{:S(2)}) async-start(bf16[32,64,128]{2,1,0:T(8,128)(2,1)} %split_query.1), calls=%async_computation | async-start | bytes 1048576 | tf_op jit(solution)/shard_map/all_to_all | solution.py:22
  12.4 25.0 %collective-permute-start = (bf16[128,1024]{1,0:T(8,128)(2,1)S(1)}, bf16[128,1024]{1,0:T(8,128)(2,1)S(1)}, u32[]{:S(2)}, u32[]{:S(2)}) collective-permute-start(bf16[128,1024]{1,0:T(8,128)(2,1)S(1)} %copy-done.3), channel_id=1, source_target_pairs={{128,0},{256,128},{384,256},{0,384},{129,1},{257,129},{385,257},{1... | collective-permute-start | bytes 786440 | tf_op jit(solution)/shard_map/ppermute | solution.py:189
  24.4 35.8 %all-to-all-start.1 = ((bf16[16,128,128]{2,1,0:T(8,128)(2,1)}), bf16[16,128,128]{2,1,0:T(8,128)(2,1)S(1)}, u32[]{:S(2)}, u32[]{:S(2)}) async-start(bf16[16,128,128]{2,1,0:T(8,128)(2,1)} %bitcast.3), calls=%async_computation.1 | async-start | bytes 1048576 | tf_op jit(solution)/shard_map/all_to_all | solution.py:22
  37.4 8.4 %collective-permute-start.1 = (bf16[128,1024]{1,0:T(8,128)(2,1)S(1)}, bf16[128,1024]{1,0:T(8,128)(2,1)S(1)}, u32[]{:S(2)}, u32[]{:S(2)}) collective-permute-start(bf16[128,1024]{1,0:T(8,128)(2,1)S(1)} %collective-permute-done), channel_id=1, source_target_pairs={{128,0},{256,128},{384,256},{0,384},{129,1},{257,129},{385,257},{1... | collective-permute-start | bytes 786440 | tf_op jit(solution)/shard_map/ppermute | solution.py:191
  40.5 10.0 %collective-permute-start.2 = (bf16[128,1024]{1,0:T(8,128)(2,1)S(1)}, bf16[128,1024]{1,0:T(8,128)(2,1)S(1)}, u32[]{:S(2)}, u32[]{:S(2)}) collective-permute-start(bf16[128,1024]{1,0:T(8,128)(2,1)S(1)} %copy-done.3), channel_id=1, source_target_pairs={{0,128},{128,256},{256,384},{384,0},{1,129},{129,257},{257,385},{3... | collective-permute-start | bytes 786440 | tf_op jit(solution)/shard_map/ppermute | solution.py:190
  45.8 8.6 %copy-start.4 = (bf16[1024,128]{1,0:T(8,128)(2,1)S(1)}, bf16[1024,128]{1,0:T(8,128)(2,1)}, u32[]{:S(2)}) copy-start(bf16[1024,128]{1,0:T(8,128)(2,1)} %param.10) | copy-start | bytes 786436
  50.5 4.0 %copy-start.5 = (bf16[1024,128]{1,0:T(8,128)(2,1)S(1)}, bf16[1024,128]{1,0:T(8,128)(2,1)}, u32[]{:S(2)}) copy-start(bf16[1024,128]{1,0:T(8,128)(2,1)} %param.11) | copy-start | bytes 786436
  50.5 6.2 %collective-permute-start.3 = (bf16[512,1024]{1,0:T(8,128)(2,1)S(1)}, bf16[512,1024]{1,0:T(8,128)(2,1)S(1)}, u32[]{:S(2)}, u32[]{:S(2)}) collective-permute-start(bf16[512,1024]{1,0:T(8,128)(2,1)S(1)} %constant_dynamic-update-slice_fusion), channel_id=1, source_target_pairs={{0,64},{64,0},{1,65},{65,1},{2,66},{66,2},{3,67},{67,3},{4,68},{68... | collective-permute-start | bytes 3145736 | tf_op jit(solution)/shard_map/ppermute | solution.py:193
  60.2 23.2 %copy-start = (bf16[1024,512]{1,0:T(8,128)(2,1)S(1)}, bf16[1024,512]{1,0:T(8,128)(2,1)}, u32[]{:S(2)}) copy-start(bf16[1024,512]{1,0:T(8,128)(2,1)} %up_ref.1) | copy-start | bytes 3145732
  63.8 19.6 %copy-start.1 = (f32[1024]{0:T(1024)S(1)}, f32[1024]{0:T(1024)}, u32[]{:S(2)}) copy-start(f32[1024]{0:T(1024)} %param.15) | copy-start | bytes 12292
  63.8 19.6 %copy-start.2 = (bf16[4,512]{1,0:T(4,128)(2,1)S(1)}, bf16[4,512]{1,0:T(4,128)(2,1)}, u32[]{:S(2)}) copy-start(bf16[4,512]{1,0:T(4,128)(2,1)} %flux_ref.1) | copy-start | bytes 12292
